TPU v7x, 32 devices: a whole 2x2x4 slice. The times are simulated.
32 devices in a mesh: ctx: 8 (over z, y), fsdp: 4 (over x, core).
Axes of the slice: x: 2, y: 2, z: 4, core: 2. Of those that a mesh axis runs over, the one named last changes fastest.
Arguments:
- byte_ids: int32 [16, 2048], P('fsdp', 'ctx'), may hold values from 0 to 258
- doc_ids: int32 [16, 2048], P('fsdp', 'ctx'), may hold values from 0 to 4, never falling along the last dimension, each value on 1 to 1024 neighbouring positions
- rel_bucket: int32 [2047], replicated, may hold values from 0 to 31
- table: float32 [259, 768], replicated, may hold values from -6 to 6
- conv_w: float32 [4, 768], replicated, may hold values from -3 to 3
- score_w: float32 [768], replicated, may hold values from -0.4375 to 0.4375
- gain_one: float32 [768], replicated, may hold values from 0.1 to 1.9
- gain_two: float32 [768], replicated, may hold values from 0.1 to 1.9
- rel_bias: float32 [32, 12], replicated, may hold values from -4 to 4
- query_master: float32 [768, 768], P('fsdp'), may hold values from -0.078125 to 0.078125
- key_master: float32 [768, 768], P('fsdp'), may hold values from -0.078125 to 0.078125
- value_master: float32 [768, 768], P('fsdp'), may hold values from -0.21875 to 0.21875
- out_master: float32 [768, 768], P('fsdp'), may hold values from -2.5 to 2.5
- gate_master: float32 [768, 2048], P('fsdp'), may hold values from -0.21875 to 0.21875
- up_master: float32 [768, 2048], P('fsdp'), may hold values from -0.21875 to 0.21875
- down_master: float32 [2048, 768], P('fsdp'), may hold values from -0.1875 to 0.1875
- out_cotangent: bfloat16 [1024, 16, 768], P('ctx', 'fsdp'), may hold values from -6 to 6
Outputs:
- output: bfloat16 [1024, 16, 768], P('ctx', 'fsdp')
- grad_table: float32 [259, 768], replicated
- grad_conv: float32 [4, 768], replicated
- grad_score: float32 [768], replicated
- grad_gain_one: float32 [768], replicated
- grad_gain_two: float32 [768], replicated
- grad_rel_bias: float32 [32, 12], replicated
- grad_query: float32 [768, 768], P('fsdp')
- grad_key: float32 [768, 768], P('fsdp')
- grad_value: float32 [768, 768], P('fsdp')
- grad_out_proj: float32 [768, 768], P('fsdp')
- grad_gate: float32 [768, 2048], P('fsdp')
- grad_up: float32 [768, 2048], P('fsdp')
- grad_down: float32 [2048, 768], P('fsdp')
Inputs may be any that keep to these rules, and one draw needn't show every extreme that they name: `doc_ids`: along each sequence the document numbers never fall, so each document is one run of bytes.
All inputs are finite; a program needn't handle non-finite values.
Results may differ from a plain program's by a relative error of at most 0.02.
Values may be sent and summed in bfloat16 or wider, within the bound.
No kernel may reach another device: no remote copies, remote signals or barrier semaphores. Data moves between devices by JAX's collectives and lax.ppermute only.
A program may use at most 256 MiB of HBM per device.

v0:
```python
import jax
import jax.numpy as jnp
from jax import lax
from jax.sharding import PartitionSpec as P

masked_fill = -1e30


def padded(block, sides, width):
    for axis, dim in sides:
        count = lax.axis_size(axis)
        forward = [(i, i + 1) for i in range(count - 1)]
        backward = [(target, source) for source, target in forward]
        low = lax.ppermute(
            lax.slice_in_dim(block, block.shape[dim] - width, None, axis=dim), axis, forward
        )
        high = lax.ppermute(lax.slice_in_dim(block, 0, width, axis=dim), axis, backward)
        block = jnp.concatenate([low, block, high], axis=dim)
    return block


def from_behind(value, axis, steps):
    count = lax.axis_size(axis)
    pairs = [(source, (source + steps) % count) for source in range(count)]
    return lax.ppermute(value, axis, pairs)


def rms_scale(values, gain_vec):
    return values * lax.rsqrt(jnp.mean(values * values, axis=-1, keepdims=True) + 1e-06) * gain_vec


def gelu_product(gate_pre, up_pre):
    return jax.nn.gelu(gate_pre, approximate=True) * up_pre


def block_bias(bias_table, rel_bucket, query_start, key_start, query_count, key_count, seq_tokens):
    span_len = query_count + key_count - 1
    first_index = key_start - query_start - (query_count - 1) + seq_tokens - 1
    buckets = lax.dynamic_slice_in_dim(rel_bucket, first_index, span_len)
    onehot = (buckets[:, None] == jnp.arange(bias_table.shape[0])[None, :]).astype(jnp.float32)
    per_offset = jnp.transpose(jnp.dot(onehot, bias_table, precision=lax.Precision.HIGHEST))
    head_count = per_offset.shape[0]
    repeated = jnp.tile(per_offset, (1, query_count))
    strided = repeated[:, query_count - 1 : query_count - 1 + query_count * (span_len - 1)]
    toeplitz = strided.reshape(head_count, query_count, span_len - 1)
    return toeplitz[:, :, :key_count]


def gbst_one(table, conv_w, score_w, ids_row, byte_first, total_bytes):
    ext_len = ids_row.shape[0]
    own_len = ext_len - 12
    conv_len = own_len + 7
    width_model = table.shape[1]
    ext_pos = byte_first + jnp.arange(ext_len)
    inside = ((ext_pos >= 0) & (ext_pos < total_bytes)).astype(jnp.float32)
    onehot = (jnp.arange(table.shape[0])[:, None] == ids_row[None, :]).astype(jnp.float32) * inside[
        None, :
    ]
    embedded = jnp.einsum("vr,vd->rd", onehot, table, precision=lax.Precision.HIGHEST)
    conv_out = embedded[0:conv_len] * conv_w[0]
    for offset in range(1, 4):
        conv_out = conv_out + embedded[offset : offset + conv_len] * conv_w[offset]
    conv_pos = byte_first + 3 + jnp.arange(conv_len)
    keep_mask = ((conv_pos >= 0) & (conv_pos < total_bytes)).astype(jnp.float32)
    conv_out = conv_out * keep_mask[:, None]
    own_pos = byte_first + 6 + jnp.arange(own_len)
    pooled_list = []
    for width in range(1, 5):
        phase = (own_pos % width)[:, None]
        pooled = jnp.zeros((own_len, width_model), jnp.float32)
        for rest in range(width):
            begin = 3 - rest
            window = conv_out[begin : begin + own_len]
            for extra in range(1, width):
                window = window + conv_out[begin + extra : begin + extra + own_len]
            pooled = pooled + jnp.where(phase == rest, window, 0.0)
        pooled_list.append(pooled / width)
    stacked = jnp.stack(pooled_list)
    logits = jnp.sum(stacked * score_w, axis=-1)
    mixing = jax.nn.softmax(logits, axis=0)
    mixed = jnp.sum(mixing[:, :, None] * stacked, axis=0)
    return jnp.mean(mixed.reshape(own_len // 2, 2, width_model), axis=1)


def local(
    byte_ids,
    doc_ids,
    rel_bucket,
    table,
    conv_w,
    score_w,
    gain_one,
    gain_two,
    rel_bias,
    query_master,
    key_master,
    value_master,
    out_master,
    gate_master,
    up_master,
    down_master,
    out_cotangent,
):
    ctx_count = lax.axis_size("ctx")
    ctx_index = lax.axis_index("ctx")
    seq_count, byte_count = byte_ids.shape
    tok_count = byte_count // 2
    seq_tokens = tok_count * ctx_count
    model_width = table.shape[1]
    heads = rel_bias.shape[1]
    head_size = query_master.shape[1] // heads
    joined_width = heads * head_size
    row_count = tok_count * seq_count
    query_start = ctx_index * tok_count
    f32 = jnp.float32
    bf16 = jnp.bfloat16
    query_low = query_master.astype(bf16)
    key_low = key_master.astype(bf16)
    value_low = value_master.astype(bf16)
    out_low = out_master.astype(bf16)
    gate_low = gate_master.astype(bf16)
    up_low = up_master.astype(bf16)
    down_low = down_master.astype(bf16)
    full_fwd = (
        lax.all_gather(query_low, "fsdp", axis=0, tiled=True),
        lax.all_gather(key_low, "fsdp", axis=0, tiled=True),
        lax.all_gather(value_low, "fsdp", axis=0, tiled=True),
        lax.all_gather(out_low, "fsdp", axis=0, tiled=True),
        lax.all_gather(gate_low, "fsdp", axis=0, tiled=True),
        lax.all_gather(up_low, "fsdp", axis=0, tiled=True),
        lax.all_gather(down_low, "fsdp", axis=0, tiled=True),
    )
    query_weight, key_weight, value_weight, out_weight, gate_weight, up_weight, down_weight = (
        full_fwd
    )
    ext_ids = padded(byte_ids, (("ctx", 1),), 6)
    byte_first = ctx_index * byte_count - 6
    total_bytes = byte_count * ctx_count

    def gbst_forward(ids_row):
        return gbst_one(table, conv_w, score_w, ids_row, byte_first, total_bytes)

    token_rows = lax.map(gbst_forward, ext_ids)
    tokens = jnp.transpose(token_rows, (1, 0, 2))
    tokens_flat = tokens.reshape(row_count, model_width)
    norm_one = rms_scale(tokens_flat, gain_one).astype(bf16)
    queries = jnp.dot(norm_one, query_weight, preferred_element_type=f32).astype(bf16)
    keys_own = jnp.dot(norm_one, key_weight, preferred_element_type=f32).astype(bf16)
    values_own = jnp.dot(norm_one, value_weight, preferred_element_type=f32).astype(bf16)
    queries3 = queries.reshape(tok_count, seq_count, joined_width)
    keys3 = keys_own.reshape(tok_count, seq_count, joined_width)
    values3 = values_own.reshape(tok_count, seq_count, joined_width)
    query4 = queries.reshape(tok_count, seq_count, heads, head_size)
    token_docs = jnp.transpose(doc_ids[:, ::2])
    row_best = jnp.full((seq_count, heads, tok_count), masked_fill, f32)
    key_piece = lax.all_gather(keys3, "ctx", axis=0, tiled=True)
    value_piece = lax.all_gather(values3, "ctx", axis=0, tiled=True)
    doc_piece = lax.all_gather(token_docs, "ctx", axis=0, tiled=True)
    key_count = key_piece.shape[0]
    key4 = key_piece.reshape(key_count, seq_count, heads, head_size)
    value4 = value_piece.reshape(key_count, seq_count, heads, head_size)
    pos_bias = block_bias(
        rel_bias, rel_bucket, query_start, jnp.int32(0), tok_count, key_count, seq_tokens
    )
    scores = (
        jnp.einsum("qshe,kshe->shqk", query4, key4, preferred_element_type=f32) + pos_bias[None]
    )
    allowed = (jnp.transpose(token_docs)[:, :, None] == jnp.transpose(doc_piece)[:, None, :])[
        :, None
    ]
    scores = jnp.where(allowed, scores, masked_fill)
    new_best = jnp.maximum(row_best, jnp.max(scores, axis=-1))
    weights = jnp.where(allowed, jnp.exp(scores - new_best[..., None]), 0.0)
    row_total = jnp.sum(weights, axis=-1)
    row_accum = jnp.einsum(
        "shqk,kshe->shqe", weights.astype(bf16), value4, preferred_element_type=f32
    )
    row_best, row_total, row_accum = (new_best, row_total, row_accum)
    attended = row_accum / row_total[..., None]
    log_total = row_best + jnp.log(row_total)
    attended_low = (
        jnp.transpose(attended, (2, 0, 1, 3)).reshape(row_count, joined_width).astype(bf16)
    )
    branch = jnp.dot(attended_low, out_weight, preferred_element_type=f32)
    resid = tokens_flat + branch
    norm_two = rms_scale(resid, gain_two).astype(bf16)
    gate_pre = jnp.dot(norm_two, gate_weight, preferred_element_type=f32)
    up_pre = jnp.dot(norm_two, up_weight, preferred_element_type=f32)
    hidden = gelu_product(gate_pre, up_pre).astype(bf16)
    down_out = jnp.dot(hidden, down_weight, preferred_element_type=f32)
    output = (resid + down_out).astype(bf16).reshape(tok_count, seq_count, model_width)
    full_back = (
        lax.all_gather(query_low, "fsdp", axis=0, tiled=True),
        lax.all_gather(key_low, "fsdp", axis=0, tiled=True),
        lax.all_gather(value_low, "fsdp", axis=0, tiled=True),
        lax.all_gather(out_low, "fsdp", axis=0, tiled=True),
        lax.all_gather(gate_low, "fsdp", axis=0, tiled=True),
        lax.all_gather(up_low, "fsdp", axis=0, tiled=True),
        lax.all_gather(down_low, "fsdp", axis=0, tiled=True),
    )
    query_back, key_back, value_back, out_back, gate_back, up_back, down_back = full_back
    cotangent = out_cotangent.reshape(row_count, model_width)
    grad_down_full = jnp.einsum("rf,rd->fd", hidden, cotangent, preferred_element_type=f32)
    d_hidden = jnp.einsum("rd,fd->rf", cotangent, down_back, preferred_element_type=f32)
    _, gelu_pull = jax.vjp(gelu_product, gate_pre, up_pre)
    d_gate_full, d_up_full = gelu_pull(d_hidden)
    d_gate = d_gate_full.astype(bf16)
    d_up = d_up_full.astype(bf16)
    grad_gate_full = jnp.einsum("rd,rf->df", norm_two, d_gate, preferred_element_type=f32)
    grad_up_full = jnp.einsum("rd,rf->df", norm_two, d_up, preferred_element_type=f32)
    d_norm_two = jnp.einsum(
        "rf,df->rd", d_gate, gate_back, preferred_element_type=f32
    ) + jnp.einsum("rf,df->rd", d_up, up_back, preferred_element_type=f32)
    _, norm_pull_two = jax.vjp(rms_scale, resid, gain_two)
    d_resid_norm, grad_gain_two = norm_pull_two(d_norm_two)
    d_resid = cotangent.astype(f32) + d_resid_norm
    d_branch = d_resid.astype(bf16)
    grad_out_full = jnp.einsum("ra,rd->ad", attended_low, d_branch, preferred_element_type=f32)
    d_attended = jnp.einsum("rd,ad->ra", d_branch, out_back, preferred_element_type=f32).astype(
        bf16
    )
    d_attended3 = d_attended.reshape(tok_count, seq_count, joined_width)
    delta = jnp.einsum(
        "qshe,shqe->shq",
        d_attended.reshape(tok_count, seq_count, heads, head_size).astype(f32),
        attended,
        precision=lax.Precision.HIGHEST,
    )

    def block_grads(
        query_piece,
        dout_piece,
        query_docs,
        query_log,
        query_delta,
        q_start,
        key_piece,
        value_piece,
        key_docs,
        k_start,
    ):
        query_rows = query_piece.shape[0]
        key_rows = key_piece.shape[0]
        q_four = query_piece.reshape(query_rows, seq_count, heads, head_size)
        d_four = dout_piece.reshape(query_rows, seq_count, heads, head_size)
        k_four = key_piece.reshape(key_rows, seq_count, heads, head_size)
        v_four = value_piece.reshape(key_rows, seq_count, heads, head_size)

        def bias_of(table_in):
            return block_bias(
                table_in, rel_bucket, q_start, k_start, query_rows, key_rows, seq_tokens
            )

        pos_bias, bias_pull = jax.vjp(bias_of, rel_bias)
        scores = (
            jnp.einsum("qshe,kshe->shqk", q_four, k_four, preferred_element_type=f32)
            + pos_bias[None]
        )
        allowed = (jnp.transpose(query_docs)[:, :, None] == jnp.transpose(key_docs)[:, None, :])[
            :, None
        ]
        probs = jnp.where(allowed, jnp.exp(scores - query_log[..., None]), 0.0)
        d_probs = jnp.einsum("qshe,kshe->shqk", d_four, v_four, preferred_element_type=f32)
        d_scores = (probs * (d_probs - query_delta[..., None])).astype(bf16)
        dq_term = jnp.einsum("shqk,kshe->qshe", d_scores, k_four, preferred_element_type=f32)
        dk_term = jnp.einsum("shqk,qshe->kshe", d_scores, q_four, preferred_element_type=f32)
        dv_term = jnp.einsum(
            "shqk,qshe->kshe", probs.astype(bf16), d_four, preferred_element_type=f32
        )
        (bias_term,) = bias_pull(jnp.sum(d_scores.astype(f32), axis=0))
        return (
            dq_term.reshape(query_rows, seq_count, joined_width),
            dk_term.reshape(key_rows, seq_count, joined_width),
            dv_term.reshape(key_rows, seq_count, joined_width),
            bias_term,
        )

    zero_rows = jnp.zeros((tok_count, seq_count, joined_width), f32)
    zero_bias = jnp.zeros(rel_bias.shape, f32)

    def key_turn(turn, state):
        key_hold, value_hold, docs_hold, d_key_hold, d_value_hold, d_query_acc, bias_acc = state
        anchor = (ctx_index - turn) % ctx_count
        terms = block_grads(
            queries3,
            d_attended3,
            token_docs,
            log_total,
            delta,
            query_start,
            key_hold,
            value_hold,
            docs_hold,
            anchor * tok_count,
        )
        d_query_acc = d_query_acc + terms[0]
        d_key_hold = d_key_hold + terms[1]
        d_value_hold = d_value_hold + terms[2]
        bias_acc = bias_acc + terms[3]
        key_hold, value_hold, docs_hold = from_behind((key_hold, value_hold, docs_hold), "ctx", 1)
        d_key_hold, d_value_hold = (
            from_behind(d_key_hold.astype(jnp.bfloat16), "ctx", 1).astype(d_key_hold.dtype),
            from_behind(d_value_hold.astype(jnp.bfloat16), "ctx", 1).astype(d_value_hold.dtype),
        )
        return (key_hold, value_hold, docs_hold, d_key_hold, d_value_hold, d_query_acc, bias_acc)

    final_state = lax.fori_loop(
        0,
        ctx_count,
        key_turn,
        (keys3, values3, token_docs, zero_rows, zero_rows, zero_rows, zero_bias),
    )
    d_key_sum = final_state[3]
    d_value_sum = final_state[4]
    d_query_sum = final_state[5]
    bias_grad = final_state[6]
    d_queries = d_query_sum.reshape(row_count, joined_width).astype(bf16)
    d_keys = d_key_sum.reshape(row_count, joined_width).astype(bf16)
    d_values = d_value_sum.reshape(row_count, joined_width).astype(bf16)
    grad_query_full = jnp.einsum("rd,ra->da", norm_one, d_queries, preferred_element_type=f32)
    grad_key_full = jnp.einsum("rd,ra->da", norm_one, d_keys, preferred_element_type=f32)
    grad_value_full = jnp.einsum("rd,ra->da", norm_one, d_values, preferred_element_type=f32)
    d_norm_one = (
        jnp.einsum("ra,da->rd", d_queries, query_back, preferred_element_type=f32)
        + jnp.einsum("ra,da->rd", d_keys, key_back, preferred_element_type=f32)
        + jnp.einsum("ra,da->rd", d_values, value_back, preferred_element_type=f32)
    )
    _, norm_pull_one = jax.vjp(rms_scale, tokens_flat, gain_one)
    d_tokens_norm, grad_gain_one = norm_pull_one(d_norm_one)
    d_tokens = d_resid + d_tokens_norm
    d_token_rows = jnp.transpose(d_tokens.reshape(tok_count, seq_count, model_width), (1, 0, 2))

    def gbst_backward(totals, inputs):
        ids_row, d_row = inputs

        def local_tokens(table_in, conv_in, score_in):
            return gbst_one(table_in, conv_in, score_in, ids_row, byte_first, total_bytes)

        _, gbst_pull = jax.vjp(local_tokens, table, conv_w, score_w)
        grads = gbst_pull(d_row)
        return (jax.tree.map(jnp.add, totals, grads), 0.0)

    gbst_zero = (
        jnp.zeros(table.shape, f32),
        jnp.zeros(conv_w.shape, f32),
        jnp.zeros(score_w.shape, f32),
    )
    gbst_grads, _ = lax.scan(gbst_backward, gbst_zero, (ext_ids, d_token_rows))
    grad_table_part, grad_conv_part, grad_score_part = gbst_grads
    shard_grads = (
        lax.psum_scatter(
            grad_query_full.astype(jnp.bfloat16), "fsdp", scatter_dimension=0, tiled=True
        ).astype(jnp.float32),
        lax.psum_scatter(
            grad_key_full.astype(jnp.bfloat16), "fsdp", scatter_dimension=0, tiled=True
        ).astype(jnp.float32),
        lax.psum_scatter(
            grad_value_full.astype(jnp.bfloat16), "fsdp", scatter_dimension=0, tiled=True
        ).astype(jnp.float32),
        lax.psum_scatter(
            grad_out_full.astype(jnp.bfloat16), "fsdp", scatter_dimension=0, tiled=True
        ).astype(jnp.float32),
        lax.psum_scatter(
            grad_gate_full.astype(jnp.bfloat16), "fsdp", scatter_dimension=0, tiled=True
        ).astype(jnp.float32),
        lax.psum_scatter(
            grad_up_full.astype(jnp.bfloat16), "fsdp", scatter_dimension=0, tiled=True
        ).astype(jnp.float32),
        lax.psum_scatter(
            grad_down_full.astype(jnp.bfloat16), "fsdp", scatter_dimension=0, tiled=True
        ).astype(jnp.float32),
    )
    summed = (
        lax.psum(shard_grads[0].astype(jnp.bfloat16), "ctx").astype(jnp.float32),
        lax.psum(shard_grads[1].astype(jnp.bfloat16), "ctx").astype(jnp.float32),
        lax.psum(shard_grads[2].astype(jnp.bfloat16), "ctx").astype(jnp.float32),
        lax.psum(shard_grads[3].astype(jnp.bfloat16), "ctx").astype(jnp.float32),
        lax.psum(shard_grads[4].astype(jnp.bfloat16), "ctx").astype(jnp.float32),
        lax.psum(shard_grads[5].astype(jnp.bfloat16), "ctx").astype(jnp.float32),
        lax.psum(shard_grads[6].astype(jnp.bfloat16), "ctx").astype(jnp.float32),
        lax.psum(grad_table_part.astype(jnp.bfloat16), "ctx").astype(jnp.float32),
        lax.psum(grad_conv_part.astype(jnp.bfloat16), "ctx").astype(jnp.float32),
        lax.psum(grad_score_part.astype(jnp.bfloat16), "ctx").astype(jnp.float32),
        lax.psum(grad_gain_one.astype(jnp.bfloat16), "ctx").astype(jnp.float32),
        lax.psum(grad_gain_two.astype(jnp.bfloat16), "ctx").astype(jnp.float32),
        lax.psum(bias_grad.astype(jnp.bfloat16), "ctx").astype(jnp.float32),
    )
    small_sums = (
        lax.psum(summed[7].astype(jnp.bfloat16), "fsdp").astype(jnp.float32),
        lax.psum(summed[8].astype(jnp.bfloat16), "fsdp").astype(jnp.float32),
        lax.psum(summed[9].astype(jnp.bfloat16), "fsdp").astype(jnp.float32),
        lax.psum(summed[10].astype(jnp.bfloat16), "fsdp").astype(jnp.float32),
        lax.psum(summed[11].astype(jnp.bfloat16), "fsdp").astype(jnp.float32),
        lax.psum(summed[12].astype(jnp.bfloat16), "fsdp").astype(jnp.float32),
    )
    return (
        output,
        small_sums[0],
        small_sums[1],
        small_sums[2],
        small_sums[3],
        small_sums[4],
        small_sums[5],
        summed[0],
        summed[1],
        summed[2],
        summed[3],
        summed[4],
        summed[5],
        summed[6],
    )


def solution(mesh):
    placed = (
        P("fsdp", "ctx"),
        P("fsdp", "ctx"),
        P(),
        P(),
        P(),
        P(),
        P(),
        P(),
        P(),
        P("fsdp", None),
        P("fsdp", None),
        P("fsdp", None),
        P("fsdp", None),
        P("fsdp", None),
        P("fsdp", None),
        P("fsdp", None),
        P("ctx", "fsdp", None),
    )
    return jax.shard_map(
        local,
        mesh=mesh,
        in_specs=placed,
        out_specs=(
            P("ctx", "fsdp", None),
            P(),
            P(),
            P(),
            P(),
            P(),
            P(),
            P("fsdp", None),
            P("fsdp", None),
            P("fsdp", None),
            P("fsdp", None),
            P("fsdp", None),
            P("fsdp", None),
            P("fsdp", None),
        ),
        check_vma=False,
    )
```

profile of v0, /device:TPU:0, one launch (start us, length us, event | category | flops | bytes accessed | tf_op | source)
XLA Modules:
  0.0 1445.5 jit_solution(8257005103321174705)
XLA Ops:
  21.7 36.1 %while.61 = (s32[]{:T(128)}, f32[4,128,768]{2,1,0:T(8,128)}, s32[4,268]{1,0:T(4,128)S(1)}, s32[]{:T(128)}, f32[259,768]{1,0:T(8,128)S(1)}, /*index=5*/f32[4,768]...) while((s32[]{:T(128)}, f32[4,128,768]{2,1,0:T(8,128)}, ...), condition=%wide.region_6.7_spmd, body=%wide.region_0.6_spmd.sunk | while | flops 656425664 | bytes 32123368 | solution.py:143
  86.2 26.8 %all_gather.37 = s32[1024,4]{0,1:T(4,128)S(1)} all-gather(s32[128,4]{0,1:T(4,128)S(1)} %bitcast.212), channel_id=1, replica_groups=mesh['ctx'=8,'fsdp'=4] {'ctx'}, dimensions={0}, use_global_device_ids=true | all-gather | bytes 18432 | tf_op jit(solution)/shard_map/all_gather | solution.py:158
  117.2 13.5 tile.37
  138.1 15.7 %reshape.580 = f32[12,128,1150]{2,1,0:T(8,128)} reshape(f32[12,147200]{1,0:T(8,128)} %slice.343) | data formatting | bytes 14131200 | tf_op jit(solution)/shard_map/reshape | solution.py:45
  175.8 10.8 copy.121
  186.6 16.4 %fusion.91 = (f32[4,12,128]{2,1,0:T(8,128)S(1)}, f32[4,12,128,1024]{3,2,1,0:T(8,128)}) fusion(f32[12,128,1024]{2,1,0:T(8,128)} %slice.344, pred[4,128,1024]{2,1,0:T(8,128)(4,1)S(1)} %copy-done.24, bf16[1024,4,12,64]{0,3,2,1:T(8,128)(2,1)} %bitcast.206, bf16[128,4,12,64]{3,2,1,0:T(8,128)(2,1)} %reshape.577), kind=kOutput, calls=%fused_computation.207 | convolution fusion | flops 824174592 | bytes 39084032 | tf_op jit(solution)/shard_map/qshe,kshe->shqk/dot_general | solution.py:166
  203.0 13.4 fusion.92
  216.5 55.0 %all-gather.18.cloned.1.call-done = bf16[1024,4,768]{2,1,0:T(4,128)(2,1)} async-done(((bf16[128,4,768]{2,1,0:T(4,128)(2,1)}), bf16[1024,4,768]{2,1,0:T(4,128)(2,1)}) %all-gather.18.cloned.1.call-update) | async-done | bytes 6291472 | tf_op jit(solution)/shard_map/all_gather | solution.py:157
  271.5 10.7 copy.123
  282.1 16.7 %fusion.106 = (bf16[128,4,12,64]{0,3,2,1:T(8,128)(2,1)S(1)}, f32[4,12,128,64]{2,3,1,0:T(8,128)}) fusion(f32[128,4,12]{0,2,1:T(8,128)S(1)} %bitcast.210, bf16[1024,4,12,64]{0,3,2,1:T(8,128)(2,1)} %bitcast.209, f32[4,12,128,1024]{3,2,1,0:T(8,128)} %get-tuple-element.1205, f32[4,12,128]{2,1,0:T(8,128)S(1)} %broadcast_maximum_fusion, ...), kind=kOutput, calls=%fused_computation.237 | convolution fusion | flops 837550080 | bytes 40681472 | tf_op jit(solution)/shard_map/shqk,kshe->shqe/dot_general | solution.py:175
  309.2 10.7 all-gather.22.cloned.1.call-done
  325.5 24.5 %all-gather.24.cloned.1.call-done = bf16[768,2048]{1,0:T(8,128)(2,1)} async-done(((bf16[192,2048]{1,0:T(8,128)(2,1)}), bf16[768,2048]{1,0:T(8,128)(2,1)}) %all-gather.24.cloned.1.call-update) | async-done | bytes 3145744 | tf_op jit(solution)/shard_map/all_gather | solution.py:130
  355.6 24.5 %all-gather.26.cloned.1.call-done = bf16[2048,768]{1,0:T(8,128)(2,1)} async-done(((bf16[512,768]{1,0:T(8,128)(2,1)}), bf16[2048,768]{1,0:T(8,128)(2,1)}) %all-gather.26.cloned.1.call-update) | async-done | bytes 3145744 | tf_op jit(solution)/shard_map/all_gather | solution.py:131
  409.9 602.1 %while.62 = (s32[]{:T(128)}, bf16[128,4,768]{0,2,1:T(8,128)(2,1)}, bf16[128,4,768]{0,2,1:T(8,128)(2,1)}, s32[128,4]{0,1:T(4,128)S(1)}, f32[128,4,768]{0,2,1:T(8,...) while((s32[]{:T(128)}, bf16[128,4,768]{0,2,1:T(8,128)(2,1)}, ...), condition=%wide.region_15.16_spmd.clone, body=%wide.region_12.15_spmd.clone.sunk | while | flops 519310528 | bytes 133110936 | solution.py:307
  474.1 12.7 collective-permute-done.4
  550.2 11.8 collective-permute-done.4
  848.7 10.5 collective-permute-done.4
  923.4 10.9 collective-permute-done.4
  998.4 11.1 collective-permute-done.4
  1050.2 93.3 %while.63 = (s32[]{:T(128)}, f32[259,768]{1,0:T(8,128)}, f32[4,768]{1,0:T(4,128)S(1)}, f32[768]{0:T(1024)S(1)}, s32[4,268]{1,0:T(4,128)}, /*index=5*/s32[]{:T(12...) while((s32[]{:T(128)}, f32[259,768]{1,0:T(8,128)}, ...), condition=%wide.region_28.29_spmd.clone, body=%wide.region_17.28_spmd.clone.sunk | while | flops 1312176384 | bytes 71154072 | solution.py:348
  1145.5 30.9 %reduce-scatter.16.cloned.1.call-done = bf16[192,2048]{1,0:T(8,128)(2,1)} async-done(((bf16[768,2048]{1,0:T(8,128)(2,1)}), bf16[192,2048]{1,0:T(8,128)(2,1)}) %reduce-scatter.16.cloned.1.call-update) | async-done | bytes 786448 | tf_op jit(solution)/shard_map/reduce_scatter | solution.py:363
  1176.4 40.4 %reduce-scatter.20.cloned.1.call-done = bf16[512,768]{1,0:T(8,128)(2,1)} async-done(((bf16[2048,768]{1,0:T(8,128)(2,1)}), bf16[512,768]{1,0:T(8,128)(2,1)}) %reduce-scatter.20.cloned.1.call-update) | async-done | bytes 786448 | tf_op jit(solution)/shard_map/reduce_scatter | solution.py:369
  1216.8 158.7 %all-reduce.48.cloned.1.call-done = (bf16[259,768]{1,0:T(8,128)(2,1)}, bf16[192,768]{1,0:T(8,128)(2,1)}, bf16[192,768]{1,0:T(8,128)(2,1)}, bf16[192,768]{1,0:T(8...) async-done(((bf16[259,768]{1,0:T(8,128)(2,1)}, bf16[192,768]{1,0:T(8,128)(2,1)}, ...) | async-done | bytes 3936784 | tf_op jit(solution)/shard_map/psum | solution.py:381
  1380.0 34.9 %all-reduce.40 = (bf16[4,768]{1,0:T(4,128)(2,1)S(1)}, bf16[768]{0:T(1024)(128)(2,1)S(1)}, bf16[768]{0:T(1024)(128)(2,1)S(1)}, bf16[768]{0:T(1024)(128)(2,1)S(1)}, bf16[32,12]{0,1:T(8,128)(2,1)S(1)}) all-reduce(bf16[4,768]{1,0:T(4,128)(2,1)S(1)} %convert_element_type.368, ...), channel_id=1, replica_groups=mesh['ctx'=8,'fsdp'=4] {'ctx'}, use_global_device_ids=true, to_apply=%region_31.32 | all-reduce | flops 5760 | bytes 23040 | tf_op jit(solution)/shard_map/psum | solution.py:382
  (979 shorter events, 866.1 us)
Async XLA Ops:
  11.1 157.9 %all-gather.10.cloned.1.call-start = ((), (), s32[]{:S(2)}) async-start(), calls=%async_computation.7 | async-start | bytes 1474560 | tf_op jit(solution)/shard_map/all_gather | solution.py:125
  18.2 157.6 %all-gather.14.cloned.1.call-start = ((), (), s32[]{:S(2)}) async-start(), calls=%async_computation.9 | async-start | bytes 7077888 | tf_op jit(solution)/shard_map/all_gather | solution.py:156
  70.7 200.8 %all-gather.18.cloned.1.call-start = ((), (), s32[]{:S(2)}) async-start(), calls=%async_computation.11 | async-start | bytes 7077888 | tf_op jit(solution)/shard_map/all_gather | solution.py:157
  76.4 230.1 %all-gather.20.cloned.1.call-start = ((), (), s32[]{:S(2)}) async-start(), calls=%async_computation.12 | async-start | bytes 1474560 | tf_op jit(solution)/shard_map/all_gather | solution.py:128
  78.2 241.6 %all-gather.22.cloned.1.call-start = ((), (), s32[]{:S(2)}) async-start(), calls=%async_computation.13 | async-start | bytes 3932160 | tf_op jit(solution)/shard_map/all_gather | solution.py:129
  80.8 269.1 %all-gather.24.cloned.1.call-start = ((), (), s32[]{:S(2)}) async-start(), calls=%async_computation.14 | async-start | bytes 3932160 | tf_op jit(solution)/shard_map/all_gather | solution.py:130
  83.5 296.6 %all-gather.26.cloned.1.call-start = ((), (), s32[]{:S(2)}) async-start(), calls=%async_computation.15 | async-start | bytes 3932160 | tf_op jit(solution)/shard_map/all_gather | solution.py:131
  86.0 1059.5 %reduce-scatter.14.cloned.1.call-start = ((), (), s32[]{:S(2)}) async-start(), calls=%async_computation.20 | async-start | bytes 1474560 | tf_op jit(solution)/shard_map/reduce_scatter | solution.py:360
  398.8 746.7 %reduce-scatter.10.cloned.1.call-start = ((), (), s32[]{:S(2)}) async-start(), calls=%async_computation.18 | async-start | bytes 1474560 | tf_op jit(solution)/shard_map/reduce_scatter | solution.py:354
  411.8 77.4 %collective-permute-start = (bf16[128,4,768]{0,2,1:T(8,128)(2,1)S(1)}, bf16[128,4,768]{0,2,1:T(8,128)(2,1)}, u32[]{:S(2)}, u32[]{:S(2)}) collective-permute-start(bf16[128,4,768]{0,2,1:T(8,128)(2,1)S(1)} %copy.175), channel_id=1, source_target_pairs={{0,4},{4,8},{8,12},{12,16},{16,20},{20,24},{24,28},{28,0},{1,5},{5... | collective-permute-start | bytes 2359304 | tf_op jit(solution)/shard_map/while/body/eval_jaxpr/ppermute | solution.py:25
  415.3 73.9 %collective-permute-start.1 = (bf16[128,4,768]{0,2,1:T(8,128)(2,1)}, bf16[128,4,768]{0,2,1:T(8,128)(2,1)}, u32[]{:S(2)}, u32[]{:S(2)}) collective-permute-start(bf16[128,4,768]{0,2,1:T(8,128)(2,1)} %copy.176), channel_id=1, source_target_pairs={{0,4},{4,8},{8,12},{12,16},{16,20},{20,24},{24,28},{28,0},{1,5},{5... | collective-permute-start | bytes 2359304 | tf_op jit(solution)/shard_map/while/body/eval_jaxpr/ppermute | solution.py:25
  490.7 73.8 %collective-permute-start = (bf16[128,4,768]{0,2,1:T(8,128)(2,1)S(1)}, bf16[128,4,768]{0,2,1:T(8,128)(2,1)}, u32[]{:S(2)}, u32[]{:S(2)}) collective-permute-start(bf16[128,4,768]{0,2,1:T(8,128)(2,1)S(1)} %copy.175), channel_id=1, source_target_pairs={{0,4},{4,8},{8,12},{12,16},{16,20},{20,24},{24,28},{28,0},{1,5},{5... | collective-permute-start | bytes 2359304 | tf_op jit(solution)/shard_map/while/body/eval_jaxpr/ppermute | solution.py:25
  565.9 72.8 %collective-permute-start = (bf16[128,4,768]{0,2,1:T(8,128)(2,1)S(1)}, bf16[128,4,768]{0,2,1:T(8,128)(2,1)}, u32[]{:S(2)}, u32[]{:S(2)}) collective-permute-start(bf16[128,4,768]{0,2,1:T(8,128)(2,1)S(1)} %copy.175), channel_id=1, source_target_pairs={{0,4},{4,8},{8,12},{12,16},{16,20},{20,24},{24,28},{28,0},{1,5},{5... | collective-permute-start | bytes 2359304 | tf_op jit(solution)/shard_map/while/body/eval_jaxpr/ppermute | solution.py:25
  640.1 72.8 %collective-permute-start = (bf16[128,4,768]{0,2,1:T(8,128)(2,1)S(1)}, bf16[128,4,768]{0,2,1:T(8,128)(2,1)}, u32[]{:S(2)}, u32[]{:S(2)}) collective-permute-start(bf16[128,4,768]{0,2,1:T(8,128)(2,1)S(1)} %copy.175), channel_id=1, source_target_pairs={{0,4},{4,8},{8,12},{12,16},{16,20},{20,24},{24,28},{28,0},{1,5},{5... | collective-permute-start | bytes 2359304 | tf_op jit(solution)/shard_map/while/body/eval_jaxpr/ppermute | solution.py:25
  788.4 73.2 %collective-permute-start = (bf16[128,4,768]{0,2,1:T(8,128)(2,1)S(1)}, bf16[128,4,768]{0,2,1:T(8,128)(2,1)}, u32[]{:S(2)}, u32[]{:S(2)}) collective-permute-start(bf16[128,4,768]{0,2,1:T(8,128)(2,1)S(1)} %copy.175), channel_id=1, source_target_pairs={{0,4},{4,8},{8,12},{12,16},{16,20},{20,24},{24,28},{28,0},{1,5},{5... | collective-permute-start | bytes 2359304 | tf_op jit(solution)/shard_map/while/body/eval_jaxpr/ppermute | solution.py:25
  863.0 73.6 %collective-permute-start = (bf16[128,4,768]{0,2,1:T(8,128)(2,1)S(1)}, bf16[128,4,768]{0,2,1:T(8,128)(2,1)}, u32[]{:S(2)}, u32[]{:S(2)}) collective-permute-start(bf16[128,4,768]{0,2,1:T(8,128)(2,1)S(1)} %copy.175), channel_id=1, source_target_pairs={{0,4},{4,8},{8,12},{12,16},{16,20},{20,24},{24,28},{28,0},{1,5},{5... | collective-permute-start | bytes 2359304 | tf_op jit(solution)/shard_map/while/body/eval_jaxpr/ppermute | solution.py:25
  938.1 73.8 %collective-permute-start = (bf16[128,4,768]{0,2,1:T(8,128)(2,1)S(1)}, bf16[128,4,768]{0,2,1:T(8,128)(2,1)}, u32[]{:S(2)}, u32[]{:S(2)}) collective-permute-start(bf16[128,4,768]{0,2,1:T(8,128)(2,1)S(1)} %copy.175), channel_id=1, source_target_pairs={{0,4},{4,8},{8,12},{12,16},{16,20},{20,24},{24,28},{28,0},{1,5},{5... | collective-permute-start | bytes 2359304 | tf_op jit(solution)/shard_map/while/body/eval_jaxpr/ppermute | solution.py:25
  1015.6 129.9 %reduce-scatter.12.cloned.1.call-start = ((), (), s32[]{:S(2)}) async-start(), calls=%async_computation.19 | async-start | bytes 1474560 | tf_op jit(solution)/shard_map/reduce_scatter | solution.py:357
  1018.9 126.6 %reduce-scatter.8.cloned.1.call-start = ((), (), s32[]{:S(2)}) async-start(), calls=%async_computation.17 | async-start | bytes 1474560 | tf_op jit(solution)/shard_map/reduce_scatter | solution.py:351
  1022.3 123.2 %reduce-scatter.18.cloned.1.call-start = ((), (), s32[]{:S(2)}) async-start(), calls=%async_computation.22 | async-start | bytes 3932160 | tf_op jit(solution)/shard_map/reduce_scatter | solution.py:366
  1027.4 149.0 %reduce-scatter.16.cloned.1.call-start = ((), (), s32[]{:S(2)}) async-start(), calls=%async_computation.21 | async-start | bytes 3932160 | tf_op jit(solution)/shard_map/reduce_scatter | solution.py:363
  1032.6 184.2 %reduce-scatter.20.cloned.1.call-start = ((), (), s32[]{:S(2)}) async-start(), calls=%async_computation.23 | async-start | bytes 3932160 | tf_op jit(solution)/shard_map/reduce_scatter | solution.py:369
  1049.5 326.0 %all-reduce.48.cloned.1.call-start = ((), (), s32[]{:S(2)}) async-start(), calls=%async_computation.24 | async-start | bytes 7888896 | tf_op jit(solution)/shard_map/psum | solution.py:381
  1216.8 219.6 %all-reduce.46.cloned.1.call-start = ((), (), s32[]{:S(2)}) async-start(), calls=%async_computation.16 | async-start | bytes 811008 | tf_op jit(solution)/shard_map/psum | solution.py:389
  (174 other events, 2952.6 us)
Sparse Core Ops, SparseCore 0:
  10.2 20.1 all-gather.11
  32.5 17.4 all-gather.15
  52.2 17.4 all-gather.9
  72.3 99.2 all-gather.13
  174.2 97.2 all-gather.17
  273.5 15.6 all-gather.19
  291.3 28.5 all-gather.21
  321.4 28.5 all-gather.23
  351.5 28.5 all-gather.25
  398.9 25.7 reduce-scatter.13
  1015.7 23.1 reduce-scatter.9
  1041.3 25.7 reduce-scatter.11
  1069.8 25.6 reduce-scatter.7
  1097.9 37.9 reduce-scatter.17
  1138.4 37.9 reduce-scatter.15
  1178.8 37.9 reduce-scatter.19
  1222.5 152.9 all-reduce.47
  1377.7 31.0 all-reduce.45
where the time goes:
time: 1460 us; the launch traced here: 1450 us
  local copies, waits for them, and re-layouts  469 us (32%)
  waiting for transfers between devices  436 us (30%)
  other arithmetic  200 us (14%)
  matrix products  198 us (14%)
  blocking collectives  71.8 us (5%)
  starting transfers between devices  52 us (4%)
  between operations  15.5 us (1%)
    psum x1, waiting for transfers between devices, local(): lax.psum(grad_table_part.astype(jnp.bfloat16), 'ctx').astype(jnp.float32)  159 us
    ppermute x40, waiting for transfers between devices, from_behind(): return lax.ppermute(value, axis, pairs)  87.5 us
    reshape x17, local copies, waits for them, and re-layouts, block_bias(): toeplitz = strided.reshape(head_count, query_count, span_len - 1)  77.6 us
    all_gather x1, waiting for transfers between devices, local(): value_piece = lax.all_gather(values3, 'ctx', axis=0, tiled=True)  55 us
    while x192, local copies, waits for them, and re-layouts  52.5 us
    another operation x18, local copies, waits for them, and re-layouts, block_bias(): repeated = jnp.tile(per_offset, (1, query_count))  47.7 us
    ppermute x40, starting transfers between devices, from_behind(): return lax.ppermute(value, axis, pairs)  45.1 us
    another operation x16, local copies, waits for them, and re-layouts, block_grads(): q_four = query_piece.reshape(query_rows, seq_count, heads, head_size)  41.9 us
  transfers between devices with their start and end apart: 60, of which 18 were waited for; matrix products, arithmetic and copies ran while one was open for 56% of the time, Pallas kernels for 0%

commit v1 on v0

v1 whole, which is shorter than its diff:
```python
import functools

import jax
import jax.numpy as jnp
from jax import lax
from jax.experimental import pallas as pl
from jax.experimental.pallas import tpu as pltpu
from jax.sharding import PartitionSpec as P

f32 = jnp.float32
bf16 = jnp.bfloat16
LANE = 128
BLK = 128
VMEM_CAP = 60 * 1024 * 1024
HIGH = lax.Precision.HIGHEST
NT = (((1,), (1,)), ((), ()))
NN = (((1,), (0,)), ((), ()))


def lane_iota(rows):
    return lax.broadcasted_iota(jnp.int32, (rows, LANE), 1)


def block_sum(value, width, lane):
    def ahead(v, n):
        return pltpu.roll(v, LANE - n, 1)

    def behind(v, n):
        return pltpu.roll(v, n, 1)

    if width == 1:
        return value
    if width == 3:
        lead = value + ahead(value, 1) + ahead(value, 2)
        phase = lane % 3
        return jnp.where(phase == 0, lead, jnp.where(phase == 1, behind(lead, 1), behind(lead, 2)))
    pair = value + jnp.where(lane % 2 == 0, ahead(value, 1), behind(value, 1))
    if width == 2:
        return pair
    return pair + jnp.where(lane % 4 < 2, ahead(pair, 2), behind(pair, 2))


def pick(value, lane_index):
    return value[:, lane_index : lane_index + 1]


def byte_forward_kernel(
    total_bytes,
    ids_ref,
    hi_ref,
    lo_ref,
    conv_w_ref,
    score_ref,
    gain_ref,
    tok_ref,
    norm_ref,
    conv_ref,
    mix_ref,
    emb,
    flat,
):
    groups = conv_ref.shape[1]
    width = conv_ref.shape[2]
    tiles = width // LANE
    token_count = norm_ref.shape[0]
    vocab_pad = hi_ref.shape[0]
    ids_cols = jnp.transpose(ids_ref[...].astype(f32))
    vocab = lax.broadcasted_iota(jnp.int32, (groups, vocab_pad), 1).astype(f32)
    for r in range(15):
        onehot = (ids_cols[0:groups, r : r + 1] == vocab).astype(bf16)
        emb[r] = jnp.dot(onehot, hi_ref[...], preferred_element_type=f32) + jnp.dot(
            onehot, lo_ref[...], preferred_element_type=f32
        )
    lane = lane_iota(8)

    def chunk(i, masked):
        r0 = pl.multiple_of(i * 8, 8)
        rows = pl.ds(r0, 8)
        sums = [jnp.zeros((8, LANE), f32) for _ in range(12)]
        for tile in range(tiles):
            cols = slice(tile * LANE, (tile + 1) * LANE)
            taps = [conv_w_ref[k : k + 1, cols] for k in range(4)]
            piece = [emb[r, rows, cols] for r in range(15)]
            score = score_ref[0:1, cols]
            for r in range(12):
                value = (
                    piece[r] * taps[0]
                    + piece[r + 1] * taps[1]
                    + piece[r + 2] * taps[2]
                    + piece[r + 3] * taps[3]
                )
                if masked:
                    group = r0 + lax.broadcasted_iota(jnp.int32, (8, LANE), 0)
                    value = jnp.where(group * 12 + r < total_bytes, value, 0.0)
                conv_ref[r, rows, cols] = value
                sums[r] = sums[r] + value * score
        packed = jnp.zeros((8, LANE), f32)
        for r in range(12):
            packed = jnp.where(lane == r, jnp.sum(sums[r], axis=1, keepdims=True), packed)
        logits = [block_sum(packed, b, lane) * (1.0 / b) for b in range(1, 5)]
        best = jnp.maximum(jnp.maximum(logits[0], logits[1]), jnp.maximum(logits[2], logits[3]))
        parts = [jnp.exp(value - best) for value in logits]
        total = parts[0] + parts[1] + parts[2] + parts[3]
        mix = [part / total for part in parts]
        for b in range(4):
            mix_ref[b, rows, :] = mix[b]
        half_one = mix[0] * 0.5
        pair_two = block_sum(mix[1], 2, lane) * 0.25
        single_three = mix[2] * (1.0 / 6.0)
        pair_three = block_sum(mix[2], 2, lane) * (1.0 / 6.0)
        pair_four = block_sum(mix[3], 2, lane) * 0.125
        coef_one = [pick(half_one, r) for r in range(12)]
        coef_two = [pick(pair_two, 2 * j) for j in range(6)]
        coef_four = [pick(pair_four, 2 * j) for j in range(6)]
        coef_three = []
        for j in range(6):
            if j % 3 == 1:
                coef_three.append((pick(single_three, 2 * j), pick(single_three, 2 * j + 1)))
            else:
                coef_three.append((pick(pair_three, 2 * j), None))
        for tile in range(tiles):
            cols = slice(tile * LANE, (tile + 1) * LANE)
            conv = [conv_ref[r, rows, cols] for r in range(12)]
            two = [conv[2 * j] + conv[2 * j + 1] for j in range(6)]
            three = [conv[3 * q] + conv[3 * q + 1] + conv[3 * q + 2] for q in range(4)]
            four = [two[2 * q] + two[2 * q + 1] for q in range(3)]
            for j in range(6):
                a, b = 2 * j, 2 * j + 1
                value = coef_one[a] * conv[a] + coef_one[b] * conv[b]
                value = value + coef_two[j] * two[j] + coef_four[j] * four[j // 2]
                value = value + coef_three[j][0] * three[a // 3]
                if j % 3 == 1:
                    value = value + coef_three[j][1] * three[b // 3]
                flat[tile, pl.ds(6 * r0 + j, 8, stride=6), :] = value

    whole = (total_bytes // 12) // 8

    def plain(i, carry):
        chunk(i, False)
        return carry

    lax.fori_loop(0, whole, plain, 0)
    for i in range(whole, groups // 8):
        chunk(i, True)

    def norm(i, carry):
        rows = pl.ds(pl.multiple_of(i * 16, 16), 16)
        value = jnp.concatenate([flat[tile, rows, :] for tile in range(tiles)], axis=1)
        tok_ref[rows, :] = value
        scale = lax.rsqrt(jnp.mean(value * value, axis=1, keepdims=True) + 1e-06)
        norm_ref[rows, :] = (value * scale * gain_ref[...]).astype(bf16)
        return carry

    lax.fori_loop(0, token_count // 16, norm, 0)


def phase_ids(ids_row, total_bytes):
    groups = -(-total_bytes // 12)
    padded = jnp.pad(ids_row, (0, 12 * groups - total_bytes), constant_values=-1)
    phases = jnp.transpose(padded.reshape(groups, 12))
    before = jnp.pad(phases[9:12, :-1], ((0, 0), (1, 0)), constant_values=-1)
    lanes = -(-groups // LANE) * LANE
    both = jnp.concatenate([before, phases], axis=0)
    return jnp.pad(both, ((0, 1), (0, lanes - groups)), constant_values=-1)


def byte_forward(ids, hi, lo, conv_w, score_w, gain_one, total_bytes):
    width = conv_w.shape[1]
    token_count = total_bytes // 2
    groups = -(-(-(-total_bytes // 12)) // 16) * 16
    return pl.pallas_call(
        functools.partial(byte_forward_kernel, total_bytes),
        out_shape=(
            jax.ShapeDtypeStruct((token_count, width), f32),
            jax.ShapeDtypeStruct((token_count, width), bf16),
            jax.ShapeDtypeStruct((12, groups, width), f32),
            jax.ShapeDtypeStruct((4, groups, LANE), f32),
        ),
        scratch_shapes=[
            pltpu.VMEM((15, groups, width), f32),
            pltpu.VMEM((width // LANE, 6 * groups, LANE), f32),
        ],
        compiler_params=pltpu.CompilerParams(vmem_limit_bytes=VMEM_CAP),
        name="byte_forward",
    )(ids, hi, lo, conv_w, score_w.reshape(1, width), gain_one.reshape(1, width))


def byte_backward_kernel(
    total_bytes,
    first_ref,
    ids_ref,
    tok_ref,
    dnorm_ref,
    dres_ref,
    conv_ref,
    mix_ref,
    table_ref,
    conv_w_ref,
    score_ref,
    gain_ref,
    out_ref,
    dtok,
    dconv,
    onehot,
):
    groups = conv_ref.shape[1]
    width = conv_ref.shape[2]
    tiles = width // LANE
    token_count = dnorm_ref.shape[0]
    vocab_rows = onehot.shape[0]
    lanes = ids_ref.shape[1]
    gain = gain_ref[...]

    def norm_back(i, acc):
        rows = pl.ds(pl.multiple_of(i * 8, 8), 8)
        value = tok_ref[rows, :]
        grad = dnorm_ref[rows, :]
        scale = lax.rsqrt(jnp.mean(value * value, axis=1, keepdims=True) + 1e-06)
        grad_gain = grad * gain
        inner = jnp.mean(value * grad_gain, axis=1, keepdims=True)
        total = 0.5 * scale * grad_gain - value * (0.5 * scale * scale * scale * inner)
        for tile in range(tiles):
            dtok[tile, rows, :] = total[:, tile * LANE : (tile + 1) * LANE]
        return acc + grad * value * scale

    gain_acc = lax.fori_loop(0, token_count // 8, norm_back, jnp.zeros((8, width), f32))
    rest = dtok.shape[1] - token_count
    dtok[:, token_count:, :] = jnp.zeros((tiles, rest, LANE), f32)
    for slot in range(dres_ref.shape[0]):
        start = pl.multiple_of(first_ref[slot] * BLK, BLK)

        def add(i, carry, slot=slot, start=start):
            r = pl.multiple_of(i * 8, 8)
            rows = pl.ds(start + r, 8)
            more = 0.5 * dres_ref[slot, pl.ds(r, 8), :]
            for tile in range(tiles):
                dtok[tile, rows, :] = (
                    dtok[tile, rows, :] + more[:, tile * LANE : (tile + 1) * LANE]
                )
            return carry

        lax.fori_loop(0, BLK // 8, add, 0)
    vocab = lax.broadcasted_iota(jnp.int32, (vocab_rows, lanes), 0)
    for r in range(15):
        onehot[:, r * lanes : (r + 1) * lanes] = (vocab == ids_ref[r : r + 1, :]).astype(bf16)
    for r in range(12):
        dconv[r * lanes + groups : (r + 1) * lanes, :] = jnp.zeros((lanes - groups, width), bf16)
    lane = lane_iota(8)

    def scalars(r0):
        rows = pl.ds(r0, 8)
        one = [jnp.zeros((8, LANE), f32) for _ in range(12)]
        cross = [jnp.zeros((8, LANE), f32) for _ in range(6)]
        tri = [jnp.zeros((8, LANE), f32) for _ in range(8)]
        for tile in range(tiles):
            cols = slice(tile * LANE, (tile + 1) * LANE)
            conv = [conv_ref[r, rows, cols] for r in range(12)]
            grad = [dtok[tile, pl.ds(6 * r0 + j, 8, stride=6), :] for j in range(6)]
            two = [conv[2 * j] + conv[2 * j + 1] for j in range(6)]
            three = [conv[3 * q] + conv[3 * q + 1] + conv[3 * q + 2] for q in range(4)]
            for r in range(12):
                one[r] = one[r] + conv[r] * grad[r // 2]
            slot = 0
            for j in range(6):
                cross[j] = cross[j] + two[j ^ 1] * grad[j]
                for q in sorted({(2 * j) // 3, (2 * j + 1) // 3}):
                    tri[slot] = tri[slot] + three[q] * grad[j]
                    slot += 1
        inner_one = jnp.zeros((8, LANE), f32)
        for r in range(12):
            inner_one = jnp.where(lane == r, jnp.sum(one[r], axis=1, keepdims=True), inner_one)
        inner_cross = jnp.zeros((8, LANE), f32)
        for j in range(6):
            inner_cross = jnp.where(
                lane // 2 == j, jnp.sum(cross[j], axis=1, keepdims=True), inner_cross
            )
        inner_three = jnp.zeros((8, LANE), f32)
        slot = 0
        for j in range(6):
            for q in sorted({(2 * j) // 3, (2 * j + 1) // 3}):
                here = (lane // 2 == j) & (lane // 3 == q)
                inner_three = jnp.where(
                    here, jnp.sum(tri[slot], axis=1, keepdims=True), inner_three
                )
                slot += 1
        inner_two = block_sum(inner_one, 2, lane)
        mix = [mix_ref[b, rows, :] for b in range(4)]
        d_mix = [
            inner_one,
            inner_two * 0.5,
            inner_three * (1.0 / 3.0),
            (inner_two + inner_cross) * 0.25,
        ]
        mean = mix[0] * d_mix[0] + mix[1] * d_mix[1] + mix[2] * d_mix[2] + mix[3] * d_mix[3]
        d_logit = [mix[b] * (d_mix[b] - mean) for b in range(4)]
        d_logit = [jnp.where(lane < 12, value, 0.0) for value in d_logit]
        slope = d_logit[0]
        for b in range(2, 5):
            slope = slope + block_sum(d_logit[b - 1], b, lane) * (1.0 / b)
        pair_two = block_sum(mix[1], 2, lane) * 0.5
        single_three = mix[2] * (1.0 / 3.0)
        pair_three = block_sum(mix[2], 2, lane) * (1.0 / 3.0)
        pair_four = block_sum(mix[3], 2, lane) * 0.25
        return mix[0], pair_two, single_three, pair_three, pair_four, slope

    def spread(r0, coefs, tile, masked, score_acc):
        one, pair_two, single_three, pair_three, pair_four, slope = coefs
        rows = pl.ds(r0, 8)
        cols = slice(tile * LANE, (tile + 1) * LANE)
        grad = [dtok[tile, pl.ds(6 * r0 + j, 8, stride=6), :] for j in range(6)]
        score = score_ref[0:1, cols]
        four = [
            pick(pair_four, 4 * q) * grad[2 * q] + pick(pair_four, 4 * q + 2) * grad[2 * q + 1]
            for q in range(3)
        ]
        three = []
        for q in range(4):
            a = 3 * q
            if a % 2 == 0:
                three.append(
                    pick(pair_three, a) * grad[a // 2]
                    + pick(single_three, a + 2) * grad[a // 2 + 1]
                )
            else:
                three.append(
                    pick(single_three, a) * grad[a // 2]
                    + pick(pair_three, a + 1) * grad[a // 2 + 1]
                )
        result = []
        for r in range(12):
            weight = pick(slope, r)
            own = (pick(one, r) + pick(pair_two, r)) * grad[r // 2]
            value = own + three[r // 3] + four[r // 4] + weight * score
            score_acc = score_acc + weight * conv_ref[r, rows, cols]
            if masked:
                group = r0 + lax.broadcasted_iota(jnp.int32, (8, LANE), 0)
                value = jnp.where(group * 12 + r < total_bytes, value, 0.0)
            result.append(value)
        return result, score_acc

    def chunk(i, accs, masked):
        r0 = pl.multiple_of(i * 16, 16)
        r1 = pl.multiple_of(i * 16 + 8, 8)
        low_coefs = scalars(r0)
        high_coefs = scalars(r1)
        new = []
        for tile in range(tiles):
            cols = slice(tile * LANE, (tile + 1) * LANE)
            low, acc = spread(r0, low_coefs, tile, masked, accs[tile])
            high, acc = spread(r1, high_coefs, tile, masked, acc)
            new.append(acc)
            for r in range(12):
                both = jnp.concatenate([low[r], high[r]], axis=0).astype(bf16)
                dconv[pl.ds(pl.multiple_of(r * lanes + r0, 16), 16), cols] = both
        return tuple(new)

    accs = tuple(jnp.zeros((8, LANE), f32) for _ in range(tiles))
    whole = (total_bytes // 12) // 16
    accs = lax.fori_loop(0, whole, lambda i, a: chunk(i, a, False), accs)
    for i in range(whole, groups // 16):
        accs = chunk(i, accs, True)
    tail = [jnp.zeros((1, width), f32) for _ in range(8)]
    for k in range(4):
        part = jnp.dot(
            onehot[:, k * lanes : (k + 12) * lanes], dconv[...], preferred_element_type=f32
        )
        if k == 0:
            out_ref[0:vocab_rows, :] = part * conv_w_ref[k : k + 1, :]
        else:
            out_ref[0:vocab_rows, :] = out_ref[0:vocab_rows, :] + part * conv_w_ref[k : k + 1, :]
        tail[k] = jnp.sum(part * table_ref[...], axis=0, keepdims=True)
    tail[4] = jnp.sum(jnp.concatenate(accs, axis=1), axis=0, keepdims=True)
    tail[5] = jnp.sum(gain_acc, axis=0, keepdims=True)
    out_ref[vocab_rows:, :] = jnp.concatenate(tail, axis=0)


def byte_backward(
    first, ids, tokens, d_norm, d_resid, conv, mix, table, conv_w, score_w, gain_one, total_bytes
):
    width = conv.shape[2]
    groups = conv.shape[1]
    lanes = ids.shape[1]
    vocab_rows = table.shape[0]
    return pl.pallas_call(
        functools.partial(byte_backward_kernel, total_bytes),
        out_shape=jax.ShapeDtypeStruct((vocab_rows + 8, width), f32),
        in_specs=[pl.BlockSpec(memory_space=pltpu.SMEM)]
        + [pl.BlockSpec(memory_space=pltpu.VMEM)] * 10,
        scratch_shapes=[
            pltpu.VMEM((width // LANE, 6 * groups, LANE), f32),
            pltpu.VMEM((12 * lanes, width), bf16),
            pltpu.VMEM((vocab_rows, 15 * lanes), bf16),
        ],
        compiler_params=pltpu.CompilerParams(vmem_limit_bytes=VMEM_CAP),
        name="byte_backward",
    )(
        first,
        ids,
        tokens,
        d_norm,
        d_resid,
        conv,
        mix,
        table,
        conv_w,
        score_w.reshape(1, width),
        gain_one.reshape(1, width),
    )


def head_mask(value, head):
    half = value.shape[1] // 2
    lane = lax.broadcasted_iota(jnp.int32, value.shape, 1)
    keep = lane < half if head == 0 else lane >= half
    return jnp.where(keep, value, jnp.zeros_like(value))


def two_heads(value):
    return jnp.concatenate([head_mask(value, 0), head_mask(value, 1)], axis=0)


def doc_operands(docs_ref, known, barred):
    blocks = docs_ref.shape[0]
    cols = jnp.transpose(docs_ref[...].astype(f32))
    lane = lane_iota(BLK).astype(f32)
    for b in range(blocks):
        same = cols[:, b : b + 1] == lane
        known[b * BLK : (b + 1) * BLK, :] = same.astype(bf16)
        barred[b * BLK : (b + 1) * BLK, :] = jnp.where(
            same | (lane >= 16.0), 0.0, -1e30
        ).astype(bf16)


def bias_tiles(buckets_ref, rel_ref, tiles):
    count = tiles.shape[0]
    blocks = buckets_ref.shape[0] // 2
    reach = count // 2
    levels = rel_ref.shape[1]
    level = lax.broadcasted_iota(jnp.int32, (levels, 2 * BLK), 0)
    for n in range(count):
        row = blocks - 1 - (n - reach)
        bucket = jnp.concatenate(
            [buckets_ref[row : row + 1, :], buckets_ref[row + 1 : row + 2, :]], axis=1
        )
        onehot = (level == bucket).astype(f32)
        values = lax.dot_general(
            rel_ref[...], onehot, NN, precision=HIGH, preferred_element_type=f32
        )
        for head in range(2):
            spread = jnp.broadcast_to(values[head : head + 1, :], (BLK, 2 * BLK))
            rolled = pltpu.roll(spread, BLK + 1, 1, stride=1, stride_axis=0)
            tiles[n, :, head * BLK : (head + 1) * BLK] = rolled[:, :BLK]


def attend_kernel(
    lead_ref,
    low_ref,
    high_ref,
    q_ref,
    k_ref,
    v_ref,
    docs_ref,
    buckets_ref,
    rel_ref,
    out_ref,
    low_out_ref,
    log_ref,
    known,
    barred,
    tiles,
    v_turned,
    held,
):
    reach = tiles.shape[0] // 2
    slots = q_ref.shape[0] // BLK

    @pl.when(pl.program_id(0) == 0)
    def _():
        doc_operands(docs_ref, known, barred)

    bias_tiles(buckets_ref, rel_ref.at[0], tiles)
    v_turned[...] = jnp.transpose(v_ref[...])
    for slot in range(slots):
        block = lead_ref[slot]
        first = low_ref[slot]
        last = high_ref[slot]
        base = pl.multiple_of(block * BLK, BLK)
        q_two = two_heads(q_ref[slot * BLK : (slot + 1) * BLK, :])
        bar = barred[pl.ds(base, BLK), :]
        q_full = jnp.concatenate([q_two, jnp.concatenate([bar, bar], axis=0)], axis=1)

        def score(kb, best):
            rows = pl.ds(pl.multiple_of(kb * BLK, BLK), BLK)
            k_full = jnp.concatenate([k_ref[rows, :], known[rows, :]], axis=1)
            value = lax.dot_general(k_full, q_full, NT, preferred_element_type=f32)
            value = value + tiles[kb - block + reach]
            held[kb - first] = value
            return jnp.maximum(best, jnp.max(value.reshape(BLK // 8, 8, 2 * BLK), axis=0))

        best = lax.fori_loop(first, last, score, jnp.full((8, 2 * BLK), -3e38, f32))
        best = jnp.max(best, axis=0, keepdims=True)

        def gather(kb, state):
            total, accum = state
            weight = jnp.exp(held[kb - first] - best)
            total = total + jnp.sum(weight.reshape(BLK // 8, 8, 2 * BLK), axis=0)
            cols = pl.ds(pl.multiple_of(kb * BLK, BLK), BLK)
            accum = accum + jnp.dot(
                v_turned[:, cols], weight.astype(bf16), preferred_element_type=f32
            )
            return total, accum

        total, accum = lax.fori_loop(
            first,
            last,
            gather,
            (jnp.zeros((8, 2 * BLK), f32), jnp.zeros((BLK, 2 * BLK), f32)),
        )
        total = jnp.sum(total, axis=0, keepdims=True)
        accum = accum / total
        half = BLK // 2
        both = jnp.concatenate([accum[:half, :BLK], accum[half:, BLK:]], axis=0)
        both = jnp.transpose(both)
        out_ref[slot * BLK : (slot + 1) * BLK, :] = both
        low_out_ref[slot * BLK : (slot + 1) * BLK, :] = both.astype(bf16)
        log_ref[0, slot : slot + 1, :] = best + jnp.log(total)


def attend(lead, low, high, q, k, v, docs, buckets, rel):
    rows, width = q.shape
    keys = k.shape[0]
    pairs = width // BLK
    blocks = docs.shape[0]
    slots = rows // BLK
    reach = blocks // 2
    smem = pl.BlockSpec(memory_space=pltpu.SMEM)

    def cols(count):
        return pl.BlockSpec((count, BLK), lambda i: (0, i))

    def whole(array):
        return pl.BlockSpec(array.shape, lambda i: (0,) * array.ndim)

    return pl.pallas_call(
        attend_kernel,
        grid=(pairs,),
        out_shape=(
            jax.ShapeDtypeStruct((rows, width), f32),
            jax.ShapeDtypeStruct((rows, width), bf16),
            jax.ShapeDtypeStruct((pairs, slots, 2 * BLK), f32),
        ),
        in_specs=[
            smem,
            smem,
            smem,
            cols(rows),
            cols(keys),
            cols(keys),
            whole(docs),
            whole(buckets),
            pl.BlockSpec((1,) + rel.shape[1:], lambda i: (i, 0, 0)),
        ],
        out_specs=(
            cols(rows),
            cols(rows),
            pl.BlockSpec((1, slots, 2 * BLK), lambda i: (i, 0, 0)),
        ),
        scratch_shapes=[
            pltpu.VMEM((keys, BLK), bf16),
            pltpu.VMEM((keys, BLK), bf16),
            pltpu.VMEM((2 * reach + 1, BLK, 2 * BLK), f32),
            pltpu.VMEM((BLK, keys), bf16),
            pltpu.VMEM((blocks, BLK, 2 * BLK), f32),
        ],
        compiler_params=pltpu.CompilerParams(vmem_limit_bytes=VMEM_CAP),
        name="attend",
    )(lead, low, high, q, k, v, docs, buckets, rel)


def attend_back_kernel(
    lead_ref,
    low_ref,
    high_ref,
    q_ref,
    k_ref,
    v_ref,
    g_ref,
    out_ref,
    log_ref,
    docs_ref,
    buckets_ref,
    rel_ref,
    dq_ref,
    dk_ref,
    dv_ref,
    dbias_ref,
    known,
    barred,
    tiles,
    k_turned,
    dk_acc,
    dv_acc,
    d_tiles,
):
    reach = tiles.shape[0] // 2
    count = tiles.shape[0]
    blocks = docs_ref.shape[0]
    slots = q_ref.shape[0] // BLK
    half = BLK // 2

    @pl.when(pl.program_id(0) == 0)
    def _():
        doc_operands(docs_ref, known, barred)

    bias_tiles(buckets_ref, rel_ref.at[0], tiles)
    k_turned[...] = jnp.transpose(k_ref[...])
    dk_acc[...] = jnp.zeros_like(dk_acc)
    dv_acc[...] = jnp.zeros_like(dv_acc)
    d_tiles[...] = jnp.zeros_like(d_tiles)
    sub = lax.broadcasted_iota(jnp.int32, (8, BLK), 0)
    lane = lane_iota(8)
    chooser = jnp.where((lane // half) == sub, 1.0, 0.0)
    for slot in range(slots):
        block = lead_ref[slot]
        first = low_ref[slot]
        last = high_ref[slot]
        base = pl.multiple_of(block * BLK, BLK)
        own = slice(slot * BLK, (slot + 1) * BLK)
        q_two = two_heads(q_ref[own, :])
        g_two = two_heads(g_ref[own, :])
        bar = barred[pl.ds(base, BLK), :]
        q_full = jnp.concatenate([q_two, jnp.concatenate([bar, bar], axis=0)], axis=1)
        product = g_ref[own, :].astype(f32) * out_ref[own, :]
        delta = lax.dot_general(chooser, product, NT, precision=HIGH, preferred_element_type=f32)
        delta = jnp.concatenate([delta[0:1, :], delta[1:2, :]], axis=1)
        log_total = log_ref[0, slot : slot + 1, :]

        def step(kb, dq):
            rows = pl.ds(pl.multiple_of(kb * BLK, BLK), BLK)
            k_full = jnp.concatenate([k_ref[rows, :], known[rows, :]], axis=1)
            value = lax.dot_general(k_full, q_full, NT, preferred_element_type=f32)
            prob = jnp.exp(value + tiles[kb - block + reach] - log_total)
            d_prob = lax.dot_general(v_ref[rows, :], g_two, NT, preferred_element_type=f32)
            d_score = prob * (d_prob - delta)
            d_tiles[kb - block + reach] = d_tiles[kb - block + reach] + d_score
            d_low = d_score.astype(bf16)
            dv_acc[rows, :] = dv_acc[rows, :] + jnp.dot(
                prob.astype(bf16), g_two, preferred_element_type=f32
            )
            dk_acc[rows, :] = dk_acc[rows, :] + jnp.dot(
                d_low, q_two, preferred_element_type=f32
            )
            return dq + jnp.dot(k_turned[:, rows], d_low, preferred_element_type=f32)

        dq = lax.fori_loop(first, last, step, jnp.zeros((BLK, 2 * BLK), f32))
        both = jnp.concatenate([dq[:half, :BLK], dq[half:, BLK:]], axis=0)
        dq_ref[own, :] = jnp.transpose(both).astype(bf16)
    dk_ref[...] = dk_acc[...].astype(bf16)
    dv_ref[...] = dv_acc[...].astype(bf16)
    levels = rel_ref.shape[2]
    level = lax.broadcasted_iota(jnp.int32, (levels, 2 * BLK), 0)
    total = jnp.zeros((8, levels), f32)
    pad = jnp.zeros((BLK, BLK), f32)
    mirror = (
        lax.broadcasted_iota(jnp.int32, (BLK, BLK), 0)
        + lax.broadcasted_iota(jnp.int32, (BLK, BLK), 1)
        == BLK - 1
    ).astype(bf16)
    for n in range(count):
        flipped = jnp.dot(mirror, d_tiles[n].astype(bf16), preferred_element_type=f32)
        row = blocks - 1 - (n - reach)
        bucket = jnp.concatenate(
            [buckets_ref[row : row + 1, :], buckets_ref[row + 1 : row + 2, :]], axis=1
        )
        onehot = (level == bucket).astype(f32)
        sums = []
        for head in range(2):
            part = flipped[:, head * BLK : (head + 1) * BLK]
            wide = jnp.concatenate([part, pad], axis=1)
            rolled = pltpu.roll(wide, 0, 1, stride=1, stride_axis=0)
            sums.append(jnp.sum(rolled, axis=0, keepdims=True))
        stacked = jnp.concatenate(sums + [jnp.zeros((6, 2 * BLK), f32)], axis=0)
        total = total + lax.dot_general(
            stacked, onehot, NT, precision=HIGH, preferred_element_type=f32
        )
    dbias_ref[0] = total


def attend_back(lead, low, high, q, k, v, g, out, log, docs, buckets, rel):
    rows, width = q.shape
    keys = k.shape[0]
    pairs = width // BLK
    blocks = docs.shape[0]
    slots = rows // BLK
    reach = blocks // 2
    levels = rel.shape[2]
    smem = pl.BlockSpec(memory_space=pltpu.SMEM)

    def cols(count):
        return pl.BlockSpec((count, BLK), lambda i: (0, i))

    def whole(array):
        return pl.BlockSpec(array.shape, lambda i: (0,) * array.ndim)

    def lead_block(shape):
        return pl.BlockSpec((1,) + shape, lambda i: (i,) + (0,) * len(shape))

    return pl.pallas_call(
        attend_back_kernel,
        grid=(pairs,),
        out_shape=(
            jax.ShapeDtypeStruct((rows, width), bf16),
            jax.ShapeDtypeStruct((keys, width), bf16),
            jax.ShapeDtypeStruct((keys, width), bf16),
            jax.ShapeDtypeStruct((pairs, 8, levels), f32),
        ),
        in_specs=[
            smem,
            smem,
            smem,
            cols(rows),
            cols(keys),
            cols(keys),
            cols(rows),
            cols(rows),
            lead_block((slots, 2 * BLK)),
            whole(docs),
            whole(buckets),
            lead_block(rel.shape[1:]),
        ],
        out_specs=(cols(rows), cols(keys), cols(keys), lead_block((8, levels))),
        scratch_shapes=[
            pltpu.VMEM((keys, BLK), bf16),
            pltpu.VMEM((keys, BLK), bf16),
            pltpu.VMEM((2 * reach + 1, BLK, 2 * BLK), f32),
            pltpu.VMEM((BLK, keys), bf16),
            pltpu.VMEM((keys, BLK), f32),
            pltpu.VMEM((keys, BLK), f32),
            pltpu.VMEM((2 * reach + 1, BLK, 2 * BLK), f32),
        ],
        compiler_params=pltpu.CompilerParams(vmem_limit_bytes=VMEM_CAP),
        name="attend_back",
    )(lead, low, high, q, k, v, g, out, log, docs, buckets, rel)


def attention_tables(docs, rel_bucket, rel_bias, lead):
    blocks = docs.shape[0]
    starts = docs[:, 0]
    ends = docs[:, -1]
    own_start = jnp.take(starts, lead)
    own_end = jnp.take(ends, lead)
    low = jnp.sum((ends[None, :] < own_start[:, None]).astype(jnp.int32), axis=1)
    high = jnp.sum((starts[None, :] <= own_end[:, None]).astype(jnp.int32), axis=1)
    buckets = jnp.pad(jnp.flip(rel_bucket), (0, 1)).reshape(2 * blocks, BLK)
    levels, heads = rel_bias.shape
    rel = jnp.transpose(rel_bias).reshape(heads // 2, 2, levels)
    rel = jnp.pad(rel, ((0, 0), (0, 6), (0, 0)))
    return low, high, buckets, rel


def bits_of(count):
    bits = count.bit_length() - 1
    assert 1 << bits == count
    return bits


def swap(value, axis, bit):
    count = lax.axis_size(axis)
    return lax.ppermute(value, axis, [(i, i ^ (1 << bit)) for i in range(count)])


def ordered(mine, other, index, bit, axis=0):
    upper = ((index >> bit) & 1) == 1
    return jnp.concatenate(
        [jnp.where(upper, other, mine), jnp.where(upper, mine, other)], axis=axis
    )


def gather_small(value, axis):
    index = lax.axis_index(axis)
    value = value[None]
    for bit in range(bits_of(lax.axis_size(axis))):
        value = ordered(value, swap(value, axis, bit), index, bit)
    return value


def gather_rows(shard, axis):
    count = lax.axis_size(axis)
    index = lax.axis_index(axis)
    parts = [(0, shard)]
    for bit in reversed(range(bits_of(count))):
        parts = parts + [(j | (1 << bit), swap(part, axis, bit)) for j, part in parts]
    rows = shard.shape[0]
    result = jnp.zeros((rows * count,) + shard.shape[1:], shard.dtype)
    for j, part in parts:
        result = lax.dynamic_update_slice_in_dim(result, part, (index ^ j) * rows, axis=0)
    return result


def half_step(value, axis, bit, dim):
    index = lax.axis_index(axis)
    own = (index >> bit) & 1
    size = value.shape[dim] // 2
    keep = lax.dynamic_slice_in_dim(value, own * size, size, dim)
    send = lax.dynamic_slice_in_dim(value, (1 - own) * size, size, dim)
    other = swap(send.astype(bf16), axis, bit)
    return (keep.astype(f32) + other.astype(f32)).astype(bf16)


def reduce_rows(value, scatter_axis, sum_axis):
    count = lax.axis_size(scatter_axis)
    bits = bits_of(count)
    rows = value.shape[0] // count
    value = value.reshape((2,) * bits + (rows,) + value.shape[1:])
    for bit in range(bits):
        value = half_step(value, scatter_axis, bit, bits - 1 - bit)
    value = value.reshape((rows,) + value.shape[bits + 1 :])
    steps = bits_of(lax.axis_size(sum_axis))
    done = 0
    while done < steps and value.shape[0] % 2 == 0:
        value = half_step(value, sum_axis, done, 0)
        done += 1
    for bit in range(done, steps):
        value = (value.astype(f32) + swap(value, sum_axis, bit).astype(f32)).astype(bf16)
    index = lax.axis_index(sum_axis)
    for bit in reversed(range(done)):
        value = ordered(value, swap(value, sum_axis, bit), index, bit)
    return value


def reduce_all(value, axes):
    stages = [(axis, bit) for axis in axes for bit in range(bits_of(lax.axis_size(axis)))]
    halved = []
    for axis, bit in stages:
        if value.shape[0] % 2 == 0:
            value = half_step(value, axis, bit, 0)
            halved.append((axis, bit))
        else:
            value = (value.astype(f32) + swap(value, axis, bit).astype(f32)).astype(bf16)
    for axis, bit in reversed(halved):
        value = ordered(value, swap(value, axis, bit), lax.axis_index(axis), bit)
    return value


def rms_scale(values, gain_vec):
    return values * lax.rsqrt(jnp.mean(values * values, axis=-1, keepdims=True) + 1e-06) * gain_vec


def gelu_product(gate_pre, up_pre):
    return jax.nn.gelu(gate_pre, approximate=True) * up_pre


def local(
    byte_ids,
    doc_ids,
    rel_bucket,
    table,
    conv_w,
    score_w,
    gain_one,
    gain_two,
    rel_bias,
    query_master,
    key_master,
    value_master,
    out_master,
    gate_master,
    up_master,
    down_master,
    out_cotangent,
):
    ctx_count = lax.axis_size("ctx")
    ctx_index = lax.axis_index("ctx")
    seq_count, byte_count = byte_ids.shape
    total_bytes = byte_count * ctx_count
    width = table.shape[1]
    vocab = table.shape[0]
    hidden_width = gate_master.shape[1]
    levels, heads = rel_bias.shape
    share = ctx_count // seq_count
    assert share * seq_count == ctx_count and byte_count == 2 * BLK
    seq = ctx_index // share
    part = ctx_index % share
    near = [seq ^ slot for slot in range(seq_count)]
    lead = jnp.stack([share * other + part for other in near]).astype(jnp.int32)
    rows = seq_count * BLK

    both = jnp.stack([byte_ids, doc_ids], axis=1)
    both = gather_small(both, "ctx")
    both = lax.dynamic_index_in_dim(both, seq, 1, keepdims=False)
    ids = both[:, 0].reshape(total_bytes)
    docs = both[:, 1, ::2]

    qkv_low = jnp.concatenate([query_master, key_master, value_master], axis=1).astype(bf16)
    ogu_low = jnp.concatenate([out_master, gate_master, up_master], axis=1).astype(bf16)
    down_low = down_master.astype(bf16)
    qkv = gather_rows(qkv_low, "fsdp")
    ogu = gather_rows(ogu_low, "fsdp")
    down_weight = gather_rows(down_low, "fsdp")
    query_weight = qkv[:, :width]
    key_weight = qkv[:, width : 2 * width]
    value_weight = qkv[:, 2 * width :]
    out_weight = ogu[:, :width]
    gate_up = ogu[:, width:]

    def to_owner(block, slot):
        if slot == 0:
            return block
        pairs = []
        for c in range(ctx_count):
            pairs.append((c, ((c // share) ^ slot) * share + c % share))
        return lax.ppermute(block, "ctx", pairs)

    cotangent = jnp.concatenate(
        [
            to_owner(lax.dynamic_index_in_dim(out_cotangent, near[s], 1, keepdims=False), s)
            for s in range(seq_count)
        ],
        axis=0,
    )

    phases = phase_ids(ids, total_bytes)
    table_wide = jnp.pad(table, ((0, -vocab % LANE), (0, 0)))
    table_hi = lax.reduce_precision(table_wide, 8, 7)
    table_lo = (table_wide - table_hi).astype(bf16)
    tokens, norm_one, conv, mix = byte_forward(
        phases, table_hi.astype(bf16), table_lo, conv_w, score_w, gain_one, total_bytes
    )

    def own_rows(array):
        return jnp.concatenate(
            [lax.dynamic_slice_in_dim(array, lead[s] * BLK, BLK, 0) for s in range(seq_count)],
            axis=0,
        )

    tokens_own = own_rows(tokens)
    norm_own = own_rows(norm_one)

    queries = jnp.dot(norm_own, query_weight, preferred_element_type=f32).astype(bf16)
    keys = jnp.dot(norm_one, key_weight, preferred_element_type=f32).astype(bf16)
    values = jnp.dot(norm_one, value_weight, preferred_element_type=f32).astype(bf16)
    low, high, buckets, rel = attention_tables(docs, rel_bucket, rel_bias, lead)
    attended, attended_low, log_total = attend(
        lead, low, high, queries, keys, values, docs, buckets, rel
    )

    resid = tokens_own + jnp.dot(attended_low, out_weight, preferred_element_type=f32)
    norm_two = rms_scale(resid, gain_two).astype(bf16)
    gate_pre = jnp.dot(norm_two, gate_up[:, :hidden_width], preferred_element_type=f32)
    up_pre = jnp.dot(norm_two, gate_up[:, hidden_width:], preferred_element_type=f32)
    hidden = gelu_product(gate_pre, up_pre).astype(bf16)
    output = (resid + jnp.dot(hidden, down_weight, preferred_element_type=f32)).astype(bf16)
    output = output.reshape(seq_count, BLK, width)
    arrived = jnp.stack([to_owner(output[s], s) for s in range(seq_count)])
    output = jnp.stack(
        [lax.dynamic_index_in_dim(arrived, seq ^ s, 0, keepdims=False) for s in range(seq_count)],
        axis=1,
    )

    grad_down = jnp.einsum("rf,rd->fd", hidden, cotangent, preferred_element_type=f32)
    grad_down = reduce_rows(grad_down.astype(bf16), "fsdp", "ctx")
    d_hidden = jnp.einsum("rd,fd->rf", cotangent, down_weight, preferred_element_type=f32)
    _, gelu_pull = jax.vjp(gelu_product, gate_pre, up_pre)
    d_gate, d_up = gelu_pull(d_hidden)
    d_both = jnp.concatenate([d_gate.astype(bf16), d_up.astype(bf16)], axis=1)
    grad_gu = jnp.einsum("rd,rf->df", norm_two, d_both, preferred_element_type=f32)
    grad_gu = reduce_rows(grad_gu.astype(bf16), "fsdp", "ctx")
    d_norm_two = jnp.einsum("rf,df->rd", d_both, gate_up, preferred_element_type=f32)
    _, norm_pull_two = jax.vjp(rms_scale, resid, gain_two)
    d_resid_norm, grad_gain_two = norm_pull_two(d_norm_two)
    d_resid = cotangent.astype(f32) + d_resid_norm
    d_branch = d_resid.astype(bf16)
    grad_out = jnp.einsum("ra,rd->ad", attended_low, d_branch, preferred_element_type=f32)
    d_attended = jnp.einsum("rd,ad->ra", d_branch, out_weight, preferred_element_type=f32)
    d_attended = d_attended.astype(bf16)

    d_queries, d_keys, d_values, d_bias = attend_back(
        lead,
        low,
        high,
        queries,
        keys,
        values,
        d_attended,
        attended,
        log_total,
        docs,
        buckets,
        rel,
    )
    grad_qkv = jnp.concatenate(
        [
            jnp.einsum("rd,ra->da", norm_own, d_queries, preferred_element_type=f32),
            jnp.einsum("rd,ra->da", norm_one, d_keys, preferred_element_type=f32),
            jnp.einsum("rd,ra->da", norm_one, d_values, preferred_element_type=f32),
            grad_out,
        ],
        axis=1,
    )
    grad_qkv = reduce_rows(grad_qkv.astype(bf16), "fsdp", "ctx")
    d_norm_query = jnp.einsum("ra,da->rd", d_queries, query_weight, preferred_element_type=f32)
    d_norm_one = jnp.einsum(
        "ra,da->rd", d_keys, key_weight, preferred_element_type=f32
    ) + jnp.einsum("ra,da->rd", d_values, value_weight, preferred_element_type=f32)
    for s in range(seq_count):
        start = lead[s] * BLK
        old = lax.dynamic_slice_in_dim(d_norm_one, start, BLK, 0)
        d_norm_one = lax.dynamic_update_slice_in_dim(
            d_norm_one, old + d_norm_query[s * BLK : (s + 1) * BLK], start, 0
        )

    vocab_rows = -(-vocab // 16) * 16
    table_tall = jnp.pad(table, ((0, vocab_rows - vocab), (0, 0)))
    small = byte_backward(
        lead,
        phases,
        tokens,
        d_norm_one,
        d_resid.reshape(seq_count, BLK, width),
        conv,
        mix,
        table_tall,
        conv_w,
        score_w,
        gain_one,
        total_bytes,
    )
    bias_grad = jnp.transpose(d_bias[:, :2].reshape(heads, levels)).reshape(1, levels * heads)
    bias_grad = jnp.pad(bias_grad, ((0, 0), (0, width - levels * heads)))
    small = jnp.concatenate([small[: vocab_rows + 6], grad_gain_two[None], bias_grad], axis=0)
    small = jnp.pad(small, ((0, -small.shape[0] % 32), (0, 0))).astype(bf16)
    small = reduce_all(small, ("fsdp", "ctx")).astype(f32)
    top = vocab_rows
    return (
        output,
        small[:vocab],
        small[top : top + 4],
        small[top + 4],
        small[top + 5],
        small[top + 6],
        small[top + 7, : levels * heads].reshape(levels, heads),
        grad_qkv[:, :width].astype(f32),
        grad_qkv[:, width : 2 * width].astype(f32),
        grad_qkv[:, 2 * width : 3 * width].astype(f32),
        grad_qkv[:, 3 * width :].astype(f32),
        grad_gu[:, :hidden_width].astype(f32),
        grad_gu[:, hidden_width:].astype(f32),
        grad_down.astype(f32),
    )


def solution(mesh):
    placed = (
        P("fsdp", "ctx"),
        P("fsdp", "ctx"),
        P(),
        P(),
        P(),
        P(),
        P(),
        P(),
        P(),
        P("fsdp", None),
        P("fsdp", None),
        P("fsdp", None),
        P("fsdp", None),
        P("fsdp", None),
        P("fsdp", None),
        P("fsdp", None),
        P("ctx", "fsdp", None),
    )
    return jax.shard_map(
        local,
        mesh=mesh,
        in_specs=placed,
        out_specs=(
            P("ctx", "fsdp", None),
            P(),
            P(),
            P(),
            P(),
            P(),
            P(),
            P("fsdp", None),
            P("fsdp", None),
            P("fsdp", None),
            P("fsdp", None),
            P("fsdp", None),
            P("fsdp", None),
            P("fsdp", None),
        ),
        check_vma=False,
    )
```

time: 1460 us -> 574 us (0.39)
  local copies, waits for them, and re-layouts: 469 us -> 67.3 us
  waiting for transfers between devices: 436 us -> 138 us
  Pallas kernels: 0 us -> 161 us
  other arithmetic: 200 us -> 45.1 us
  matrix products: 198 us -> 66 us
  blocking collectives: 71.8 us -> 0 us
  starting transfers between devices: 52 us -> 86.3 us
    pallas_call x0 -> x4, Pallas kernels: none -> 161 us  [the longest x1 55 us: attend_back(): pl.pallas_call(attend_back_kernel, grid=(pairs,), out_shape=(jax.ShapeDty...]
    psum x2 -> x0, waiting for transfers between devices: 159 us -> none  [the longest x1 159 us: local(): lax.psum(grad_table_part.astype(jnp.bfloat16), 'ctx').astype(jnp.float32)]
    reshape x58 -> x10, local copies, waits for them, and re-layouts: 151 us -> 7.71 us  [the longest x2 3.04 us: phase_ids(): phases = jnp.transpose(padded.reshape(groups, 12))]
    another operation x54 -> x2, local copies, waits for them, and re-layouts: 132 us -> 0.15 us  [the longest x1 0.1 us: local(): small[top + 7, :levels * heads].reshape(levels, heads)]
    dot_general x86 -> x13, matrix products: 182 us -> 51.7 us  [the longest x1 8.07 us: local(): jnp.dot(norm_two, gate_up[:, :hidden_width], preferred_element_type=f32)]
    all_gather x9 -> x0, waiting for transfers between devices: 115 us -> none  [the longest x1 55 us: local(): value_piece = lax.all_gather(values3, 'ctx', axis=0, tiled=True)]
    convert_element_type x77 -> x25, other arithmetic: 88.4 us -> 14.1 us  [the longest x20 7.06 us: half_step(): return (keep.astype(f32) + other.astype(f32)).astype(bf16)]
    reduce_scatter x7 -> x0, waiting for transfers between devices: 71.3 us -> none  [the longest x1 40.4 us: local(): lax.psum_scatter(grad_down_full.astype(jnp.bfloat16), 'fsdp', scatter_dim...]
  transfers between devices with their start and end apart: 60 -> 52, of which waited for: 18 -> 25; matrix products, arithmetic and copies ran while one was open for 56% -> 21% of each run, Pallas kernels for 0% -> 19%
where the time goes in v1:
time: 574 us; the launch traced here: 566 us
  Pallas kernels  161 us (28%)
  waiting for transfers between devices  138 us (24%)
  starting transfers between devices  86.3 us (15%)
  local copies, waits for them, and re-layouts  67.3 us (12%)
  matrix products  66 us (11%)
  other arithmetic  45.1 us (8%)
    ppermute x46, waiting for transfers between devices, swap(): return lax.ppermute(value, axis, [(i, i ^ 1 << bit) for i in range(count)])  128 us
    ppermute x46, starting transfers between devices, swap(): return lax.ppermute(value, axis, [(i, i ^ 1 << bit) for i in range(count)])  61.7 us
    pallas_call x1, Pallas kernels, attend_back(): pl.pallas_call(attend_back_kernel, grid=(pairs,), out_shape=(jax.ShapeDty...  55 us
    pallas_call x1, Pallas kernels, attend(): pl.pallas_call(attend_kernel, grid=(pairs,), out_shape=(jax.ShapeDtypeStr...  44.1 us
    pallas_call x1, Pallas kernels, byte_backward(): pl.pallas_call(functools.partial(byte_backward_kernel, total_bytes), out_...  33 us
    pallas_call x1, Pallas kernels, byte_forward(): pl.pallas_call(functools.partial(byte_forward_kernel, total_bytes), out_s...  28.4 us
    ppermute x6, starting transfers between devices, to_owner(): return lax.ppermute(block, 'ctx', pairs)  24.6 us
    dynamic_update_slice x9, local copies, waits for them, and re-layouts, gather_rows(): lax.dynamic_update_slice_in_dim(result, part, (index ^ j) * rows, axis=0)  16.5 us
  transfers between devices with their start and end apart: 52, of which 25 were waited for; matrix products, arithmetic and copies ran while one was open for 21% of the time, Pallas kernels for 19%

profile of v1, /device:TPU:0, one launch (start us, length us, event | category | flops | bytes accessed | tf_op | source)
XLA Modules:
  0.0 565.7 jit_solution(17224041499959677880)
XLA Ops:
  68.2 28.4 %byte_forward.1 = (f32[1024,768]{1,0:T(8,128)}, bf16[1024,768]{1,0:T(8,128)(2,1)}, f32[12,176,768]{2,1,0:T(8,128)}, f32[4,176,128]{2,1,0:T(8,128)}) custom-call(s32[16,256]{1,0:T(8,128)} %pad.40.ids_ref, bf16[384,768]{1,0:T(8,128)(2,1)} %get-tuple-element.116.hi_ref, bf16[384,768]{1,0:T(8,128)(2,1)} %get-tuple-element.115.lo_ref, f32[4,768]{1,0:T(4,128)} %conv_w_ref.3, ...), custom_call_target="tpu_custom_call" | custom-call | tf_op jit(solution)/shard_map/byte_forward/pallas_call | solution.py:171
  113.9 10.5 %collective-permute-done.16 = bf16[128,768]{1,0:T(8,128)(2,1)S(1)} collective-permute-done((bf16[128,768]{1,0:T(8,128)(2,1)S(1)}, bf16[128,768]{1,0:T(8,128)(2,1)S(1)}, u32[]{:S(2)}, u32[]{:S(2)}) %collective-permute-start.16) | collective-permute-done | bytes 196640 | tf_op jit(solution)/shard_map/ppermute | solution.py:912
  124.4 5.9 %fusion.52 = f32[512,2048]{1,0:T(8,128)} fusion(bf16[2048,768]{1,0:T(8,128)(2,1)} %constant_dynamic-update-slice_fusion, bf16[128,768]{1,0:T(8,128)(2,1)S(1)} %collective-permute-done.17, bf16[128,768]{1,0:T(8,128)(2,1)S(1)} %collective-permute-done.16, bf16[128,768]{1,0:T(8,128)(2,1)S(1)} %collective-permute-done.15, bf16[128,768]{1,0:T(8,128)(2,1)S(1)} %bitcast.103), kind=kOutput, calls=%fused_computation.251 | convolution fusion | flops 1613758464 | bytes 8126464 | tf_op jit(solution)/shard_map/rd,fd->rf/dot_general | solution.py:962
  137.2 44.1 %attend.1 = (f32[512,768]{1,0:T(8,128)}, bf16[512,768]{1,0:T(8,128)(2,1)}, f32[6,4,256]{2,1,0:T(4,128)}) custom-call(s32[4]{0:T(128)} %get-tuple-element.89.lead_ref.first_ref, s32[4]{0:T(128)} %get-tuple-element.165.low_ref, s32[4]{0:T(128)} %get-tuple-element.164.high_ref, bf16[512,768]{1,0:T(8,128)(2,1)} %convolution_convert_fusion.9.q_ref, ...), custom_call_target="tpu_custom_call" | custom-call | tf_op jit(solution)/shard_map/attend/pallas_call | solution.py:544
  197.0 8.1 %fusion.8 = (bf16[512,2048]{1,0:T(8,128)(2,1)S(1)}, bf16[512,2048]{1,0:T(8,128)(2,1)S(1)}, bf16[512,2048]{1,0:T(8,128)(2,1)}) fusion(f32[512,2048]{1,0:T(8,128)S(1)} %copy-done.81, f32[512,2048]{1,0:T(8,128)S(1)} %fusion.9, bf16[512,768]{1,0:T(8,128)(2,1)S(1)} %multiply_convert_fusion.2, bf16[768,4864]{1,0:T(8,128)(2,1)} %constant_dynamic-update-slice_fusion.4), kind=kOutput, calls=%fused_computation.16 | convolution fusion | flops 1637875712 | bytes 18612224 | tf_op jit(solution)/shard_map/dot_general | solution.py:949
  205.1 8.0 %multiply_reduce_fusion = (bf16[768]{0:T(1024)(128)(2,1)S(1)}, f32[512]{0:T(512)S(1)}, f32[512,768]{1,0:T(8,128)S(1)}) fusion(f32[512,768]{1,0:T(8,128)S(1)} %get-tuple-element.162, f32[512]{0:T(512)S(1)} %fusion.47, f32[768]{0:T(1024)S(1)} %copy-done.69, bf16[768,4864]{1,0:T(8,128)(2,1)} %constant_dynamic-update-slice_fusion.4, ...), kind=kOutput, calls=%fused_computation.43 | convolution fusion | flops 3231972096 | bytes 13640192 | tf_op jit(solution)/shard_map/rf,df->rd/dot_general | solution.py:968
  217.7 55.0 %attend_back.1 = (bf16[512,768]{1,0:T(8,128)(2,1)}, bf16[1024,768]{1,0:T(8,128)(2,1)}, bf16[1024,768]{1,0:T(8,128)(2,1)}, f32[6,8,32]{2,1,0:T(8,128)}) custom-call(s32[4]{0:T(128)} %get-tuple-element.89.lead_ref.first_ref, s32[4]{0:T(128)} %get-tuple-element.165.low_ref, s32[4]{0:T(128)} %get-tuple-element.164.high_ref, ...), custom_call_target="tpu_custom_call" | custom-call | tf_op jit(solution)/shard_map/attend_back/pallas_call | solution.py:708
  279.8 5.7 convolution_convert_fusion
  290.2 19.5 %collective-permute-start.14 = (bf16[128,768]{1,0:T(8,128)(2,1)}, bf16[128,768]{1,0:T(8,128)(2,1)}, u32[]{:S(2)}, u32[]{:S(2)}) collective-permute-start(bf16[128,768]{1,0:T(8,128)(2,1)} %get-tuple-element.130), channel_id=1, source_target_pairs={{0,24},{4,28},{8,16},{12,20},{16,8},{20,12},{24,0},{28,4},{1,25},{... | collective-permute-start | bytes 589832 | tf_op jit(solution)/shard_map/ppermute | solution.py:912
  321.1 33.0 %byte_backward.1 = f32[280,768]{1,0:T(8,128)} custom-call(s32[4]{0:T(128)} %get-tuple-element.89.lead_ref.first_ref, s32[16,256]{1,0:T(8,128)} %pad.40.ids_ref, f32[1024,768]{1,0:T(8,128)} %get-tuple-element.26.tok_ref, f32[1024,768]{1,0:T(8,128)} %copy-done, f32[4,128,768]{2,1,0:T(8,128)} %bitcast.92, f32[12,176,768]{2,1,0:T(8,128)} %get-tuple-element.34.conv_ref, ...), custom_call_target="tpu_custom_call" | custom-call | tf_op jit(solution)/shard_map/byte_backward/pallas_call | solution.py:384
  355.4 7.6 %collective-permute-start.18 = (bf16[144,768]{1,0:T(8,128)(2,1)S(1)}, bf16[144,768]{1,0:T(8,128)(2,1)S(1)}, u32[]{:S(2)}, u32[]{:S(2)}) collective-permute-start(bf16[144,768]{1,0:T(8,128)(2,1)S(1)} %pad_dynamic-slice_fusion), channel_id=1, source_target_pairs={{0,1},{1,0},{2,3},{3,2},{4,5},{5,4},{6,7},{7,6},{8,9},{9,8},{10,11... | collective-permute-start | bytes 663560 | tf_op jit(solution)/shard_map/ppermute | solution.py:769
  368.7 4.9 collective-permute-start.19
  405.8 11.7 %collective-permute-done.45 = bf16[1,1,512,768]{3,2,1,0:T(8,128)(2,1)S(1)} collective-permute-done((bf16[1,1,512,768]{3,2,1,0:T(8,128)(2,1)S(1)}, bf16[1,1,512,768]{3,2,1,0:T(8,128)(2,1)S(1)}, u32[]{:S(2)}, u32[]{:S(2)}) %collective-permute-start.45) | collective-permute-done | bytes 786464 | tf_op jit(solution)/shard_map/ppermute | solution.py:769
  419.6 6.0 %collective-permute-done.46 = bf16[256,768]{1,0:T(8,128)(2,1)S(1)} collective-permute-done((bf16[256,768]{1,0:T(8,128)(2,1)S(1)}, bf16[256,768]{1,0:T(8,128)(2,1)S(1)}, u32[]{:S(2)}, u32[]{:S(2)}) %collective-permute-start.46) | collective-permute-done | bytes 393248 | tf_op jit(solution)/shard_map/ppermute | solution.py:769
  426.3 6.2 %collective-permute-done.47 = bf16[128,768]{1,0:T(8,128)(2,1)S(1)} collective-permute-done((bf16[128,768]{1,0:T(8,128)(2,1)S(1)}, bf16[128,768]{1,0:T(8,128)(2,1)S(1)}, u32[]{:S(2)}, u32[]{:S(2)}) %collective-permute-start.47) | collective-permute-done | bytes 196640 | tf_op jit(solution)/shard_map/ppermute | solution.py:769
  433.9 5.0 collective-permute-done.48
  452.6 15.4 %collective-permute-done.29 = bf16[1,1,192,3072]{3,2,1,0:T(8,128)(2,1)S(1)} collective-permute-done((bf16[1,1,192,3072]{3,2,1,0:T(8,128)(2,1)S(1)}, bf16[1,1,192,3072]{3,2,1,0:T(8,128)(2,1)S(1)}, u32[]{:S(2)}, u32[]{:S(2)}) %collective-permute-start.29) | collective-permute-done | bytes 1179680 | tf_op jit(solution)/shard_map/ppermute | solution.py:769
  482.8 10.2 %collective-permute-done.37 = bf16[1,1,192,4096]{3,2,1,0:T(8,128)(2,1)} collective-permute-done((bf16[1,1,192,4096]{3,2,1,0:T(8,128)(2,1)}, bf16[1,1,192,4096]{3,2,1,0:T(8,128)(2,1)}, u32[]{:S(2)}, u32[]{:S(2)}) %collective-permute-start.37) | collective-permute-done | bytes 1572896 | tf_op jit(solution)/shard_map/ppermute | solution.py:769
  499.2 7.8 %collective-permute-done.38 = bf16[96,4096]{1,0:T(8,128)(2,1)S(1)} collective-permute-done((bf16[96,4096]{1,0:T(8,128)(2,1)S(1)}, bf16[96,4096]{1,0:T(8,128)(2,1)S(1)}, u32[]{:S(2)}, u32[]{:S(2)}) %collective-permute-start.38) | collective-permute-done | bytes 786464 | tf_op jit(solution)/shard_map/ppermute | solution.py:769
  511.6 7.2 %collective-permute-done.39 = bf16[48,4096]{1,0:T(8,128)(2,1)S(1)} collective-permute-done((bf16[48,4096]{1,0:T(8,128)(2,1)S(1)}, bf16[48,4096]{1,0:T(8,128)(2,1)S(1)}, u32[]{:S(2)}, u32[]{:S(2)}) %collective-permute-start.39) | collective-permute-done | bytes 393248 | tf_op jit(solution)/shard_map/ppermute | solution.py:769
  520.7 7.9 %collective-permute-done.40 = bf16[24,4096]{1,0:T(8,128)(2,1)S(1)} collective-permute-done((bf16[24,4096]{1,0:T(8,128)(2,1)S(1)}, bf16[24,4096]{1,0:T(8,128)(2,1)S(1)}, u32[]{:S(2)}, u32[]{:S(2)}) %collective-permute-start.40) | collective-permute-done | bytes 196640 | tf_op jit(solution)/shard_map/ppermute | solution.py:769
  531.6 5.8 %collective-permute-done.41 = bf16[24,4096]{1,0:T(8,128)(2,1)S(1)} collective-permute-done((bf16[24,4096]{1,0:T(8,128)(2,1)S(1)}, bf16[24,4096]{1,0:T(8,128)(2,1)S(1)}, u32[]{:S(2)}, u32[]{:S(2)}) %collective-permute-start.41) | collective-permute-done | bytes 196640 | tf_op jit(solution)/shard_map/ppermute | solution.py:769
  547.5 7.0 %collective-permute-done.35 = bf16[96,3072]{1,0:T(8,128)(2,1)S(1)} collective-permute-done((bf16[96,3072]{1,0:T(8,128)(2,1)S(1)}, bf16[96,3072]{1,0:T(8,128)(2,1)S(1)}, u32[]{:S(2)}, u32[]{:S(2)}) %collective-permute-start.35) | collective-permute-done | bytes 589856 | tf_op jit(solution)/shard_map/ppermute | solution.py:769
  556.2 6.8 %collective-permute-done.43 = bf16[96,4096]{1,0:T(8,128)(2,1)S(1)} collective-permute-done((bf16[96,4096]{1,0:T(8,128)(2,1)S(1)}, bf16[96,4096]{1,0:T(8,128)(2,1)S(1)}, u32[]{:S(2)}, u32[]{:S(2)}) %collective-permute-start.43) | collective-permute-done | bytes 786464 | tf_op jit(solution)/shard_map/ppermute | solution.py:769
  (432 shorter events, 235.8 us)
Async XLA Ops:
  8.1 98.7 %collective-permute-start.3 = (bf16[192,2304]{1,0:T(8,128)(2,1)}, bf16[192,2304]{1,0:T(8,128)(2,1)}, u32[]{:S(2)}, u32[]{:S(2)}) collective-permute-start(bf16[192,2304]{1,0:T(8,128)(2,1)} %get-tuple-element.113), channel_id=1, source_target_pairs={{0,2},{1,3},{2,0},{3,1},{4,6},{5,7},{6,4},{7,5},{8,10},{9,11},{10,... | collective-permute-start | bytes 2654216 | tf_op jit(solution)/shard_map/ppermute | solution.py:769
  11.1 98.7 %collective-permute-start.4 = (bf16[192,2304]{1,0:T(8,128)(2,1)}, bf16[192,2304]{1,0:T(8,128)(2,1)}, u32[]{:S(2)}, u32[]{:S(2)}) collective-permute-start(bf16[192,2304]{1,0:T(8,128)(2,1)} %get-tuple-element.113), channel_id=1, source_target_pairs={{0,1},{1,0},{2,3},{3,2},{4,5},{5,4},{6,7},{7,6},{8,9},{9,8},{10,11... | collective-permute-start | bytes 2654216 | tf_op jit(solution)/shard_map/ppermute | solution.py:769
  14.4 83.6 %collective-permute-start.9 = (bf16[512,768]{1,0:T(8,128)(2,1)}, bf16[512,768]{1,0:T(8,128)(2,1)}, u32[]{:S(2)}, u32[]{:S(2)}) collective-permute-start(bf16[512,768]{1,0:T(8,128)(2,1)} %get-tuple-element.87), channel_id=1, source_target_pairs={{0,2},{1,3},{2,0},{3,1},{4,6},{5,7},{6,4},{7,5},{8,10},{9,11},{10,... | collective-permute-start | bytes 2359304 | tf_op jit(solution)/shard_map/ppermute | solution.py:769
  14.4 89.0 %collective-permute-start.10 = (bf16[512,768]{1,0:T(8,128)(2,1)}, bf16[512,768]{1,0:T(8,128)(2,1)}, u32[]{:S(2)}, u32[]{:S(2)}) collective-permute-start(bf16[512,768]{1,0:T(8,128)(2,1)} %get-tuple-element.87), channel_id=1, source_target_pairs={{0,1},{1,0},{2,3},{3,2},{4,5},{5,4},{6,7},{7,6},{8,9},{9,8},{10,11... | collective-permute-start | bytes 2359304 | tf_op jit(solution)/shard_map/ppermute | solution.py:769
  15.5 17.3 %collective-permute-start = (s32[1,4,2,256]{3,1,2,0:T(4,128)}, s32[1,4,2,256]{3,1,2,0:T(4,128)}, u32[]{:S(2)}, u32[]{:S(2)}) collective-permute-start(s32[1,4,2,256]{3,1,2,0:T(4,128)} %add_bitcast_fusion), channel_id=1, source_target_pairs={{0,4},{4,0},{8,12},{12,8},{16,20},{20,16},{24,28},{28,24},{1,5},{5... | collective-permute-start | bytes 24584 | tf_op jit(solution)/shard_map/ppermute | solution.py:769
  53.8 79.1 %collective-permute-start.6 = (bf16[192,4864]{1,0:T(8,128)(2,1)}, bf16[192,4864]{1,0:T(8,128)(2,1)}, u32[]{:S(2)}, u32[]{:S(2)}) collective-permute-start(bf16[192,4864]{1,0:T(8,128)(2,1)} %get-tuple-element.97), channel_id=1, source_target_pairs={{0,2},{1,3},{2,0},{3,1},{4,6},{5,7},{6,4},{7,5},{8,10},{9,11},{10,... | collective-permute-start | bytes 5603336 | tf_op jit(solution)/shard_map/ppermute | solution.py:769
  106.8 17.5 %collective-permute-start.16 = (bf16[128,768]{1,0:T(8,128)(2,1)S(1)}, bf16[128,768]{1,0:T(8,128)(2,1)S(1)}, u32[]{:S(2)}, u32[]{:S(2)}) collective-permute-start(bf16[128,768]{1,0:T(8,128)(2,1)S(1)} %bitcast.107), channel_id=1, source_target_pairs={{0,16},{4,20},{8,24},{12,28},{16,0},{20,4},{24,8},{28,12},{1,17},{... | collective-permute-start | bytes 589832 | tf_op jit(solution)/shard_map/ppermute | solution.py:912
  111.2 19.1 %collective-permute-start.5 = (bf16[192,2304]{1,0:T(8,128)(2,1)}, bf16[192,2304]{1,0:T(8,128)(2,1)S(1)}, u32[]{:S(2)}, u32[]{:S(2)}) collective-permute-start(bf16[192,2304]{1,0:T(8,128)(2,1)} %collective-permute-done.3), channel_id=1, source_target_pairs={{0,1},{1,0},{2,3},{3,2},{4,5},{5,4},{6,7},{7,6},{8,9},{9,8},{10,11... | collective-permute-start | bytes 2654216 | tf_op jit(solution)/shard_map/ppermute | solution.py:769
  113.4 70.8 %collective-permute-start.7 = (bf16[192,4864]{1,0:T(8,128)(2,1)}, bf16[192,4864]{1,0:T(8,128)(2,1)}, u32[]{:S(2)}, u32[]{:S(2)}) collective-permute-start(bf16[192,4864]{1,0:T(8,128)(2,1)} %get-tuple-element.97), channel_id=1, source_target_pairs={{0,1},{1,0},{2,3},{3,2},{4,5},{5,4},{6,7},{7,6},{8,9},{9,8},{10,11... | collective-permute-start | bytes 5603336 | tf_op jit(solution)/shard_map/ppermute | solution.py:769
  132.9 54.1 %collective-permute-start.8 = (bf16[192,4864]{1,0:T(8,128)(2,1)}, bf16[192,4864]{1,0:T(8,128)(2,1)}, u32[]{:S(2)}, u32[]{:S(2)}) collective-permute-start(bf16[192,4864]{1,0:T(8,128)(2,1)} %collective-permute-done.6), channel_id=1, source_target_pairs={{0,1},{1,0},{2,3},{3,2},{4,5},{5,4},{6,7},{7,6},{8,9},{9,8},{10,11... | collective-permute-start | bytes 5603336 | tf_op jit(solution)/shard_map/ppermute | solution.py:769
  290.2 100.0 %collective-permute-start.14 = (bf16[128,768]{1,0:T(8,128)(2,1)}, bf16[128,768]{1,0:T(8,128)(2,1)}, u32[]{:S(2)}, u32[]{:S(2)}) collective-permute-start(bf16[128,768]{1,0:T(8,128)(2,1)} %get-tuple-element.130), channel_id=1, source_target_pairs={{0,24},{4,28},{8,16},{12,20},{16,8},{20,12},{24,0},{28,4},{1,25},{... | collective-permute-start | bytes 589832 | tf_op jit(solution)/shard_map/ppermute | solution.py:912
  309.7 81.1 %collective-permute-start.13 = (bf16[128,768]{1,0:T(8,128)(2,1)}, bf16[128,768]{1,0:T(8,128)(2,1)}, u32[]{:S(2)}, u32[]{:S(2)}) collective-permute-start(bf16[128,768]{1,0:T(8,128)(2,1)} %get-tuple-element.131), channel_id=1, source_target_pairs={{0,16},{4,20},{8,24},{12,28},{16,0},{20,4},{24,8},{28,12},{1,17},{... | collective-permute-start | bytes 589832 | tf_op jit(solution)/shard_map/ppermute | solution.py:912
  309.7 82.6 %collective-permute-start.12 = (bf16[128,768]{1,0:T(8,128)(2,1)}, bf16[128,768]{1,0:T(8,128)(2,1)}, u32[]{:S(2)}, u32[]{:S(2)}) collective-permute-start(bf16[128,768]{1,0:T(8,128)(2,1)} %get-tuple-element.132), channel_id=1, source_target_pairs={{0,8},{4,12},{8,0},{12,4},{16,24},{20,28},{24,16},{28,20},{1,9},{5... | collective-permute-start | bytes 589832 | tf_op jit(solution)/shard_map/ppermute | solution.py:912
  377.1 20.5 %collective-permute-start.44 = (bf16[2,1,512,768]{3,2,1,0:T(8,128)(2,1)S(1)}, bf16[2,1,512,768]{3,2,1,0:T(8,128)(2,1)S(1)}, u32[]{:S(2)}, u32[]{:S(2)}) collective-permute-start(bf16[2,1,512,768]{3,2,1,0:T(8,128)(2,1)S(1)} %constant_dynamic-slice_fusion.3), channel_id=1, source_target_pairs={{0,1},{1,0},{2,3},{3,2},{4,5},{5,4},{6,7},{7,6},{8,9},{9,8},{10,11... | collective-permute-start | bytes 4718600 | tf_op jit(solution)/shard_map/ppermute | solution.py:769
  390.1 42.8 %collective-permute-start.28 = (bf16[2,1,192,3072]{3,2,1,0:T(8,128)(2,1)S(1)}, bf16[2,1,192,3072]{3,2,1,0:T(8,128)(2,1)S(1)}, u32[]{:S(2)}, u32[]{:S(2)}) collective-permute-start(bf16[2,1,192,3072]{3,2,1,0:T(8,128)(2,1)S(1)} %constant_dynamic-slice_fusion.11), channel_id=1, source_target_pairs={{0,1},{1,0},{2,3},{3,2},{4,5},{5,4},{6,7},{7,6},{8,9},{9,8},{10,11... | collective-permute-start | bytes 7077896 | tf_op jit(solution)/shard_map/ppermute | solution.py:769
  390.2 54.4 %collective-permute-start.36 = (bf16[2,1,192,4096]{3,2,1,0:T(8,128)(2,1)S(1)}, bf16[2,1,192,4096]{3,2,1,0:T(8,128)(2,1)S(1)}, u32[]{:S(2)}, u32[]{:S(2)}) collective-permute-start(bf16[2,1,192,4096]{3,2,1,0:T(8,128)(2,1)S(1)} %constant_dynamic-slice_fusion.7), channel_id=1, source_target_pairs={{0,1},{1,0},{2,3},{3,2},{4,5},{5,4},{6,7},{7,6},{8,9},{9,8},{10,11... | collective-permute-start | bytes 9437192 | tf_op jit(solution)/shard_map/ppermute | solution.py:769
  398.1 19.4 %collective-permute-start.45 = (bf16[1,1,512,768]{3,2,1,0:T(8,128)(2,1)S(1)}, bf16[1,1,512,768]{3,2,1,0:T(8,128)(2,1)S(1)}, u32[]{:S(2)}, u32[]{:S(2)}) collective-permute-start(bf16[1,1,512,768]{3,2,1,0:T(8,128)(2,1)S(1)} %constant_dynamic-slice_fusion.2), channel_id=1, source_target_pairs={{0,2},{1,3},{2,0},{3,1},{4,6},{5,7},{6,4},{7,5},{8,10},{9,11},{10,... | collective-permute-start | bytes 2359304 | tf_op jit(solution)/shard_map/ppermute | solution.py:769
  404.1 15.3 %collective-permute-start.26 = (bf16[72,768]{1,0:T(8,128)(2,1)S(1)}, bf16[72,768]{1,0:T(8,128)(2,1)S(1)}, u32[]{:S(2)}, u32[]{:S(2)}) collective-permute-start(bf16[72,768]{1,0:T(8,128)(2,1)S(1)} %pad_maximum_fusion.21), channel_id=1, source_target_pairs={{0,2},{1,3},{2,0},{3,1},{4,6},{5,7},{6,4},{7,5},{8,10},{9,11},{10,... | collective-permute-start | bytes 331784 | tf_op jit(solution)/shard_map/ppermute | solution.py:769
  439.0 29.0 %collective-permute-start.29 = (bf16[1,1,192,3072]{3,2,1,0:T(8,128)(2,1)S(1)}, bf16[1,1,192,3072]{3,2,1,0:T(8,128)(2,1)S(1)}, u32[]{:S(2)}, u32[]{:S(2)}) collective-permute-start(bf16[1,1,192,3072]{3,2,1,0:T(8,128)(2,1)S(1)} %constant_dynamic-slice_fusion.10), channel_id=1, source_target_pairs={{0,2},{1,3},{2,0},{3,1},{4,6},{5,7},{6,4},{7,5},{8,10},{9,11},{10,... | collective-permute-start | bytes 3538952 | tf_op jit(solution)/shard_map/ppermute | solution.py:769
  447.1 45.9 %collective-permute-start.37 = (bf16[1,1,192,4096]{3,2,1,0:T(8,128)(2,1)}, bf16[1,1,192,4096]{3,2,1,0:T(8,128)(2,1)}, u32[]{:S(2)}, u32[]{:S(2)}) collective-permute-start(bf16[1,1,192,4096]{3,2,1,0:T(8,128)(2,1)} %constant_dynamic-slice_fusion.6), channel_id=1, source_target_pairs={{0,2},{1,3},{2,0},{3,1},{4,6},{5,7},{6,4},{7,5},{8,10},{9,11},{10,... | collective-permute-start | bytes 4718600 | tf_op jit(solution)/shard_map/ppermute | solution.py:769
  451.2 24.0 %collective-permute-start.51 = (bf16[256,768]{1,0:T(8,128)(2,1)}, bf16[256,768]{1,0:T(8,128)(2,1)}, u32[]{:S(2)}, u32[]{:S(2)}) collective-permute-start(bf16[256,768]{1,0:T(8,128)(2,1)} %pad_maximum_fusion.14), channel_id=1, source_target_pairs={{0,4},{4,0},{8,12},{12,8},{16,20},{20,16},{24,28},{28,24},{1,5},{5... | collective-permute-start | bytes 1179656 | tf_op jit(solution)/shard_map/ppermute | solution.py:769
  480.8 15.6 %collective-permute-start.31 = (bf16[48,3072]{1,0:T(8,128)(2,1)S(1)}, bf16[48,3072]{1,0:T(8,128)(2,1)S(1)}, u32[]{:S(2)}, u32[]{:S(2)}) collective-permute-start(bf16[48,3072]{1,0:T(8,128)(2,1)S(1)} %constant_dynamic-slice_fusion.9), channel_id=1, source_target_pairs={{0,8},{4,12},{8,0},{12,4},{16,24},{20,28},{24,16},{28,20},{1,9},{5... | collective-permute-start | bytes 884744 | tf_op jit(solution)/shard_map/ppermute | solution.py:769
  538.6 16.0 %collective-permute-start.35 = (bf16[96,3072]{1,0:T(8,128)(2,1)S(1)}, bf16[96,3072]{1,0:T(8,128)(2,1)S(1)}, u32[]{:S(2)}, u32[]{:S(2)}) collective-permute-start(bf16[96,3072]{1,0:T(8,128)(2,1)S(1)} %pad_maximum_fusion.12), channel_id=1, source_target_pairs={{0,4},{4,0},{8,12},{12,8},{16,20},{20,16},{24,28},{28,24},{1,5},{5... | collective-permute-start | bytes 1769480 | tf_op jit(solution)/shard_map/ppermute | solution.py:769
  545.5 17.4 %collective-permute-start.43 = (bf16[96,4096]{1,0:T(8,128)(2,1)S(1)}, bf16[96,4096]{1,0:T(8,128)(2,1)S(1)}, u32[]{:S(2)}, u32[]{:S(2)}) collective-permute-start(bf16[96,4096]{1,0:T(8,128)(2,1)S(1)} %pad_maximum_fusion.11), channel_id=1, source_target_pairs={{0,4},{4,0},{8,12},{12,8},{16,20},{20,16},{24,28},{28,24},{1,5},{5... | collective-permute-start | bytes 2359304 | tf_op jit(solution)/shard_map/ppermute | solution.py:769
  (114 other events, 1090.7 us)

commit v2 on v1

--- a/solution.py
+++ b/solution.py
@@ -47,8 +47,7 @@
 def byte_forward_kernel(
     total_bytes,
     ids_ref,
-    hi_ref,
-    lo_ref,
+    table_ref,
     conv_w_ref,
     score_ref,
     gain_ref,
@@ -56,6 +55,8 @@
     norm_ref,
     conv_ref,
     mix_ref,
+    hi_ref,
+    lo_ref,
     emb,
     flat,
 ):
@@ -64,6 +65,9 @@
     tiles = width // LANE
     token_count = norm_ref.shape[0]
     vocab_pad = hi_ref.shape[0]
+    high = table_ref[...].astype(bf16)
+    hi_ref[...] = high
+    lo_ref[...] = (table_ref[...] - high.astype(f32)).astype(bf16)
     ids_cols = jnp.transpose(ids_ref[...].astype(f32))
     vocab = lax.broadcasted_iota(jnp.int32, (groups, vocab_pad), 1).astype(f32)
     for r in range(15):
@@ -164,7 +168,7 @@
     return jnp.pad(both, ((0, 1), (0, lanes - groups)), constant_values=-1)
 
 
-def byte_forward(ids, hi, lo, conv_w, score_w, gain_one, total_bytes):
+def byte_forward(ids, table, conv_w, score_w, gain_one, total_bytes):
     width = conv_w.shape[1]
     token_count = total_bytes // 2
     groups = -(-(-(-total_bytes // 12)) // 16) * 16
@@ -177,12 +181,15 @@
             jax.ShapeDtypeStruct((4, groups, LANE), f32),
         ),
         scratch_shapes=[
+            pltpu.VMEM(table.shape, bf16),
+            pltpu.VMEM(table.shape, bf16),
             pltpu.VMEM((15, groups, width), f32),
             pltpu.VMEM((width // LANE, 6 * groups, LANE), f32),
         ],
         compiler_params=pltpu.CompilerParams(vmem_limit_bytes=VMEM_CAP),
+        cost_estimate=pl.CostEstimate(flops=20_000_000_000, transcendentals=0, bytes_accessed=1 << 24),
         name="byte_forward",
-    )(ids, hi, lo, conv_w, score_w.reshape(1, width), gain_one.reshape(1, width))
+    )(ids, table, conv_w, score_w.reshape(1, width), gain_one.reshape(1, width))
 
 
 def byte_backward_kernel(
@@ -368,19 +375,30 @@
             out_ref[0:vocab_rows, :] = part * conv_w_ref[k : k + 1, :]
         else:
             out_ref[0:vocab_rows, :] = out_ref[0:vocab_rows, :] + part * conv_w_ref[k : k + 1, :]
-        tail[k] = jnp.sum(part * table_ref[...], axis=0, keepdims=True)
+        tail[k] = jnp.sum(part * table_ref[0:vocab_rows, :], axis=0, keepdims=True)
     tail[4] = jnp.sum(jnp.concatenate(accs, axis=1), axis=0, keepdims=True)
     tail[5] = jnp.sum(gain_acc, axis=0, keepdims=True)
     out_ref[vocab_rows:, :] = jnp.concatenate(tail, axis=0)
 
 
 def byte_backward(
-    first, ids, tokens, d_norm, d_resid, conv, mix, table, conv_w, score_w, gain_one, total_bytes
+    first,
+    ids,
+    tokens,
+    d_norm,
+    d_resid,
+    conv,
+    mix,
+    table,
+    vocab_rows,
+    conv_w,
+    score_w,
+    gain_one,
+    total_bytes,
 ):
     width = conv.shape[2]
     groups = conv.shape[1]
     lanes = ids.shape[1]
-    vocab_rows = table.shape[0]
     return pl.pallas_call(
         functools.partial(byte_backward_kernel, total_bytes),
         out_shape=jax.ShapeDtypeStruct((vocab_rows + 8, width), f32),
@@ -392,6 +410,7 @@
             pltpu.VMEM((vocab_rows, 15 * lanes), bf16),
         ],
         compiler_params=pltpu.CompilerParams(vmem_limit_bytes=VMEM_CAP),
+        cost_estimate=pl.CostEstimate(flops=20_000_000_000, transcendentals=0, bytes_accessed=1 << 24),
         name="byte_backward",
     )(
         first,
@@ -573,6 +592,7 @@
             pltpu.VMEM((blocks, BLK, 2 * BLK), f32),
         ],
         compiler_params=pltpu.CompilerParams(vmem_limit_bytes=VMEM_CAP),
+        cost_estimate=pl.CostEstimate(flops=25_000_000_000, transcendentals=0, bytes_accessed=1 << 23),
         name="attend",
     )(lead, low, high, q, k, v, docs, buckets, rel)
 
@@ -739,6 +759,7 @@
             pltpu.VMEM((2 * reach + 1, BLK, 2 * BLK), f32),
         ],
         compiler_params=pltpu.CompilerParams(vmem_limit_bytes=VMEM_CAP),
+        cost_estimate=pl.CostEstimate(flops=35_000_000_000, transcendentals=0, bytes_accessed=1 << 23),
         name="attend_back",
     )(lead, low, high, q, k, v, g, out, log, docs, buckets, rel)
 
@@ -747,14 +768,14 @@
     blocks = docs.shape[0]
     starts = docs[:, 0]
     ends = docs[:, -1]
-    own_start = jnp.take(starts, lead)
-    own_end = jnp.take(ends, lead)
+    mine = (lead[:, None] == jnp.arange(blocks)[None, :]).astype(jnp.int32)
+    own_start = jnp.sum(mine * starts[None, :], axis=1)
+    own_end = jnp.sum(mine * ends[None, :], axis=1)
     low = jnp.sum((ends[None, :] < own_start[:, None]).astype(jnp.int32), axis=1)
     high = jnp.sum((starts[None, :] <= own_end[:, None]).astype(jnp.int32), axis=1)
     buckets = jnp.pad(jnp.flip(rel_bucket), (0, 1)).reshape(2 * blocks, BLK)
     levels, heads = rel_bias.shape
     rel = jnp.transpose(rel_bias).reshape(heads // 2, 2, levels)
-    rel = jnp.pad(rel, ((0, 0), (0, 6), (0, 0)))
     return low, high, buckets, rel
 
 
@@ -797,14 +818,29 @@
     return result
 
 
-def half_step(value, axis, bit, dim):
+def add_low(left, right):
+    return (left.astype(f32) + right.astype(f32)).astype(bf16)
+
+
+def piece(value, index, dim=0):
+    return lax.dynamic_index_in_dim(value, index, dim, keepdims=False)
+
+
+def scatter_step(value, axis, bit, dim):
+    own = (lax.axis_index(axis) >> bit) & 1
+    other = swap(piece(value, 1 - own, dim), axis, bit)
+    return add_low(piece(value, own, dim), other)
+
+
+def rest_sum(value, axis):
+    count = lax.axis_size(axis)
     index = lax.axis_index(axis)
-    own = (index >> bit) & 1
-    size = value.shape[dim] // 2
-    keep = lax.dynamic_slice_in_dim(value, own * size, size, dim)
-    send = lax.dynamic_slice_in_dim(value, (1 - own) * size, size, dim)
-    other = swap(send.astype(bf16), axis, bit)
-    return (keep.astype(f32) + other.astype(f32)).astype(bf16)
+    mine = index // 2
+    total = piece(value, mine).astype(f32)
+    for j in range(1, count // 2):
+        pairs = [(i, ((i // 2) ^ j) * 2 + i % 2) for i in range(count)]
+        total = total + lax.ppermute(piece(value, mine ^ j), axis, pairs).astype(f32)
+    return total.astype(bf16)
 
 
 def reduce_rows(value, scatter_axis, sum_axis):
@@ -812,34 +848,64 @@
     bits = bits_of(count)
     rows = value.shape[0] // count
     value = value.reshape((2,) * bits + (rows,) + value.shape[1:])
+    value = yield value
     for bit in range(bits):
-        value = half_step(value, scatter_axis, bit, bits - 1 - bit)
-    value = value.reshape((rows,) + value.shape[bits + 1 :])
-    steps = bits_of(lax.axis_size(sum_axis))
-    done = 0
-    while done < steps and value.shape[0] % 2 == 0:
-        value = half_step(value, sum_axis, done, 0)
-        done += 1
-    for bit in range(done, steps):
-        value = (value.astype(f32) + swap(value, sum_axis, bit).astype(f32)).astype(bf16)
-    index = lax.axis_index(sum_axis)
-    for bit in reversed(range(done)):
-        value = ordered(value, swap(value, sum_axis, bit), index, bit)
-    return value
-
-
-def reduce_all(value, axes):
-    stages = [(axis, bit) for axis in axes for bit in range(bits_of(lax.axis_size(axis)))]
-    halved = []
-    for axis, bit in stages:
-        if value.shape[0] % 2 == 0:
-            value = half_step(value, axis, bit, 0)
-            halved.append((axis, bit))
-        else:
-            value = (value.astype(f32) + swap(value, axis, bit).astype(f32)).astype(bf16)
-    for axis, bit in reversed(halved):
-        value = ordered(value, swap(value, axis, bit), lax.axis_index(axis), bit)
-    return value
+        value = yield scatter_step(value, scatter_axis, bit, bits - 1 - bit)
+    count = lax.axis_size(sum_axis)
+    value = value.reshape((count // 2, 2, rows // count) + value.shape[1:])
+    value = yield scatter_step(value, sum_axis, 0, 1)
+    value = yield rest_sum(value, sum_axis)
+    yield lax.all_gather(value, sum_axis, axis=0, tiled=True)
+
+
+class Chain:
+    def __init__(self, value):
+        self.steps = reduce_rows(value, "fsdp", "ctx")
+        self.value = next(self.steps)
+
+    def advance(self, value):
+        self.value = self.steps.send(value)
+
+    def finish(self):
+        for value in self.steps_left():
+            self.value = value
+        return self.value.astype(f32)
+
+    def steps_left(self):
+        while True:
+            try:
+                yield self.steps.send(self.value)
+            except StopIteration:
+                return
+
+
+def gate(anchor, *chains):
+    joined = lax.optimization_barrier((anchor,) + tuple(chain.value for chain in chains))
+    for chain, value in zip(chains, joined[1:]):
+        chain.advance(value)
+    return joined[0]
+
+
+def reduce_small(value):
+    fsdp_bits = bits_of(lax.axis_size("fsdp"))
+    count = lax.axis_size("ctx")
+    rows, width = value.shape
+    value = value.reshape(2, count // 2, 2 * rows // (2 * count), width)
+    value = scatter_step(value, "fsdp", 0, 0)
+    value = rest_sum(value, "ctx")
+    value = add_low(value, swap(value, "ctx", 0))
+    for bit in range(1, fsdp_bits):
+        value = add_low(value, swap(value, "fsdp", bit))
+    mine = lax.axis_index("ctx") // 2
+    parts = [(0, value)]
+    for j in range(1, count // 2):
+        pairs = [(i, ((i // 2) ^ j) * 2 + i % 2) for i in range(count)]
+        parts.append((j, lax.ppermute(value, "ctx", pairs)))
+    whole = jnp.zeros((count // 2,) + value.shape, value.dtype)
+    for j, part in parts:
+        whole = lax.dynamic_update_index_in_dim(whole, part, mine ^ j, 0)
+    whole = whole.reshape((rows // 2, width))
+    return ordered(whole, swap(whole, "fsdp", 0), lax.axis_index("fsdp"), 0)
 
 
 def rms_scale(values, gain_vec):
@@ -885,16 +951,19 @@
     lead = jnp.stack([share * other + part for other in near]).astype(jnp.int32)
     rows = seq_count * BLK
 
+    qkv_low = jnp.concatenate([query_master, key_master, value_master], axis=1).astype(bf16)
     both = jnp.stack([byte_ids, doc_ids], axis=1)
+    both, qkv_low = lax.optimization_barrier((both, qkv_low))
+    qkv = gather_rows(qkv_low, "fsdp")
     both = gather_small(both, "ctx")
-    both = lax.dynamic_index_in_dim(both, seq, 1, keepdims=False)
+    both, out_master, gate_master, up_master, down_master = lax.optimization_barrier(
+        (both, out_master, gate_master, up_master, down_master)
+    )
+    both = piece(both, seq, 1)
     ids = both[:, 0].reshape(total_bytes)
     docs = both[:, 1, ::2]
-
-    qkv_low = jnp.concatenate([query_master, key_master, value_master], axis=1).astype(bf16)
     ogu_low = jnp.concatenate([out_master, gate_master, up_master], axis=1).astype(bf16)
     down_low = down_master.astype(bf16)
-    qkv = gather_rows(qkv_low, "fsdp")
     ogu = gather_rows(ogu_low, "fsdp")
     down_weight = gather_rows(down_low, "fsdp")
     query_weight = qkv[:, :width]
@@ -921,10 +990,8 @@
 
     phases = phase_ids(ids, total_bytes)
     table_wide = jnp.pad(table, ((0, -vocab % LANE), (0, 0)))
-    table_hi = lax.reduce_precision(table_wide, 8, 7)
-    table_lo = (table_wide - table_hi).astype(bf16)
     tokens, norm_one, conv, mix = byte_forward(
-        phases, table_hi.astype(bf16), table_lo, conv_w, score_w, gain_one, total_bytes
+        phases, table_wide, conv_w, score_w, gain_one, total_bytes
     )
 
     def own_rows(array):
@@ -958,21 +1025,23 @@
     )
 
     grad_down = jnp.einsum("rf,rd->fd", hidden, cotangent, preferred_element_type=f32)
-    grad_down = reduce_rows(grad_down.astype(bf16), "fsdp", "ctx")
+    down_chain = Chain(grad_down.astype(bf16))
+    cotangent = gate(cotangent, down_chain)
     d_hidden = jnp.einsum("rd,fd->rf", cotangent, down_weight, preferred_element_type=f32)
     _, gelu_pull = jax.vjp(gelu_product, gate_pre, up_pre)
     d_gate, d_up = gelu_pull(d_hidden)
     d_both = jnp.concatenate([d_gate.astype(bf16), d_up.astype(bf16)], axis=1)
+    d_both = gate(d_both, down_chain)
     grad_gu = jnp.einsum("rd,rf->df", norm_two, d_both, preferred_element_type=f32)
-    grad_gu = reduce_rows(grad_gu.astype(bf16), "fsdp", "ctx")
+    gu_chain = Chain(grad_gu.astype(bf16))
+    d_both = gate(d_both, gu_chain)
     d_norm_two = jnp.einsum("rf,df->rd", d_both, gate_up, preferred_element_type=f32)
     _, norm_pull_two = jax.vjp(rms_scale, resid, gain_two)
     d_resid_norm, grad_gain_two = norm_pull_two(d_norm_two)
     d_resid = cotangent.astype(f32) + d_resid_norm
     d_branch = d_resid.astype(bf16)
-    grad_out = jnp.einsum("ra,rd->ad", attended_low, d_branch, preferred_element_type=f32)
     d_attended = jnp.einsum("rd,ad->ra", d_branch, out_weight, preferred_element_type=f32)
-    d_attended = d_attended.astype(bf16)
+    d_attended = gate(d_attended.astype(bf16), gu_chain, down_chain)
 
     d_queries, d_keys, d_values, d_bias = attend_back(
         lead,
@@ -988,16 +1057,20 @@
         buckets,
         rel,
     )
+    d_queries = gate(d_queries, gu_chain, down_chain)
     grad_qkv = jnp.concatenate(
         [
             jnp.einsum("rd,ra->da", norm_own, d_queries, preferred_element_type=f32),
             jnp.einsum("rd,ra->da", norm_one, d_keys, preferred_element_type=f32),
             jnp.einsum("rd,ra->da", norm_one, d_values, preferred_element_type=f32),
-            grad_out,
+            jnp.einsum("ra,rd->ad", attended_low, d_branch, preferred_element_type=f32),
         ],
         axis=1,
     )
-    grad_qkv = reduce_rows(grad_qkv.astype(bf16), "fsdp", "ctx")
+    qkv_chain = Chain(grad_qkv.astype(bf16))
+    d_queries, d_keys, d_values = gate(
+        (d_queries, d_keys, d_values), qkv_chain, down_chain
+    )
     d_norm_query = jnp.einsum("ra,da->rd", d_queries, query_weight, preferred_element_type=f32)
     d_norm_one = jnp.einsum(
         "ra,da->rd", d_keys, key_weight, preferred_element_type=f32
@@ -1008,9 +1081,9 @@
         d_norm_one = lax.dynamic_update_slice_in_dim(
             d_norm_one, old + d_norm_query[s * BLK : (s + 1) * BLK], start, 0
         )
+    d_norm_one = gate(d_norm_one, qkv_chain, gu_chain)
 
     vocab_rows = -(-vocab // 16) * 16
-    table_tall = jnp.pad(table, ((0, vocab_rows - vocab), (0, 0)))
     small = byte_backward(
         lead,
         phases,
@@ -1019,7 +1092,8 @@
         d_resid.reshape(seq_count, BLK, width),
         conv,
         mix,
-        table_tall,
+        table_wide,
+        vocab_rows,
         conv_w,
         score_w,
         gain_one,
@@ -1028,8 +1102,12 @@
     bias_grad = jnp.transpose(d_bias[:, :2].reshape(heads, levels)).reshape(1, levels * heads)
     bias_grad = jnp.pad(bias_grad, ((0, 0), (0, width - levels * heads)))
     small = jnp.concatenate([small[: vocab_rows + 6], grad_gain_two[None], bias_grad], axis=0)
-    small = jnp.pad(small, ((0, -small.shape[0] % 32), (0, 0))).astype(bf16)
-    small = reduce_all(small, ("fsdp", "ctx")).astype(f32)
+    small = jnp.pad(small, ((0, -small.shape[0] % (8 * ctx_count)), (0, 0))).astype(bf16)
+    small = gate(small, qkv_chain, gu_chain)
+    small = reduce_small(small).astype(f32)
+    grad_down = down_chain.finish()
+    grad_gu = gu_chain.finish()
+    grad_qkv = qkv_chain.finish()
     top = vocab_rows
     return (
         output,
@@ -1039,13 +1117,13 @@
         small[top + 5],
         small[top + 6],
         small[top + 7, : levels * heads].reshape(levels, heads),
-        grad_qkv[:, :width].astype(f32),
-        grad_qkv[:, width : 2 * width].astype(f32),
-        grad_qkv[:, 2 * width : 3 * width].astype(f32),
-        grad_qkv[:, 3 * width :].astype(f32),
-        grad_gu[:, :hidden_width].astype(f32),
-        grad_gu[:, hidden_width:].astype(f32),
-        grad_down.astype(f32),
+        grad_qkv[:, :width],
+        grad_qkv[:, width : 2 * width],
+        grad_qkv[:, 2 * width : 3 * width],
+        grad_qkv[:, 3 * width :],
+        grad_gu[:, :hidden_width],
+        grad_gu[:, hidden_width:],
+        grad_down,
     )
 
 

time: 574 us -> 544 us (0.948)
  waiting for transfers between devices: 138 us -> 82.7 us
  blocking collectives: 0 us -> 32.8 us
  Pallas kernels: 161 us -> 147 us
  between operations: 2.51 us -> 15.6 us
  starting transfers between devices: 86.3 us -> 98.7 us
  other arithmetic: 45.1 us -> 33.2 us
  matrix products: 66 us -> 57.8 us
    ppermute x46 -> x25, waiting for transfers between devices: 128 us -> 45.9 us  [swap(): return lax.ppermute(value, axis, [(i, i ^ 1 << bit) for i in range(count)])]
    ppermute x0 -> x15, starting transfers between devices: none -> 37.2 us  [the longest x12 32.2 us: rest_sum(): lax.ppermute(piece(value, mine ^ j), axis, pairs).astype(f32)]
    all_gather x0 -> x1, blocking collectives: none -> 32.8 us  [reduce_rows(): yield lax.all_gather(value, sum_axis, axis=0, tiled=True)]
    ppermute x0 -> x15, waiting for transfers between devices: none -> 22.7 us  [the longest x12 22.7 us: rest_sum(): lax.ppermute(piece(value, mine ^ j), axis, pairs).astype(f32)]
    ppermute x6, starting transfers between devices: 24.6 us -> 9.09 us  [to_owner(): return lax.ppermute(block, 'ctx', pairs)]
    ppermute x46 -> x25, starting transfers between devices: 61.7 us -> 52.4 us  [swap(): return lax.ppermute(value, axis, [(i, i ^ 1 << bit) for i in range(count)])]
    pallas_call x1, Pallas kernels: 55 us -> 48.1 us  [attend_back(): pl.pallas_call(attend_back_kernel, grid=(pairs,), out_shape=(jax.ShapeDty...]
    pallas_call x1, Pallas kernels: 44.1 us -> 37.5 us  [attend(): pl.pallas_call(attend_kernel, grid=(pairs,), out_shape=(jax.ShapeDtypeStr...]
  transfers between devices with their start and end apart: 52 -> 48, of which waited for: 25 -> 12; matrix products, arithmetic and copies ran while one was open for 21% -> 24% of each run, Pallas kernels for 19% -> 27%
where the time goes in v2:
time: 544 us; the launch traced here: 535 us
  Pallas kernels  147 us (27%)
  starting transfers between devices  98.7 us (18%)
  waiting for transfers between devices  82.7 us (15%)
  local copies, waits for them, and re-layouts  67.1 us (12%)
  matrix products  57.8 us (11%)
  other arithmetic  33.2 us (6%)
  blocking collectives  32.8 us (6%)
  between operations  15.6 us (3%)
    ppermute x25, starting transfers between devices, swap(): return lax.ppermute(value, axis, [(i, i ^ 1 << bit) for i in range(count)])  52.4 us
    pallas_call x1, Pallas kernels, attend_back(): pl.pallas_call(attend_back_kernel, grid=(pairs,), out_shape=(jax.ShapeDty...  48.1 us
    ppermute x25, waiting for transfers between devices, swap(): return lax.ppermute(value, axis, [(i, i ^ 1 << bit) for i in range(count)])  45.9 us
    pallas_call x1, Pallas kernels, attend(): pl.pallas_call(attend_kernel, grid=(pairs,), out_shape=(jax.ShapeDtypeStr...  37.5 us
    pallas_call x1, Pallas kernels, byte_backward(): pl.pallas_call(functools.partial(byte_backward_kernel, total_bytes), out_...  33.2 us
    all_gather x1, blocking collectives, reduce_rows(): yield lax.all_gather(value, sum_axis, axis=0, tiled=True)  32.8 us
    ppermute x12, starting transfers between devices, rest_sum(): lax.ppermute(piece(value, mine ^ j), axis, pairs).astype(f32)  32.2 us
    pallas_call x1, Pallas kernels, byte_forward(): pl.pallas_call(functools.partial(byte_forward_kernel, total_bytes), out_s...  28.3 us
  transfers between devices with their start and end apart: 48, of which 12 were waited for; matrix products, arithmetic and copies ran while one was open for 24% of the time, Pallas kernels for 27%

profile of v2, /device:TPU:0, one launch (start us, length us, event | category | flops | bytes accessed | tf_op | source)
XLA Modules:
  0.0 535.0 jit_solution(1886449848161833535)
XLA Ops:
  61.1 28.3 %byte_forward.1 = (f32[1024,768]{1,0:T(8,128)}, bf16[1024,768]{1,0:T(8,128)(2,1)}, f32[12,176,768]{2,1,0:T(8,128)}, f32[4,176,128]{2,1,0:T(8,128)}) custom-call(s32[16,256]{1,0:T(8,128)} %pad.32.ids_ref, f32[384,768]{1,0:T(8,128)} %pad.33.table_ref, f32[4,768]{1,0:T(4,128)} %conv_w_ref.3, f32[1,768]{1,0:T(1,128)} %reshape.154.score_ref, ...), custom_call_target="tpu_custom_call" | custom-call | flops 20000000000 | bytes 16777216 | tf_op jit(solution)/shard_map/byte_forward/pallas_call | solution.py:175
  97.4 5.5 %collective-permute-done.15 = bf16[128,768]{1,0:T(8,128)(2,1)S(1)} collective-permute-done((bf16[128,768]{1,0:T(8,128)(2,1)S(1)}, bf16[128,768]{1,0:T(8,128)(2,1)S(1)}, u32[]{:S(2)}, u32[]{:S(2)}) %collective-permute-start.15) | collective-permute-done | bytes 196640 | tf_op jit(solution)/shard_map/ppermute | solution.py:981
  121.4 23.6 %collective-permute-done.6 = bf16[192,4864]{1,0:T(8,128)(2,1)} collective-permute-done((bf16[192,4864]{1,0:T(8,128)(2,1)}, bf16[192,4864]{1,0:T(8,128)(2,1)}, u32[]{:S(2)}, u32[]{:S(2)}) %collective-permute-start.6) | collective-permute-done | bytes 1867808 | tf_op jit(solution)/shard_map/ppermute | solution.py:790
  145.0 37.5 %attend.1 = (f32[512,768]{1,0:T(8,128)}, bf16[512,768]{1,0:T(8,128)(2,1)}, f32[6,4,256]{2,1,0:T(4,128)}) custom-call(s32[4]{0:T(128)} %pad_add_fusion.4.lead_ref.first_ref, s32[4]{0:T(128)} %convert_reduce_fusion.4.low_ref, s32[4]{0:T(128)} %get-tuple-element.131.high_ref, bf16[512,768]{1,0:T(8,128)(2,1)} %convolution_convert_fusion.9.q_ref, ...), custom_call_target="tpu_custom_call" | custom-call | flops 24999999488 | bytes 8388608 | tf_op jit(solution)/shard_map/attend/pallas_call | solution.py:563
  196.7 4.6 multiply_convert_fusion.1
  204.3 7.2 %collective-permute-start.18 = (bf16[2,512,768]{2,1,0:T(8,128)(2,1)S(1)}, bf16[2,512,768]{2,1,0:T(8,128)(2,1)S(1)}, u32[]{:S(2)}, u32[]{:S(2)}) collective-permute-start(bf16[2,512,768]{2,1,0:T(8,128)(2,1)S(1)} %dynamic-slice_bitcast_fusion.3), channel_id=1, source_target_pairs={{0,1},{1,0},{2,3},{3,2},{4,5},{5,4},{6,7},{7,6},{8,9},{9,8},{10,11... | collective-permute-start | bytes 4718600 | tf_op jit(solution)/shard_map/ppermute | solution.py:790
  211.5 6.2 %fusion.10 = (bf16[512,2048]{1,0:T(8,128)(2,1)S(1)}, bf16[512,2048]{1,0:T(8,128)(2,1)S(1)}) fusion(f32[512,2048]{1,0:T(8,128)S(1)} %fusion.13, f32[512,2048]{1,0:T(8,128)S(1)} %get-tuple-element.190, bf16[512,768]{1,0:T(8,128)(2,1)S(1)} %copy-done.8, bf16[2048,768]{1,0:T(8,128)(2,1)} %constant_dynamic-update-slice_fusion), kind=kOutput, calls=%fused_computation.16 | convolution fusion | flops 1635778560 | bytes 16515072 | tf_op jit(solution)/shard_map/rd,fd->rf/dot_general | solution.py:1030
  218.6 3.9 convolution_convert_fusion
  230.8 10.4 %collective-permute-start.20 = (bf16[512,768]{1,0:T(8,128)(2,1)S(1)}, bf16[512,768]{1,0:T(8,128)(2,1)S(1)}, u32[]{:S(2)}, u32[]{:S(2)}) collective-permute-start(bf16[512,768]{1,0:T(8,128)(2,1)S(1)} %dynamic-slice_bitcast_fusion.6), channel_id=1, source_target_pairs={{0,2},{1,3},{2,0},{3,1},{4,6},{5,7},{6,4},{7,5},{8,10},{9,11},{10,... | collective-permute-start | bytes 2359304 | tf_op jit(solution)/shard_map/ppermute | solution.py:790
  241.1 6.4 %multiply_reduce_fusion = (bf16[768]{0:T(1024)(128)(2,1)S(1)}, f32[512]{0:T(512)S(1)}, f32[512,768]{1,0:T(8,128)S(1)}) fusion(f32[512,768]{1,0:T(8,128)S(1)} %get-tuple-element.188, f32[512]{0:T(512)S(1)} %fusion.54, f32[768]{0:T(1024)S(1)} %copy-done.41, bf16[512,4096]{1,0:T(8,128)(2,1)S(1)} %pad_maximum_fusion.1, ...), kind=kOutput, calls=%fused_computation.45 | convolution fusion | flops 3223583488 | bytes 13640192 | tf_op jit(solution)/shard_map/rf,df->rd/dot_general | solution.py:1038
  253.4 5.2 collective-permute-done.20
  263.8 3.8 collective-permute-start.22
  267.7 48.1 %attend_back.1 = (bf16[512,768]{1,0:T(8,128)(2,1)}, bf16[1024,768]{1,0:T(8,128)(2,1)}, bf16[1024,768]{1,0:T(8,128)(2,1)}, f32[6,8,32]{2,1,0:T(8,128)}) custom-call(s32[4]{0:T(128)} %pad_add_fusion.4.lead_ref.first_ref, s32[4]{0:T(128)} %convert_reduce_fusion.4.low_ref, s32[4]{0:T(128)} %get-tuple-element.131.high_ref, ...), custom_call_target="tpu_custom_call" | custom-call | flops 35000000512 | bytes 8388608 | tf_op jit(solution)/shard_map/attend_back/pallas_call | solution.py:728
  315.7 4.3 convolution_convert_fusion.5
  327.7 9.9 %collective-permute-start.25 = (bf16[64,768]{1,0:T(8,128)(2,1)S(1)}, bf16[64,768]{1,0:T(8,128)(2,1)S(1)}, u32[]{:S(2)}, u32[]{:S(2)}) collective-permute-start(bf16[64,768]{1,0:T(8,128)(2,1)S(1)} %get-tuple-element.176), channel_id=1, source_target_pairs={{0,24},{4,28},{8,16},{12,20},{16,8},{20,12},{24,0},{28,4},{1,25},{... | collective-permute-start | bytes 294920 | tf_op jit(solution)/shard_map/ppermute | solution.py:842
  337.6 9.0 %collective-permute-start.24 = (bf16[64,768]{1,0:T(8,128)(2,1)S(1)}, bf16[64,768]{1,0:T(8,128)(2,1)S(1)}, u32[]{:S(2)}, u32[]{:S(2)}) collective-permute-start(bf16[64,768]{1,0:T(8,128)(2,1)S(1)} %get-tuple-element.177), channel_id=1, source_target_pairs={{0,16},{4,20},{8,24},{12,28},{16,0},{20,4},{24,8},{28,12},{1,17},{... | collective-permute-start | bytes 294920 | tf_op jit(solution)/shard_map/ppermute | solution.py:842
  347.6 6.0 %collective-permute-start.27 = (bf16[4,24,4096]{2,1,0:T(8,128)(2,1)S(1)}, bf16[4,24,4096]{2,1,0:T(8,128)(2,1)S(1)}, u32[]{:S(2)}, u32[]{:S(2)}) collective-permute-start(bf16[4,24,4096]{2,1,0:T(8,128)(2,1)S(1)} %dynamic-slice_bitcast_fusion.5), channel_id=1, source_target_pairs={{0,4},{4,0},{8,12},{12,8},{16,20},{20,16},{24,28},{28,24},{1,5},{5... | collective-permute-start | bytes 2359304 | tf_op jit(solution)/shard_map/ppermute | solution.py:790
  359.7 3.9 collective-permute-done.27
  365.8 6.4 %collective-permute-start.28 = (bf16[192,3072]{1,0:T(8,128)(2,1)}, bf16[192,3072]{1,0:T(8,128)(2,1)}, u32[]{:S(2)}, u32[]{:S(2)}) collective-permute-start(bf16[192,3072]{1,0:T(8,128)(2,1)} %dynamic-slice_bitcast_fusion.4), channel_id=1, source_target_pairs={{0,2},{1,3},{2,0},{3,1},{4,6},{5,7},{6,4},{7,5},{8,10},{9,11},{10,... | collective-permute-start | bytes 3538952 | tf_op jit(solution)/shard_map/ppermute | solution.py:790
  377.4 33.2 %byte_backward.1 = f32[280,768]{1,0:T(8,128)} custom-call(s32[4]{0:T(128)} %pad_add_fusion.4.lead_ref.first_ref, s32[16,256]{1,0:T(8,128)} %pad.32.ids_ref, f32[1024,768]{1,0:T(8,128)} %get-tuple-element.57.tok_ref, f32[1024,768]{1,0:T(8,128)} %copy-done, f32[4,128,768]{2,1,0:T(8,128)} %bitcast.180, f32[12,176,768]{2,1,0:T(8,128)} %get-tuple-element.87.conv_ref, ...), custom_call_target="tpu_custom_call" | custom-call | flops 20000000000 | bytes 16777216 | tf_op jit(solution)/shard_map/byte_backward/pallas_call | solution.py:402
  419.6 4.9 collective-permute-done.13
  438.2 10.5 %collective-permute-done.36 = bf16[40,768]{1,0:T(8,128)(2,1)S(1)} collective-permute-done((bf16[40,768]{1,0:T(8,128)(2,1)S(1)}, bf16[40,768]{1,0:T(8,128)(2,1)S(1)}, u32[]{:S(2)}, u32[]{:S(2)}) %collective-permute-start.36) | collective-permute-done | bytes 61472 | tf_op jit(solution)/shard_map/ppermute | solution.py:790
  462.1 17.7 %collective-permute-done.44 = bf16[24,3072]{1,0:T(8,128)(2,1)S(1)} collective-permute-done((bf16[24,3072]{1,0:T(8,128)(2,1)S(1)}, bf16[24,3072]{1,0:T(8,128)(2,1)S(1)}, u32[]{:S(2)}, u32[]{:S(2)}) %collective-permute-start.44) | collective-permute-done | bytes 147488 | tf_op jit(solution)/shard_map/ppermute | solution.py:842
  480.7 32.8 %all_gather.11 = bf16[512,768]{1,0:T(8,128)(2,1)S(1)} all-gather(bf16[64,768]{1,0:T(8,128)(2,1)S(1)} %copy-done.20), channel_id=1, replica_groups=mesh['ctx'=8,'fsdp'=4] {'ctx'}, dimensions={0}, use_global_device_ids=true | all-gather | bytes 884736 | tf_op jit(solution)/shard_map/all_gather | solution.py:858
  (321 shorter events, 190.3 us)
Async XLA Ops:
  7.2 510.7 %all-gather.5.cloned.1.call-start = ((), (), s32[]{:S(2)}) async-start(), calls=%async_computation.1 | async-start | bytes 1769472 | tf_op jit(solution)/shard_map/all_gather | solution.py:858
  14.6 94.2 %collective-permute-start.3 = (bf16[192,2304]{1,0:T(8,128)(2,1)}, bf16[192,2304]{1,0:T(8,128)(2,1)}, u32[]{:S(2)}, u32[]{:S(2)}) collective-permute-start(bf16[192,2304]{1,0:T(8,128)(2,1)} %pad_maximum_fusion.3), channel_id=1, source_target_pairs={{0,2},{1,3},{2,0},{3,1},{4,6},{5,7},{6,4},{7,5},{8,10},{9,11},{10,... | collective-permute-start | bytes 2654216 | tf_op jit(solution)/shard_map/ppermute | solution.py:790
  19.3 76.0 %collective-permute-start.17 = (bf16[128,768]{1,0:T(8,128)(2,1)}, bf16[128,768]{1,0:T(8,128)(2,1)}, u32[]{:S(2)}, u32[]{:S(2)}) collective-permute-start(bf16[128,768]{1,0:T(8,128)(2,1)} %bitcast.173), channel_id=1, source_target_pairs={{0,24},{4,28},{8,16},{12,20},{16,8},{20,12},{24,0},{28,4},{1,25},{... | collective-permute-start | bytes 589832 | tf_op jit(solution)/shard_map/ppermute | solution.py:981
  23.6 72.3 %collective-permute-start.16 = (bf16[128,768]{1,0:T(8,128)(2,1)}, bf16[128,768]{1,0:T(8,128)(2,1)}, u32[]{:S(2)}, u32[]{:S(2)}) collective-permute-start(bf16[128,768]{1,0:T(8,128)(2,1)} %bitcast.174), channel_id=1, source_target_pairs={{0,16},{4,20},{8,24},{12,28},{16,0},{20,4},{24,8},{28,12},{1,17},{... | collective-permute-start | bytes 589832 | tf_op jit(solution)/shard_map/ppermute | solution.py:981
  50.1 56.1 %collective-permute-start.9 = (bf16[512,768]{1,0:T(8,128)(2,1)}, bf16[512,768]{1,0:T(8,128)(2,1)}, u32[]{:S(2)}, u32[]{:S(2)}) collective-permute-start(bf16[512,768]{1,0:T(8,128)(2,1)} %get-tuple-element.136), channel_id=1, source_target_pairs={{0,2},{1,3},{2,0},{3,1},{4,6},{5,7},{6,4},{7,5},{8,10},{9,11},{10,... | collective-permute-start | bytes 2359304 | tf_op jit(solution)/shard_map/ppermute | solution.py:790
  50.6 57.6 %collective-permute-start.10 = (bf16[512,768]{1,0:T(8,128)(2,1)}, bf16[512,768]{1,0:T(8,128)(2,1)}, u32[]{:S(2)}, u32[]{:S(2)}) collective-permute-start(bf16[512,768]{1,0:T(8,128)(2,1)} %get-tuple-element.136), channel_id=1, source_target_pairs={{0,1},{1,0},{2,3},{3,2},{4,5},{5,4},{6,7},{7,6},{8,9},{9,8},{10,11... | collective-permute-start | bytes 2359304 | tf_op jit(solution)/shard_map/ppermute | solution.py:790
  102.8 42.2 %collective-permute-start.6 = (bf16[192,4864]{1,0:T(8,128)(2,1)}, bf16[192,4864]{1,0:T(8,128)(2,1)}, u32[]{:S(2)}, u32[]{:S(2)}) collective-permute-start(bf16[192,4864]{1,0:T(8,128)(2,1)} %get-tuple-element.143), channel_id=1, source_target_pairs={{0,2},{1,3},{2,0},{3,1},{4,6},{5,7},{6,4},{7,5},{8,10},{9,11},{10,... | collective-permute-start | bytes 5603336 | tf_op jit(solution)/shard_map/ppermute | solution.py:790
  106.2 79.3 %collective-permute-start.7 = (bf16[192,4864]{1,0:T(8,128)(2,1)}, bf16[192,4864]{1,0:T(8,128)(2,1)}, u32[]{:S(2)}, u32[]{:S(2)}) collective-permute-start(bf16[192,4864]{1,0:T(8,128)(2,1)} %get-tuple-element.143), channel_id=1, source_target_pairs={{0,1},{1,0},{2,3},{3,2},{4,5},{5,4},{6,7},{7,6},{8,9},{9,8},{10,11... | collective-permute-start | bytes 5603336 | tf_op jit(solution)/shard_map/ppermute | solution.py:790
  145.0 43.4 %collective-permute-start.8 = (bf16[192,4864]{1,0:T(8,128)(2,1)}, bf16[192,4864]{1,0:T(8,128)(2,1)S(1)}, u32[]{:S(2)}, u32[]{:S(2)}) collective-permute-start(bf16[192,4864]{1,0:T(8,128)(2,1)} %collective-permute-done.6), channel_id=1, source_target_pairs={{0,1},{1,0},{2,3},{3,2},{4,5},{5,4},{6,7},{7,6},{8,9},{9,8},{10,11... | collective-permute-start | bytes 5603336 | tf_op jit(solution)/shard_map/ppermute | solution.py:790
  222.9 36.0 %collective-permute-start.19 = (bf16[2,192,4096]{2,1,0:T(8,128)(2,1)S(1)}, bf16[2,192,4096]{2,1,0:T(8,128)(2,1)S(1)}, u32[]{:S(2)}, u32[]{:S(2)}) collective-permute-start(bf16[2,192,4096]{2,1,0:T(8,128)(2,1)S(1)} %dynamic-slice_bitcast_fusion), channel_id=1, source_target_pairs={{0,1},{1,0},{2,3},{3,2},{4,5},{5,4},{6,7},{7,6},{8,9},{9,8},{10,11... | collective-permute-start | bytes 9437192 | tf_op jit(solution)/shard_map/ppermute | solution.py:790
  228.5 191.2 %collective-permute-start.14 = (bf16[128,768]{1,0:T(8,128)(2,1)}, bf16[128,768]{1,0:T(8,128)(2,1)}, u32[]{:S(2)}, u32[]{:S(2)}) collective-permute-start(bf16[128,768]{1,0:T(8,128)(2,1)} %get-tuple-element.167), channel_id=1, source_target_pairs={{0,24},{4,28},{8,16},{12,20},{16,8},{20,12},{24,0},{28,4},{1,25},{... | collective-permute-start | bytes 589832 | tf_op jit(solution)/shard_map/ppermute | solution.py:981
  230.8 27.8 %collective-permute-start.20 = (bf16[512,768]{1,0:T(8,128)(2,1)S(1)}, bf16[512,768]{1,0:T(8,128)(2,1)S(1)}, u32[]{:S(2)}, u32[]{:S(2)}) collective-permute-start(bf16[512,768]{1,0:T(8,128)(2,1)S(1)} %dynamic-slice_bitcast_fusion.6), channel_id=1, source_target_pairs={{0,2},{1,3},{2,0},{3,1},{4,6},{5,7},{6,4},{7,5},{8,10},{9,11},{10,... | collective-permute-start | bytes 2359304 | tf_op jit(solution)/shard_map/ppermute | solution.py:790
  261.3 63.3 %collective-permute-start.21 = (bf16[192,4096]{1,0:T(8,128)(2,1)}, bf16[192,4096]{1,0:T(8,128)(2,1)}, u32[]{:S(2)}, u32[]{:S(2)}) collective-permute-start(bf16[192,4096]{1,0:T(8,128)(2,1)} %dynamic-slice_bitcast_fusion.2), channel_id=1, source_target_pairs={{0,2},{1,3},{2,0},{3,1},{4,6},{5,7},{6,4},{7,5},{8,10},{9,11},{10,... | collective-permute-start | bytes 4718600 | tf_op jit(solution)/shard_map/ppermute | solution.py:790
  263.8 60.6 %collective-permute-start.22 = (bf16[4,64,768]{2,1,0:T(8,128)(2,1)}, bf16[4,64,768]{2,1,0:T(8,128)(2,1)S(1)}, u32[]{:S(2)}, u32[]{:S(2)}) collective-permute-start(bf16[4,64,768]{2,1,0:T(8,128)(2,1)} %dynamic-slice_bitcast_fusion.8), channel_id=1, source_target_pairs={{0,4},{4,0},{8,12},{12,8},{16,20},{20,16},{24,28},{28,24},{1,5},{5... | collective-permute-start | bytes 1179656 | tf_op jit(solution)/shard_map/ppermute | solution.py:790
  365.8 52.0 %collective-permute-start.28 = (bf16[192,3072]{1,0:T(8,128)(2,1)}, bf16[192,3072]{1,0:T(8,128)(2,1)}, u32[]{:S(2)}, u32[]{:S(2)}) collective-permute-start(bf16[192,3072]{1,0:T(8,128)(2,1)} %dynamic-slice_bitcast_fusion.4), channel_id=1, source_target_pairs={{0,2},{1,3},{2,0},{3,1},{4,6},{5,7},{6,4},{7,5},{8,10},{9,11},{10,... | collective-permute-start | bytes 3538952 | tf_op jit(solution)/shard_map/ppermute | solution.py:790
  373.0 39.7 %collective-permute-start.31 = (bf16[24,4096]{1,0:T(8,128)(2,1)}, bf16[24,4096]{1,0:T(8,128)(2,1)}, u32[]{:S(2)}, u32[]{:S(2)}) collective-permute-start(bf16[24,4096]{1,0:T(8,128)(2,1)} %get-tuple-element.156), channel_id=1, source_target_pairs={{0,24},{4,28},{8,16},{12,20},{16,8},{20,12},{24,0},{28,4},{1,25},{... | collective-permute-start | bytes 589832 | tf_op jit(solution)/shard_map/ppermute | solution.py:842
  375.7 38.7 %collective-permute-start.30 = (bf16[24,4096]{1,0:T(8,128)(2,1)}, bf16[24,4096]{1,0:T(8,128)(2,1)}, u32[]{:S(2)}, u32[]{:S(2)}) collective-permute-start(bf16[24,4096]{1,0:T(8,128)(2,1)} %get-tuple-element.157), channel_id=1, source_target_pairs={{0,16},{4,20},{8,24},{12,28},{16,0},{20,4},{24,8},{28,12},{1,17},{... | collective-permute-start | bytes 589832 | tf_op jit(solution)/shard_map/ppermute | solution.py:842
  377.1 38.8 %collective-permute-start.29 = (bf16[24,4096]{1,0:T(8,128)(2,1)}, bf16[24,4096]{1,0:T(8,128)(2,1)}, u32[]{:S(2)}, u32[]{:S(2)}) collective-permute-start(bf16[24,4096]{1,0:T(8,128)(2,1)} %get-tuple-element.155), channel_id=1, source_target_pairs={{0,8},{4,12},{8,0},{12,4},{16,24},{20,28},{24,16},{28,20},{1,9},{5... | collective-permute-start | bytes 589832 | tf_op jit(solution)/shard_map/ppermute | solution.py:842
  425.9 99.1 %all-gather.3.cloned.1.call-start = ((), (), s32[]{:S(2)}) async-start(), calls=%async_computation | async-start | bytes 1327104 | tf_op jit(solution)/shard_map/all_gather | solution.py:858
  450.9 28.9 %collective-permute-start.44 = (bf16[24,3072]{1,0:T(8,128)(2,1)S(1)}, bf16[24,3072]{1,0:T(8,128)(2,1)S(1)}, u32[]{:S(2)}, u32[]{:S(2)}) collective-permute-start(bf16[24,3072]{1,0:T(8,128)(2,1)S(1)} %get-tuple-element.172), channel_id=1, source_target_pairs={{0,16},{4,20},{8,24},{12,28},{16,0},{20,4},{24,8},{28,12},{1,17},{... | collective-permute-start | bytes 442376 | tf_op jit(solution)/shard_map/ppermute | solution.py:842
  451.1 28.6 %collective-permute-start.43 = (bf16[24,3072]{1,0:T(8,128)(2,1)S(1)}, bf16[24,3072]{1,0:T(8,128)(2,1)S(1)}, u32[]{:S(2)}, u32[]{:S(2)}) collective-permute-start(bf16[24,3072]{1,0:T(8,128)(2,1)S(1)} %get-tuple-element.170), channel_id=1, source_target_pairs={{0,8},{4,12},{8,0},{12,4},{16,24},{20,28},{24,16},{28,20},{1,9},{5... | collective-permute-start | bytes 442376 | tf_op jit(solution)/shard_map/ppermute | solution.py:842
  453.8 26.7 %collective-permute-start.38 = (bf16[40,768]{1,0:T(8,128)(2,1)S(1)}, bf16[40,768]{1,0:T(8,128)(2,1)S(1)}, u32[]{:S(2)}, u32[]{:S(2)}) collective-permute-start(bf16[40,768]{1,0:T(8,128)(2,1)S(1)} %get-tuple-element.134), channel_id=1, source_target_pairs={{0,8},{4,12},{8,0},{12,4},{16,24},{20,28},{24,16},{28,20},{1,9},{5... | collective-permute-start | bytes 184328 | tf_op jit(solution)/shard_map/ppermute | solution.py:903
  453.9 26.7 %collective-permute-start.39 = (bf16[40,768]{1,0:T(8,128)(2,1)S(1)}, bf16[40,768]{1,0:T(8,128)(2,1)S(1)}, u32[]{:S(2)}, u32[]{:S(2)}) collective-permute-start(bf16[40,768]{1,0:T(8,128)(2,1)S(1)} %get-tuple-element.134), channel_id=1, source_target_pairs={{0,16},{4,20},{8,24},{12,28},{16,0},{20,4},{24,8},{28,12},{1,17},{... | collective-permute-start | bytes 184328 | tf_op jit(solution)/shard_map/ppermute | solution.py:903
  480.6 34.2 %collective-permute-start.41 = (bf16[160,768]{1,0:T(8,128)(2,1)S(1)}, bf16[160,768]{1,0:T(8,128)(2,1)S(1)}, u32[]{:S(2)}, u32[]{:S(2)}) collective-permute-start(bf16[160,768]{1,0:T(8,128)(2,1)S(1)} %bitcast.195), channel_id=1, source_target_pairs={{0,1},{1,0},{2,3},{3,2},{4,5},{5,4},{6,7},{7,6},{8,9},{9,8},{10,11... | collective-permute-start | bytes 737288 | tf_op jit(solution)/shard_map/ppermute | solution.py:790
  (71 other events, 532.3 us)
Sparse Core Ops, SparseCore 0:
  426.0 54.1 all-gather.4
  483.0 41.9 all-gather.2

commit v3 on v2

--- a/solution.py
+++ b/solution.py
@@ -15,6 +15,7 @@
 HIGH = lax.Precision.HIGHEST
 NT = (((1,), (1,)), ((), ()))
 NN = (((1,), (0,)), ((), ()))
+LIGHT = pl.CostEstimate(flops=1, transcendentals=0, bytes_accessed=1)
 
 
 def lane_iota(rows):
@@ -46,35 +47,79 @@
 
 def byte_forward_kernel(
     total_bytes,
-    ids_ref,
+    seq_ref,
+    lead_ref,
+    both_ref,
     table_ref,
     conv_w_ref,
     score_ref,
     gain_ref,
     tok_ref,
     norm_ref,
+    norm_own_ref,
     conv_ref,
     mix_ref,
+    ids_ref,
+    known_ref,
+    barred_ref,
     hi_ref,
     lo_ref,
     emb,
     flat,
+    spread,
 ):
     groups = conv_ref.shape[1]
     width = conv_ref.shape[2]
     tiles = width // LANE
     token_count = norm_ref.shape[0]
-    vocab_pad = hi_ref.shape[0]
+    vocab_pad = table_ref.shape[0]
+    row_lanes = ids_ref.shape[1]
+    seq = seq_ref[0]
     high = table_ref[...].astype(bf16)
     hi_ref[...] = high
     lo_ref[...] = (table_ref[...] - high.astype(f32)).astype(bf16)
-    ids_cols = jnp.transpose(ids_ref[...].astype(f32))
-    vocab = lax.broadcasted_iota(jnp.int32, (groups, vocab_pad), 1).astype(f32)
+    lane_f = lane_iota(BLK).astype(f32)
+    chunk_bytes = both_ref.shape[3]
+
+    def lay(kind, first):
+        for block in range(both_ref.shape[0]):
+            row = both_ref[block, seq, kind : kind + 1, :].astype(f32)
+            for half in range(chunk_bytes // LANE):
+                part = jnp.broadcast_to(row[:, half * LANE : (half + 1) * LANE], (LANE, LANE))
+                start = first + block * chunk_bytes + half * LANE
+                spread[start : start + LANE, :] = jnp.transpose(part)
+
+    lay(1, 0)
+    for block in range(token_count // BLK):
+        docs = spread[pl.ds(block * 2 * BLK, BLK, stride=2), :]
+        same = docs == lane_f
+        rows = slice(block * BLK, (block + 1) * BLK)
+        known_ref[rows, :] = same.astype(bf16)
+        barred_ref[rows, :] = jnp.where(same | (lane_f >= 16.0), 0.0, -1e30).astype(bf16)
+    lay(0, 16)
+    none = jnp.full((16, LANE), -1.0, f32)
+    spread[0:16, :] = none
+    tail = spread.shape[0] - total_bytes - 16
+    spread[total_bytes + 16 :, :] = jnp.full((tail, LANE), -1.0, f32)
+    lane_g = lane_iota(groups).astype(f32)
     for r in range(15):
-        onehot = (ids_cols[0:groups, r : r + 1] == vocab).astype(bf16)
+        here = spread[pl.ds(13 + r, row_lanes, stride=12), :]
+        turned = [
+            jnp.transpose(here[n * LANE : (n + 1) * LANE, :])[0:1, :]
+            for n in range(row_lanes // LANE)
+        ]
+        ids_ref[r : r + 1, :] = jnp.concatenate(turned, axis=1)
+        onehot = jnp.concatenate(
+            [
+                (here[0:groups, :] == lane_g + n * LANE).astype(bf16)
+                for n in range(vocab_pad // LANE)
+            ],
+            axis=1,
+        )
         emb[r] = jnp.dot(onehot, hi_ref[...], preferred_element_type=f32) + jnp.dot(
             onehot, lo_ref[...], preferred_element_type=f32
         )
+    ids_ref[15:16, :] = jnp.full((1, row_lanes), -1.0, f32)
     lane = lane_iota(8)
 
     def chunk(i, masked):
@@ -156,40 +201,51 @@
         return carry
 
     lax.fori_loop(0, token_count // 16, norm, 0)
-
-
-def phase_ids(ids_row, total_bytes):
-    groups = -(-total_bytes // 12)
-    padded = jnp.pad(ids_row, (0, 12 * groups - total_bytes), constant_values=-1)
-    phases = jnp.transpose(padded.reshape(groups, 12))
-    before = jnp.pad(phases[9:12, :-1], ((0, 0), (1, 0)), constant_values=-1)
-    lanes = -(-groups // LANE) * LANE
-    both = jnp.concatenate([before, phases], axis=0)
-    return jnp.pad(both, ((0, 1), (0, lanes - groups)), constant_values=-1)
-
-
-def byte_forward(ids, table, conv_w, score_w, gain_one, total_bytes):
+    for slot in range(norm_own_ref.shape[0] // BLK):
+        start = pl.multiple_of(lead_ref[slot] * BLK, BLK)
+        norm_own_ref[slot * BLK : (slot + 1) * BLK, :] = norm_ref[pl.ds(start, BLK), :]
+
+
+def byte_forward(seq, lead, both, table, conv_w, score_w, gain_one, total_bytes):
     width = conv_w.shape[1]
     token_count = total_bytes // 2
-    groups = -(-(-(-total_bytes // 12)) // 16) * 16
+    least = -(-total_bytes // 12)
+    groups = -(-least // 16) * 16
+    row_lanes = -(-least // LANE) * LANE
+    smem = pl.BlockSpec(memory_space=pltpu.SMEM)
+    vmem = pl.BlockSpec(memory_space=pltpu.VMEM)
     return pl.pallas_call(
         functools.partial(byte_forward_kernel, total_bytes),
         out_shape=(
             jax.ShapeDtypeStruct((token_count, width), f32),
             jax.ShapeDtypeStruct((token_count, width), bf16),
+            jax.ShapeDtypeStruct((lead.shape[0] * BLK, width), bf16),
             jax.ShapeDtypeStruct((12, groups, width), f32),
             jax.ShapeDtypeStruct((4, groups, LANE), f32),
+            jax.ShapeDtypeStruct((16, row_lanes), f32),
+            jax.ShapeDtypeStruct((token_count, LANE), bf16),
+            jax.ShapeDtypeStruct((token_count, LANE), bf16),
         ),
+        in_specs=[smem, smem] + [vmem] * 5,
         scratch_shapes=[
             pltpu.VMEM(table.shape, bf16),
             pltpu.VMEM(table.shape, bf16),
             pltpu.VMEM((15, groups, width), f32),
             pltpu.VMEM((width // LANE, 6 * groups, LANE), f32),
+            pltpu.VMEM((12 * row_lanes + 32, LANE), f32),
         ],
         compiler_params=pltpu.CompilerParams(vmem_limit_bytes=VMEM_CAP),
-        cost_estimate=pl.CostEstimate(flops=20_000_000_000, transcendentals=0, bytes_accessed=1 << 24),
+        cost_estimate=LIGHT,
         name="byte_forward",
-    )(ids, table, conv_w, score_w.reshape(1, width), gain_one.reshape(1, width))
+    )(
+        seq,
+        lead,
+        both,
+        table,
+        conv_w,
+        score_w.reshape(1, width),
+        gain_one.reshape(1, width),
+    )
 
 
 def byte_backward_kernel(
@@ -247,7 +303,7 @@
             return carry
 
         lax.fori_loop(0, BLK // 8, add, 0)
-    vocab = lax.broadcasted_iota(jnp.int32, (vocab_rows, lanes), 0)
+    vocab = lax.broadcasted_iota(jnp.int32, (vocab_rows, lanes), 0).astype(f32)
     for r in range(15):
         onehot[:, r * lanes : (r + 1) * lanes] = (vocab == ids_ref[r : r + 1, :]).astype(bf16)
     for r in range(12):
@@ -410,7 +466,7 @@
             pltpu.VMEM((vocab_rows, 15 * lanes), bf16),
         ],
         compiler_params=pltpu.CompilerParams(vmem_limit_bytes=VMEM_CAP),
-        cost_estimate=pl.CostEstimate(flops=20_000_000_000, transcendentals=0, bytes_accessed=1 << 24),
+        cost_estimate=LIGHT,
         name="byte_backward",
     )(
         first,
@@ -436,18 +492,6 @@
 
 def two_heads(value):
     return jnp.concatenate([head_mask(value, 0), head_mask(value, 1)], axis=0)
-
-
-def doc_operands(docs_ref, known, barred):
-    blocks = docs_ref.shape[0]
-    cols = jnp.transpose(docs_ref[...].astype(f32))
-    lane = lane_iota(BLK).astype(f32)
-    for b in range(blocks):
-        same = cols[:, b : b + 1] == lane
-        known[b * BLK : (b + 1) * BLK, :] = same.astype(bf16)
-        barred[b * BLK : (b + 1) * BLK, :] = jnp.where(
-            same | (lane >= 16.0), 0.0, -1e30
-        ).astype(bf16)
 
 
 def bias_tiles(buckets_ref, rel_ref, tiles):
@@ -478,24 +522,19 @@
     q_ref,
     k_ref,
     v_ref,
-    docs_ref,
+    known,
+    barred,
     buckets_ref,
     rel_ref,
     out_ref,
     low_out_ref,
     log_ref,
-    known,
-    barred,
     tiles,
     v_turned,
     held,
 ):
     reach = tiles.shape[0] // 2
     slots = q_ref.shape[0] // BLK
-
-    @pl.when(pl.program_id(0) == 0)
-    def _():
-        doc_operands(docs_ref, known, barred)
 
     bias_tiles(buckets_ref, rel_ref.at[0], tiles)
     v_turned[...] = jnp.transpose(v_ref[...])
@@ -545,11 +584,11 @@
         log_ref[0, slot : slot + 1, :] = best + jnp.log(total)
 
 
-def attend(lead, low, high, q, k, v, docs, buckets, rel):
+def attend(lead, low, high, q, k, v, known, barred, buckets, rel):
     rows, width = q.shape
     keys = k.shape[0]
     pairs = width // BLK
-    blocks = docs.shape[0]
+    blocks = keys // BLK
     slots = rows // BLK
     reach = blocks // 2
     smem = pl.BlockSpec(memory_space=pltpu.SMEM)
@@ -575,7 +614,8 @@
             cols(rows),
             cols(keys),
             cols(keys),
-            whole(docs),
+            whole(known),
+            whole(barred),
             whole(buckets),
             pl.BlockSpec((1,) + rel.shape[1:], lambda i: (i, 0, 0)),
         ],
@@ -585,16 +625,14 @@
             pl.BlockSpec((1, slots, 2 * BLK), lambda i: (i, 0, 0)),
         ),
         scratch_shapes=[
-            pltpu.VMEM((keys, BLK), bf16),
-            pltpu.VMEM((keys, BLK), bf16),
             pltpu.VMEM((2 * reach + 1, BLK, 2 * BLK), f32),
             pltpu.VMEM((BLK, keys), bf16),
             pltpu.VMEM((blocks, BLK, 2 * BLK), f32),
         ],
         compiler_params=pltpu.CompilerParams(vmem_limit_bytes=VMEM_CAP),
-        cost_estimate=pl.CostEstimate(flops=25_000_000_000, transcendentals=0, bytes_accessed=1 << 23),
+        cost_estimate=LIGHT,
         name="attend",
-    )(lead, low, high, q, k, v, docs, buckets, rel)
+    )(lead, low, high, q, k, v, known, barred, buckets, rel)
 
 
 def attend_back_kernel(
@@ -607,15 +645,14 @@
     g_ref,
     out_ref,
     log_ref,
-    docs_ref,
+    known,
+    barred,
     buckets_ref,
     rel_ref,
     dq_ref,
     dk_ref,
     dv_ref,
     dbias_ref,
-    known,
-    barred,
     tiles,
     k_turned,
     dk_acc,
@@ -624,13 +661,9 @@
 ):
     reach = tiles.shape[0] // 2
     count = tiles.shape[0]
-    blocks = docs_ref.shape[0]
+    blocks = k_ref.shape[0] // BLK
     slots = q_ref.shape[0] // BLK
     half = BLK // 2
-
-    @pl.when(pl.program_id(0) == 0)
-    def _():
-        doc_operands(docs_ref, known, barred)
 
     bias_tiles(buckets_ref, rel_ref.at[0], tiles)
     k_turned[...] = jnp.transpose(k_ref[...])
@@ -706,11 +739,11 @@
     dbias_ref[0] = total
 
 
-def attend_back(lead, low, high, q, k, v, g, out, log, docs, buckets, rel):
+def attend_back(lead, low, high, q, k, v, g, out, log, known, barred, buckets, rel):
     rows, width = q.shape
     keys = k.shape[0]
     pairs = width // BLK
-    blocks = docs.shape[0]
+    blocks = keys // BLK
     slots = rows // BLK
     reach = blocks // 2
     levels = rel.shape[2]
@@ -744,14 +777,13 @@
             cols(rows),
             cols(rows),
             lead_block((slots, 2 * BLK)),
-            whole(docs),
+            whole(known),
+            whole(barred),
             whole(buckets),
             lead_block(rel.shape[1:]),
         ],
         out_specs=(cols(rows), cols(keys), cols(keys), lead_block((8, levels))),
         scratch_shapes=[
-            pltpu.VMEM((keys, BLK), bf16),
-            pltpu.VMEM((keys, BLK), bf16),
             pltpu.VMEM((2 * reach + 1, BLK, 2 * BLK), f32),
             pltpu.VMEM((BLK, keys), bf16),
             pltpu.VMEM((keys, BLK), f32),
@@ -759,15 +791,13 @@
             pltpu.VMEM((2 * reach + 1, BLK, 2 * BLK), f32),
         ],
         compiler_params=pltpu.CompilerParams(vmem_limit_bytes=VMEM_CAP),
-        cost_estimate=pl.CostEstimate(flops=35_000_000_000, transcendentals=0, bytes_accessed=1 << 23),
+        cost_estimate=LIGHT,
         name="attend_back",
-    )(lead, low, high, q, k, v, g, out, log, docs, buckets, rel)
-
-
-def attention_tables(docs, rel_bucket, rel_bias, lead):
-    blocks = docs.shape[0]
-    starts = docs[:, 0]
-    ends = docs[:, -1]
+    )(lead, low, high, q, k, v, g, out, log, known, barred, buckets, rel)
+
+
+def attention_tables(starts, ends, rel_bucket, rel_bias, lead):
+    blocks = starts.shape[0]
     mine = (lead[:, None] == jnp.arange(blocks)[None, :]).astype(jnp.int32)
     own_start = jnp.sum(mine * starts[None, :], axis=1)
     own_end = jnp.sum(mine * ends[None, :], axis=1)
@@ -777,6 +807,44 @@
     levels, heads = rel_bias.shape
     rel = jnp.transpose(rel_bias).reshape(heads // 2, 2, levels)
     return low, high, buckets, rel
+
+
+def pack_kernel(*refs):
+    outs = [ref for ref in refs if ref.dtype == bf16]
+    masters = [ref for ref in refs if ref.dtype == f32]
+    at = 0
+    for out in outs:
+        col = 0
+        while col < out.shape[1]:
+            wide = masters[at].shape[1]
+            out[:, col : col + wide] = masters[at][...].astype(bf16)
+            col += wide
+            at += 1
+
+
+def pack(groups):
+    steps = 1
+    while all(group[0].shape[0] % (32 * steps) == 0 for group in groups) and steps < 4:
+        steps *= 2
+
+    def spec(array):
+        return pl.BlockSpec((array.shape[0] // steps, array.shape[1]), lambda i: (i, 0))
+
+    outs = tuple(
+        jax.ShapeDtypeStruct((group[0].shape[0], sum(a.shape[1] for a in group)), bf16)
+        for group in groups
+    )
+    arrays = [array for group in groups for array in group]
+    return pl.pallas_call(
+        pack_kernel,
+        grid=(steps,),
+        out_shape=outs,
+        in_specs=[spec(array) for array in arrays],
+        out_specs=tuple(spec(out) for out in outs),
+        compiler_params=pltpu.CompilerParams(vmem_limit_bytes=VMEM_CAP),
+        cost_estimate=LIGHT,
+        name="pack",
+    )(*arrays)
 
 
 def bits_of(count):
@@ -841,6 +909,22 @@
         pairs = [(i, ((i // 2) ^ j) * 2 + i % 2) for i in range(count)]
         total = total + lax.ppermute(piece(value, mine ^ j), axis, pairs).astype(f32)
     return total.astype(bf16)
+
+
+def rest_gather(value, axis):
+    count = lax.axis_size(axis)
+    index = lax.axis_index(axis)
+    whole = jnp.zeros((count // 2,) + value.shape, value.dtype)
+    for j in range(count // 2):
+        part = value
+        if j:
+            pairs = [(i, ((i // 2) ^ j) * 2 + i % 2) for i in range(count)]
+            part = lax.ppermute(value, axis, pairs)
+        whole = lax.dynamic_update_index_in_dim(whole, part, (index // 2) ^ j, 0)
+    other = swap(whole, axis, 0)
+    upper = index % 2 == 1
+    both = jnp.stack([jnp.where(upper, other, whole), jnp.where(upper, whole, other)], axis=1)
+    return both.reshape((count * value.shape[0],) + value.shape[1:])
 
 
 def reduce_rows(value, scatter_axis, sum_axis):
@@ -855,7 +939,7 @@
     value = value.reshape((count // 2, 2, rows // count) + value.shape[1:])
     value = yield scatter_step(value, sum_axis, 0, 1)
     value = yield rest_sum(value, sum_axis)
-    yield lax.all_gather(value, sum_axis, axis=0, tiled=True)
+    yield rest_gather(value, sum_axis)
 
 
 class Chain:
@@ -951,19 +1035,13 @@
     lead = jnp.stack([share * other + part for other in near]).astype(jnp.int32)
     rows = seq_count * BLK
 
-    qkv_low = jnp.concatenate([query_master, key_master, value_master], axis=1).astype(bf16)
+    (qkv_low,) = pack([[query_master, key_master, value_master]])
     both = jnp.stack([byte_ids, doc_ids], axis=1)
     both, qkv_low = lax.optimization_barrier((both, qkv_low))
     qkv = gather_rows(qkv_low, "fsdp")
     both = gather_small(both, "ctx")
-    both, out_master, gate_master, up_master, down_master = lax.optimization_barrier(
-        (both, out_master, gate_master, up_master, down_master)
-    )
-    both = piece(both, seq, 1)
-    ids = both[:, 0].reshape(total_bytes)
-    docs = both[:, 1, ::2]
-    ogu_low = jnp.concatenate([out_master, gate_master, up_master], axis=1).astype(bf16)
-    down_low = down_master.astype(bf16)
+    ogu_low, down_low = pack([[out_master, gate_master, up_master], [down_master]])
+    both, ogu_low, down_low = lax.optimization_barrier((both, ogu_low, down_low))
     ogu = gather_rows(ogu_low, "fsdp")
     down_weight = gather_rows(down_low, "fsdp")
     query_weight = qkv[:, :width]
@@ -988,27 +1066,23 @@
         axis=0,
     )
 
-    phases = phase_ids(ids, total_bytes)
     table_wide = jnp.pad(table, ((0, -vocab % LANE), (0, 0)))
-    tokens, norm_one, conv, mix = byte_forward(
-        phases, table_wide, conv_w, score_w, gain_one, total_bytes
-    )
-
-    def own_rows(array):
-        return jnp.concatenate(
-            [lax.dynamic_slice_in_dim(array, lead[s] * BLK, BLK, 0) for s in range(seq_count)],
-            axis=0,
-        )
-
-    tokens_own = own_rows(tokens)
-    norm_own = own_rows(norm_one)
+    tokens, norm_one, norm_own, conv, mix, phases, known, barred = byte_forward(
+        seq[None], lead, both, table_wide, conv_w, score_w, gain_one, total_bytes
+    )
+    tokens_own = jnp.concatenate(
+        [lax.dynamic_slice_in_dim(tokens, lead[s] * BLK, BLK, 0) for s in range(seq_count)], axis=0
+    )
 
     queries = jnp.dot(norm_own, query_weight, preferred_element_type=f32).astype(bf16)
     keys = jnp.dot(norm_one, key_weight, preferred_element_type=f32).astype(bf16)
     values = jnp.dot(norm_one, value_weight, preferred_element_type=f32).astype(bf16)
-    low, high, buckets, rel = attention_tables(docs, rel_bucket, rel_bias, lead)
+    docs = piece(both[:, :, 1], seq, 1)
+    low, high, buckets, rel = attention_tables(
+        docs[:, 0], docs[:, 2 * BLK - 2], rel_bucket, rel_bias, lead
+    )
     attended, attended_low, log_total = attend(
-        lead, low, high, queries, keys, values, docs, buckets, rel
+        lead, low, high, queries, keys, values, known, barred, buckets, rel
     )
 
     resid = tokens_own + jnp.dot(attended_low, out_weight, preferred_element_type=f32)
@@ -1053,7 +1127,8 @@
         d_attended,
         attended,
         log_total,
-        docs,
+        known,
+        barred,
         buckets,
         rel,
     )

time: 544 us -> 544 us (level)
  blocking collectives: 32.8 us -> 0 us
  waiting for transfers between devices: 82.7 us -> 109 us
  Pallas kernels: 147 us -> 170 us
  between operations: 15.6 us -> 2.03 us
  other arithmetic: 33.2 us -> 25 us
    all_gather x1 -> x0, blocking collectives: 32.8 us -> none  [reduce_rows(): yield lax.all_gather(value, sum_axis, axis=0, tiled=True)]
    ppermute x25 -> x28, waiting for transfers between devices: 45.9 us -> 67 us  [swap(): return lax.ppermute(value, axis, [(i, i ^ 1 << bit) for i in range(count)])]
    ppermute x12, starting transfers between devices: 32.2 us -> 17.7 us  [rest_sum(): lax.ppermute(piece(value, mine ^ j), axis, pairs).astype(f32)]
    ppermute x0 -> x9, starting transfers between devices: none -> 13.5 us  [rest_gather(): part = lax.ppermute(value, axis, pairs)]
    pallas_call x0 -> x2, Pallas kernels: none -> 8.05 us  [pack(): pl.pallas_call(pack_kernel, grid=(steps,), out_shape=outs, in_specs=[spec...]
    ppermute x6, waiting for transfers between devices: 10.3 us -> 17.7 us  [to_owner(): return lax.ppermute(block, 'ctx', pairs)]
    pallas_call x1, Pallas kernels: 48.1 us -> 55.2 us  [attend_back(): pl.pallas_call(attend_back_kernel, grid=(pairs,), out_shape=(jax.ShapeDty...]
    ppermute x25 -> x28, starting transfers between devices: 52.4 us -> 59.3 us  [swap(): return lax.ppermute(value, axis, [(i, i ^ 1 << bit) for i in range(count)])]
  transfers between devices with their start and end apart: 48 -> 58, of which waited for: 12 -> 18; matrix products, arithmetic and copies ran while one was open for 24% -> 20% of each run, Pallas kernels for 27% -> 31%
where the time goes in v3:
time: 544 us; the launch traced here: 535 us
  Pallas kernels  170 us (31%)
  waiting for transfers between devices  109 us (20%)
  starting transfers between devices  103 us (19%)
  local copies, waits for them, and re-layouts  68.3 us (13%)
  matrix products  57.3 us (11%)
  other arithmetic  25 us (5%)
    ppermute x28, waiting for transfers between devices, swap(): return lax.ppermute(value, axis, [(i, i ^ 1 << bit) for i in range(count)])  67 us
    ppermute x28, starting transfers between devices, swap(): return lax.ppermute(value, axis, [(i, i ^ 1 << bit) for i in range(count)])  59.3 us
    pallas_call x1, Pallas kernels, attend_back(): pl.pallas_call(attend_back_kernel, grid=(pairs,), out_shape=(jax.ShapeDty...  55.2 us
    pallas_call x1, Pallas kernels, attend(): pl.pallas_call(attend_kernel, grid=(pairs,), out_shape=(jax.ShapeDtypeStr...  44.2 us
    pallas_call x1, Pallas kernels, byte_backward(): pl.pallas_call(functools.partial(byte_backward_kernel, total_bytes), out_...  33.1 us
    pallas_call x1, Pallas kernels, byte_forward(): pl.pallas_call(functools.partial(byte_forward_kernel, total_bytes), out_s...  29.3 us
    dynamic_update_slice x12, local copies, waits for them, and re-layouts, gather_rows(): lax.dynamic_update_slice_in_dim(result, part, (index ^ j) * rows, axis=0)  20.5 us
    ppermute x12, waiting for transfers between devices, rest_sum(): lax.ppermute(piece(value, mine ^ j), axis, pairs).astype(f32)  18.8 us
  transfers between devices with their start and end apart: 58, of which 18 were waited for; matrix products, arithmetic and copies ran while one was open for 20% of the time, Pallas kernels for 31%

profile of v3, /device:TPU:0, one launch (start us, length us, event | category | flops | bytes accessed | tf_op | source)
XLA Modules:
  0.0 534.6 jit_solution(2692445883693080639)
XLA Ops:
  30.6 4.5 pack.3
  55.6 29.3 %byte_forward.1 = (f32[1024,768]{1,0:T(8,128)}, bf16[1024,768]{1,0:T(8,128)(2,1)}, bf16[512,768]{1,0:T(8,128)(2,1)}, f32[12,176,768]{2,1,0:T(8,128)}, f32[4,176,...) custom-call(s32[1]{0:T(128)} %bitcast.seq_ref, ...), custom_call_target="tpu_custom_call" | custom-call | flops 1 | bytes 1 | tf_op jit(solution)/shard_map/byte_forward/pallas_call | solution.py:217
  89.7 5.6 %collective-permute-done.15 = bf16[128,768]{1,0:T(8,128)(2,1)S(1)} collective-permute-done((bf16[128,768]{1,0:T(8,128)(2,1)}, bf16[128,768]{1,0:T(8,128)(2,1)S(1)}, u32[]{:S(2)}, u32[]{:S(2)}) %collective-permute-start.15) | collective-permute-done | bytes 196640 | tf_op jit(solution)/shard_map/ppermute | solution.py:1059
  108.9 28.5 %collective-permute-done.6 = bf16[192,4864]{1,0:T(8,128)(2,1)} collective-permute-done((bf16[192,4864]{1,0:T(8,128)(2,1)}, bf16[192,4864]{1,0:T(8,128)(2,1)}, u32[]{:S(2)}, u32[]{:S(2)}) %collective-permute-start.6) | collective-permute-done | bytes 1867808 | tf_op jit(solution)/shard_map/ppermute | solution.py:858
  141.6 44.2 %attend.1 = (f32[512,768]{1,0:T(8,128)}, bf16[512,768]{1,0:T(8,128)(2,1)}, f32[6,4,256]{2,1,0:T(4,128)}) custom-call(s32[4]{0:T(128)} %pad_add_fusion.4.lead_ref.first_ref, s32[4]{0:T(128)} %convert_reduce_fusion.4.low_ref, s32[4]{0:T(128)} %get-tuple-element.153.high_ref, bf16[512,768]{1,0:T(8,128)(2,1)} %convolution_convert_fusion.9.q_ref, ...), custom_call_target="tpu_custom_call" | custom-call | flops 1 | bytes 1 | tf_op jit(solution)/shard_map/attend/pallas_call | solution.py:602
  200.9 4.1 multiply_convert_fusion.1
  208.0 5.0 collective-permute-start.18
  212.9 6.4 %fusion.10 = (bf16[512,2048]{1,0:T(8,128)(2,1)S(1)}, bf16[512,2048]{1,0:T(8,128)(2,1)S(1)}) fusion(f32[512,2048]{1,0:T(8,128)S(1)} %fusion.13, f32[512,2048]{1,0:T(8,128)S(1)} %get-tuple-element.212, bf16[512,768]{1,0:T(8,128)(2,1)S(1)} %copy-done.12, bf16[2048,768]{1,0:T(8,128)(2,1)} %constant_dynamic-update-slice_fusion), kind=kOutput, calls=%fused_computation.16 | convolution fusion | flops 1635778560 | bytes 16515072 | tf_op jit(solution)/shard_map/rd,fd->rf/dot_general | solution.py:1104
  234.6 4.4 collective-permute-start.12
  239.0 5.6 %collective-permute-done.14 = bf16[128,768]{1,0:T(8,128)(2,1)} collective-permute-done((bf16[128,768]{1,0:T(8,128)(2,1)}, bf16[128,768]{1,0:T(8,128)(2,1)}, u32[]{:S(2)}, u32[]{:S(2)}) %collective-permute-start.14) | collective-permute-done | bytes 196640 | tf_op jit(solution)/shard_map/ppermute | solution.py:1059
  244.6 6.5 %collective-permute-done.13 = bf16[128,768]{1,0:T(8,128)(2,1)} collective-permute-done((bf16[128,768]{1,0:T(8,128)(2,1)}, bf16[128,768]{1,0:T(8,128)(2,1)}, u32[]{:S(2)}, u32[]{:S(2)}) %collective-permute-start.13) | collective-permute-done | bytes 196640 | tf_op jit(solution)/shard_map/ppermute | solution.py:1059
  252.6 10.1 %collective-permute-start.20 = (bf16[512,768]{1,0:T(8,128)(2,1)S(1)}, bf16[512,768]{1,0:T(8,128)(2,1)S(1)}, u32[]{:S(2)}, u32[]{:S(2)}) collective-permute-start(bf16[512,768]{1,0:T(8,128)(2,1)S(1)} %dynamic-slice_bitcast_fusion.6), channel_id=1, source_target_pairs={{0,2},{1,3},{2,0},{3,1},{4,6},{5,7},{6,4},{7,5},{8,10},{9,11},{10,... | collective-permute-start | bytes 2359304 | tf_op jit(solution)/shard_map/ppermute | solution.py:858
  262.7 6.4 %multiply_reduce_fusion = (bf16[768]{0:T(1024)(128)(2,1)S(1)}, f32[512]{0:T(512)S(1)}, f32[512,768]{1,0:T(8,128)S(1)}) fusion(f32[512,768]{1,0:T(8,128)S(1)} %get-tuple-element.210, f32[512]{0:T(512)S(1)} %fusion.54, f32[768]{0:T(1024)S(1)} %copy-done.30, bf16[512,4096]{1,0:T(8,128)(2,1)S(1)} %copy-done.7, ...), kind=kOutput, calls=%fused_computation.46 | convolution fusion | flops 3223583488 | bytes 13640192 | tf_op jit(solution)/shard_map/rf,df->rd/dot_general | solution.py:1112
  273.1 7.3 %collective-permute-done.20 = bf16[512,768]{1,0:T(8,128)(2,1)S(1)} collective-permute-done((bf16[512,768]{1,0:T(8,128)(2,1)S(1)}, bf16[512,768]{1,0:T(8,128)(2,1)S(1)}, u32[]{:S(2)}, u32[]{:S(2)}) %collective-permute-start.20) | collective-permute-done | bytes 786464 | tf_op jit(solution)/shard_map/ppermute | solution.py:858
  294.1 55.2 %attend_back.1 = (bf16[512,768]{1,0:T(8,128)(2,1)}, bf16[1024,768]{1,0:T(8,128)(2,1)}, bf16[1024,768]{1,0:T(8,128)(2,1)}, f32[6,8,32]{2,1,0:T(8,128)}) custom-call(s32[4]{0:T(128)} %pad_add_fusion.4.lead_ref.first_ref, s32[4]{0:T(128)} %convert_reduce_fusion.4.low_ref, s32[4]{0:T(128)} %get-tuple-element.153.high_ref, ...), custom_call_target="tpu_custom_call" | custom-call | flops 1 | bytes 1 | tf_op jit(solution)/shard_map/attend_back/pallas_call | solution.py:761
  349.3 4.3 convolution_convert_fusion.5
  366.3 12.5 %collective-permute-start.27 = (bf16[4,24,4096]{2,1,0:T(8,128)(2,1)S(1)}, bf16[4,24,4096]{2,1,0:T(8,128)(2,1)S(1)}, u32[]{:S(2)}, u32[]{:S(2)}) collective-permute-start(bf16[4,24,4096]{2,1,0:T(8,128)(2,1)S(1)} %dynamic-slice_bitcast_fusion.5), channel_id=1, source_target_pairs={{0,4},{4,0},{8,12},{12,8},{16,20},{20,16},{24,28},{28,24},{1,5},{5... | collective-permute-start | bytes 2359304 | tf_op jit(solution)/shard_map/ppermute | solution.py:858
  389.1 7.8 %collective-permute-start.57 = (bf16[4,64,768]{2,1,0:T(8,128)(2,1)S(1)}, bf16[4,64,768]{2,1,0:T(8,128)(2,1)S(1)}, u32[]{:S(2)}, u32[]{:S(2)}) collective-permute-start(bf16[4,64,768]{2,1,0:T(8,128)(2,1)S(1)} %bitcast_dynamic-update-slice_fusion.8), channel_id=1, source_target_pairs={{0,4},{4,0},{8,12},{12,8},{16,20},{20,16},{24,28},{28,24},{1,5},{5... | collective-permute-start | bytes 1179656 | tf_op jit(solution)/shard_map/ppermute | solution.py:858
  397.0 9.6 %collective-permute-done.57 = bf16[4,64,768]{2,1,0:T(8,128)(2,1)S(1)} collective-permute-done((bf16[4,64,768]{2,1,0:T(8,128)(2,1)S(1)}, bf16[4,64,768]{2,1,0:T(8,128)(2,1)S(1)}, u32[]{:S(2)}, u32[]{:S(2)}) %collective-permute-start.57) | collective-permute-done | bytes 393248 | tf_op jit(solution)/shard_map/ppermute | solution.py:858
  415.9 33.1 %byte_backward.1 = f32[280,768]{1,0:T(8,128)} custom-call(s32[4]{0:T(128)} %pad_add_fusion.4.lead_ref.first_ref, f32[16,256]{1,0:T(8,128)} %get-tuple-element.72.ids_ref, f32[1024,768]{1,0:T(8,128)} %get-tuple-element.63.tok_ref, f32[1024,768]{1,0:T(8,128)} %copy-done, f32[4,128,768]{2,1,0:T(8,128)} %bitcast.231, ...), custom_call_target="tpu_custom_call" | custom-call | flops 1 | bytes 1 | tf_op jit(solution)/shard_map/byte_backward/pallas_call | solution.py:458
  467.0 7.7 %collective-permute-done.34 = bf16[40,768]{1,0:T(8,128)(2,1)S(1)} collective-permute-done((bf16[40,768]{1,0:T(8,128)(2,1)S(1)}, bf16[40,768]{1,0:T(8,128)(2,1)S(1)}, u32[]{:S(2)}, u32[]{:S(2)}) %collective-permute-start.34) | collective-permute-done | bytes 61472 | tf_op jit(solution)/shard_map/ppermute | solution.py:910
  476.8 9.3 %collective-permute-done.36 = bf16[40,768]{1,0:T(8,128)(2,1)S(1)} collective-permute-done((bf16[40,768]{1,0:T(8,128)(2,1)S(1)}, bf16[40,768]{1,0:T(8,128)(2,1)S(1)}, u32[]{:S(2)}, u32[]{:S(2)}) %collective-permute-start.36) | collective-permute-done | bytes 61472 | tf_op jit(solution)/shard_map/ppermute | solution.py:858
  507.8 4.2 collective-permute-done.44
  526.8 5.6 %collective-permute-done.49 = bf16[4,24,3072]{2,1,0:T(8,128)(2,1)S(1)} collective-permute-done((bf16[4,24,3072]{2,1,0:T(8,128)(2,1)S(1)}, bf16[4,24,3072]{2,1,0:T(8,128)(2,1)S(1)}, u32[]{:S(2)}, u32[]{:S(2)}) %collective-permute-start.49) | collective-permute-done | bytes 589856 | tf_op jit(solution)/shard_map/ppermute | solution.py:858
  (330 shorter events, 215.6 us)
Async XLA Ops:
  8.6 92.7 %collective-permute-start.3 = (bf16[192,2304]{1,0:T(8,128)(2,1)}, bf16[192,2304]{1,0:T(8,128)(2,1)}, u32[]{:S(2)}, u32[]{:S(2)}) collective-permute-start(bf16[192,2304]{1,0:T(8,128)(2,1)} %pack.2), channel_id=1, source_target_pairs={{0,2},{1,3},{2,0},{3,1},{4,6},{5,7},{6,4},{7,5},{8,10},{9,11},{10,... | collective-permute-start | bytes 2654216 | tf_op jit(solution)/shard_map/ppermute | solution.py:858
  13.3 74.1 %collective-permute-start.17 = (bf16[128,768]{1,0:T(8,128)(2,1)}, bf16[128,768]{1,0:T(8,128)(2,1)}, u32[]{:S(2)}, u32[]{:S(2)}) collective-permute-start(bf16[128,768]{1,0:T(8,128)(2,1)} %bitcast.226), channel_id=1, source_target_pairs={{0,24},{4,28},{8,16},{12,20},{16,8},{20,12},{24,0},{28,4},{1,25},{... | collective-permute-start | bytes 589832 | tf_op jit(solution)/shard_map/ppermute | solution.py:1059
  17.6 70.5 %collective-permute-start.16 = (bf16[128,768]{1,0:T(8,128)(2,1)}, bf16[128,768]{1,0:T(8,128)(2,1)}, u32[]{:S(2)}, u32[]{:S(2)}) collective-permute-start(bf16[128,768]{1,0:T(8,128)(2,1)} %bitcast.227), channel_id=1, source_target_pairs={{0,16},{4,20},{8,24},{12,28},{16,0},{20,4},{24,8},{28,12},{1,17},{... | collective-permute-start | bytes 589832 | tf_op jit(solution)/shard_map/ppermute | solution.py:1059
  45.4 53.3 %collective-permute-start.9 = (bf16[512,768]{1,0:T(8,128)(2,1)}, bf16[512,768]{1,0:T(8,128)(2,1)}, u32[]{:S(2)}, u32[]{:S(2)}) collective-permute-start(bf16[512,768]{1,0:T(8,128)(2,1)} %get-tuple-element.71), channel_id=1, source_target_pairs={{0,2},{1,3},{2,0},{3,1},{4,6},{5,7},{6,4},{7,5},{8,10},{9,11},{10,... | collective-permute-start | bytes 2359304 | tf_op jit(solution)/shard_map/ppermute | solution.py:858
  46.0 54.7 %collective-permute-start.10 = (bf16[512,768]{1,0:T(8,128)(2,1)}, bf16[512,768]{1,0:T(8,128)(2,1)}, u32[]{:S(2)}, u32[]{:S(2)}) collective-permute-start(bf16[512,768]{1,0:T(8,128)(2,1)} %get-tuple-element.71), channel_id=1, source_target_pairs={{0,1},{1,0},{2,3},{3,2},{4,5},{5,4},{6,7},{7,6},{8,9},{9,8},{10,11... | collective-permute-start | bytes 2359304 | tf_op jit(solution)/shard_map/ppermute | solution.py:858
  95.2 42.2 %collective-permute-start.6 = (bf16[192,4864]{1,0:T(8,128)(2,1)}, bf16[192,4864]{1,0:T(8,128)(2,1)}, u32[]{:S(2)}, u32[]{:S(2)}) collective-permute-start(bf16[192,4864]{1,0:T(8,128)(2,1)} %get-tuple-element.70), channel_id=1, source_target_pairs={{0,2},{1,3},{2,0},{3,1},{4,6},{5,7},{6,4},{7,5},{8,10},{9,11},{10,... | collective-permute-start | bytes 5603336 | tf_op jit(solution)/shard_map/ppermute | solution.py:858
  98.7 90.0 %collective-permute-start.7 = (bf16[192,4864]{1,0:T(8,128)(2,1)}, bf16[192,4864]{1,0:T(8,128)(2,1)}, u32[]{:S(2)}, u32[]{:S(2)}) collective-permute-start(bf16[192,4864]{1,0:T(8,128)(2,1)} %get-tuple-element.70), channel_id=1, source_target_pairs={{0,1},{1,0},{2,3},{3,2},{4,5},{5,4},{6,7},{7,6},{8,9},{9,8},{10,11... | collective-permute-start | bytes 5603336 | tf_op jit(solution)/shard_map/ppermute | solution.py:858
  137.4 54.3 %collective-permute-start.8 = (bf16[192,4864]{1,0:T(8,128)(2,1)}, bf16[192,4864]{1,0:T(8,128)(2,1)}, u32[]{:S(2)}, u32[]{:S(2)}) collective-permute-start(bf16[192,4864]{1,0:T(8,128)(2,1)} %collective-permute-done.6), channel_id=1, source_target_pairs={{0,1},{1,0},{2,3},{3,2},{4,5},{5,4},{6,7},{7,6},{8,9},{9,8},{10,11... | collective-permute-start | bytes 5603336 | tf_op jit(solution)/shard_map/ppermute | solution.py:858
  229.2 51.5 %collective-permute-start.19 = (bf16[2,192,4096]{2,1,0:T(8,128)(2,1)}, bf16[2,192,4096]{2,1,0:T(8,128)(2,1)}, u32[]{:S(2)}, u32[]{:S(2)}) collective-permute-start(bf16[2,192,4096]{2,1,0:T(8,128)(2,1)} %dynamic-slice_bitcast_fusion), channel_id=1, source_target_pairs={{0,1},{1,0},{2,3},{3,2},{4,5},{5,4},{6,7},{7,6},{8,9},{9,8},{10,11... | collective-permute-start | bytes 9437192 | tf_op jit(solution)/shard_map/ppermute | solution.py:858
  252.6 27.8 %collective-permute-start.20 = (bf16[512,768]{1,0:T(8,128)(2,1)S(1)}, bf16[512,768]{1,0:T(8,128)(2,1)S(1)}, u32[]{:S(2)}, u32[]{:S(2)}) collective-permute-start(bf16[512,768]{1,0:T(8,128)(2,1)S(1)} %dynamic-slice_bitcast_fusion.6), channel_id=1, source_target_pairs={{0,2},{1,3},{2,0},{3,1},{4,6},{5,7},{6,4},{7,5},{8,10},{9,11},{10,... | collective-permute-start | bytes 2359304 | tf_op jit(solution)/shard_map/ppermute | solution.py:858
  285.3 73.4 %collective-permute-start.21 = (bf16[192,4096]{1,0:T(8,128)(2,1)}, bf16[192,4096]{1,0:T(8,128)(2,1)}, u32[]{:S(2)}, u32[]{:S(2)}) collective-permute-start(bf16[192,4096]{1,0:T(8,128)(2,1)} %dynamic-slice_bitcast_fusion.2), channel_id=1, source_target_pairs={{0,2},{1,3},{2,0},{3,1},{4,6},{5,7},{6,4},{7,5},{8,10},{9,11},{10,... | collective-permute-start | bytes 4718600 | tf_op jit(solution)/shard_map/ppermute | solution.py:858
  291.9 66.7 %collective-permute-start.22 = (bf16[4,64,768]{2,1,0:T(8,128)(2,1)}, bf16[4,64,768]{2,1,0:T(8,128)(2,1)S(1)}, u32[]{:S(2)}, u32[]{:S(2)}) collective-permute-start(bf16[4,64,768]{2,1,0:T(8,128)(2,1)} %dynamic-slice_bitcast_fusion.8), channel_id=1, source_target_pairs={{0,4},{4,0},{8,12},{12,8},{16,20},{20,16},{24,28},{28,24},{1,5},{5... | collective-permute-start | bytes 1179656 | tf_op jit(solution)/shard_map/ppermute | solution.py:858
  361.8 17.8 %collective-permute-start.25 = (bf16[64,768]{1,0:T(8,128)(2,1)S(1)}, bf16[64,768]{1,0:T(8,128)(2,1)S(1)}, u32[]{:S(2)}, u32[]{:S(2)}) collective-permute-start(bf16[64,768]{1,0:T(8,128)(2,1)S(1)} %get-tuple-element.198), channel_id=1, source_target_pairs={{0,24},{4,28},{8,16},{12,20},{16,8},{20,12},{24,0},{28,4},{1,25},{... | collective-permute-start | bytes 294920 | tf_op jit(solution)/shard_map/ppermute | solution.py:910
  366.3 40.5 %collective-permute-start.27 = (bf16[4,24,4096]{2,1,0:T(8,128)(2,1)S(1)}, bf16[4,24,4096]{2,1,0:T(8,128)(2,1)S(1)}, u32[]{:S(2)}, u32[]{:S(2)}) collective-permute-start(bf16[4,24,4096]{2,1,0:T(8,128)(2,1)S(1)} %dynamic-slice_bitcast_fusion.5), channel_id=1, source_target_pairs={{0,4},{4,0},{8,12},{12,8},{16,20},{20,16},{24,28},{28,24},{1,5},{5... | collective-permute-start | bytes 2359304 | tf_op jit(solution)/shard_map/ppermute | solution.py:858
  388.9 18.1 %collective-permute-start.26 = (bf16[2,192,3072]{2,1,0:T(8,128)(2,1)S(1)}, bf16[2,192,3072]{2,1,0:T(8,128)(2,1)S(1)}, u32[]{:S(2)}, u32[]{:S(2)}) collective-permute-start(bf16[2,192,3072]{2,1,0:T(8,128)(2,1)S(1)} %dynamic-slice_bitcast_fusion.1), channel_id=1, source_target_pairs={{0,1},{1,0},{2,3},{3,2},{4,5},{5,4},{6,7},{7,6},{8,9},{9,8},{10,11... | collective-permute-start | bytes 7077896 | tf_op jit(solution)/shard_map/ppermute | solution.py:858
  409.0 42.1 %collective-permute-start.28 = (bf16[192,3072]{1,0:T(8,128)(2,1)}, bf16[192,3072]{1,0:T(8,128)(2,1)}, u32[]{:S(2)}, u32[]{:S(2)}) collective-permute-start(bf16[192,3072]{1,0:T(8,128)(2,1)} %dynamic-slice_bitcast_fusion.4), channel_id=1, source_target_pairs={{0,2},{1,3},{2,0},{3,1},{4,6},{5,7},{6,4},{7,5},{8,10},{9,11},{10,... | collective-permute-start | bytes 3538952 | tf_op jit(solution)/shard_map/ppermute | solution.py:858
  410.2 40.8 %collective-permute-start.31 = (bf16[24,4096]{1,0:T(8,128)(2,1)}, bf16[24,4096]{1,0:T(8,128)(2,1)S(1)}, u32[]{:S(2)}, u32[]{:S(2)}) collective-permute-start(bf16[24,4096]{1,0:T(8,128)(2,1)} %get-tuple-element.178), channel_id=1, source_target_pairs={{0,24},{4,28},{8,16},{12,20},{16,8},{20,12},{24,0},{28,4},{1,25},{... | collective-permute-start | bytes 589832 | tf_op jit(solution)/shard_map/ppermute | solution.py:910
  412.0 39.0 %collective-permute-start.30 = (bf16[24,4096]{1,0:T(8,128)(2,1)S(1)}, bf16[24,4096]{1,0:T(8,128)(2,1)S(1)}, u32[]{:S(2)}, u32[]{:S(2)}) collective-permute-start(bf16[24,4096]{1,0:T(8,128)(2,1)S(1)} %get-tuple-element.179), channel_id=1, source_target_pairs={{0,16},{4,20},{8,24},{12,28},{16,0},{20,4},{24,8},{28,12},{1,17},{... | collective-permute-start | bytes 589832 | tf_op jit(solution)/shard_map/ppermute | solution.py:910
  412.1 39.0 %collective-permute-start.29 = (bf16[24,4096]{1,0:T(8,128)(2,1)S(1)}, bf16[24,4096]{1,0:T(8,128)(2,1)S(1)}, u32[]{:S(2)}, u32[]{:S(2)}) collective-permute-start(bf16[24,4096]{1,0:T(8,128)(2,1)S(1)} %get-tuple-element.177), channel_id=1, source_target_pairs={{0,8},{4,12},{8,0},{12,4},{16,24},{20,28},{24,16},{28,20},{1,9},{5... | collective-permute-start | bytes 589832 | tf_op jit(solution)/shard_map/ppermute | solution.py:910
  452.9 23.9 %collective-permute-start.50 = (bf16[24,4096]{1,0:T(8,128)(2,1)S(1)}, bf16[24,4096]{1,0:T(8,128)(2,1)S(1)}, u32[]{:S(2)}, u32[]{:S(2)}) collective-permute-start(bf16[24,4096]{1,0:T(8,128)(2,1)S(1)} %fusion.42), channel_id=1, source_target_pairs={{0,8},{4,12},{8,0},{12,4},{16,24},{20,28},{24,16},{28,20},{1,9},{5... | collective-permute-start | bytes 589832 | tf_op jit(solution)/shard_map/ppermute | solution.py:922
  452.9 34.9 %collective-permute-start.51 = (bf16[24,4096]{1,0:T(8,128)(2,1)S(1)}, bf16[24,4096]{1,0:T(8,128)(2,1)S(1)}, u32[]{:S(2)}, u32[]{:S(2)}) collective-permute-start(bf16[24,4096]{1,0:T(8,128)(2,1)S(1)} %fusion.42), channel_id=1, source_target_pairs={{0,16},{4,20},{8,24},{12,28},{16,0},{20,4},{24,8},{28,12},{1,17},{... | collective-permute-start | bytes 589832 | tf_op jit(solution)/shard_map/ppermute | solution.py:922
  464.9 25.7 %collective-permute-start.52 = (bf16[24,4096]{1,0:T(8,128)(2,1)S(1)}, bf16[24,4096]{1,0:T(8,128)(2,1)S(1)}, u32[]{:S(2)}, u32[]{:S(2)}) collective-permute-start(bf16[24,4096]{1,0:T(8,128)(2,1)S(1)} %fusion.42), channel_id=1, source_target_pairs={{0,24},{4,28},{8,16},{12,20},{16,8},{20,12},{24,0},{28,4},{1,25},{... | collective-permute-start | bytes 589832 | tf_op jit(solution)/shard_map/ppermute | solution.py:922
  474.7 25.7 %collective-permute-start.42 = (bf16[4,24,3072]{2,1,0:T(8,128)(2,1)S(1)}, bf16[4,24,3072]{2,1,0:T(8,128)(2,1)S(1)}, u32[]{:S(2)}, u32[]{:S(2)}) collective-permute-start(bf16[4,24,3072]{2,1,0:T(8,128)(2,1)S(1)} %dynamic-slice_bitcast_fusion.7), channel_id=1, source_target_pairs={{0,4},{4,0},{8,12},{12,8},{16,20},{20,16},{24,28},{28,24},{1,5},{5... | collective-permute-start | bytes 1769480 | tf_op jit(solution)/shard_map/ppermute | solution.py:858
  490.6 33.6 %collective-permute-start.53 = (bf16[4,24,4096]{2,1,0:T(8,128)(2,1)S(1)}, bf16[4,24,4096]{2,1,0:T(8,128)(2,1)S(1)}, u32[]{:S(2)}, u32[]{:S(2)}) collective-permute-start(bf16[4,24,4096]{2,1,0:T(8,128)(2,1)S(1)} %bitcast_dynamic-update-slice_fusion), channel_id=1, source_target_pairs={{0,4},{4,0},{8,12},{12,8},{16,20},{20,16},{24,28},{28,24},{1,5},{5... | collective-permute-start | bytes 2359304 | tf_op jit(solution)/shard_map/ppermute | solution.py:858
  (72 other events, 727.6 us)
